TPU v7x, 32 devices: a whole 2x2x4 slice. The times are simulated.
32 devices in a mesh: grp: 2 (over x), seq: 8 (over z, y), head: 2 (over core).
Axes of the slice: x: 2, y: 2, z: 4, core: 2. Of those that a mesh axis runs over, the one named last changes fastest.
Arguments:
- queries: bfloat16 [8, 8, 40, 1024], P(('grp', 'head'), None, None, 'seq'), parts along dimension 0, may hold values from -160 to 160
- keys: bfloat16 [8, 8, 40, 1024], P('grp', None, None, 'seq'), parts along dimension 0, may hold values from -160 to 160
- values: bfloat16 [8, 8, 40, 1024], P('grp', None, None, 'seq'), parts along dimension 0, may hold values from -6 to 6
- final_gain: bfloat16 [1024], replicated, may hold values from 0.25 to 1.75
- out_weight: bfloat16 [1024, 64], replicated, may hold values from -0.1875 to 0.1875
- noisy_latent: bfloat16 [8, 16, 1280], P(('grp', 'head'), 'seq'), parts along dimension 0, may hold values from -6 to 6
- step_index: int32 [2], P('grp'), parts along dimension 0, may hold values from 0 to 15
- span_index: int32 [2], P('grp'), parts along dimension 0, may hold values from 0 to 63
- cache_flags: int32 [4, 2, 16], P('grp'), parts along dimension 0, may hold values 0 or 1
- latent_cache: bfloat16 [4, 2, 16, 1280], P('grp', 'head', 'seq'), parts along dimension 0, may hold values from -6 to 6
- feature_cache: bfloat16 [4, 2, 32, 61440], P('grp', 'head', 'seq'), parts along dimension 0, may hold values from -4 to 4
- first_weight: bfloat16 [432, 384], replicated, may hold values from -0.3125 to 0.3125
- first_gain: bfloat16 [384], replicated, may hold values from 0.25 to 1.75
- second_weight: bfloat16 [10368, 192], replicated, may hold values from -0.0625 to 0.0625
Outputs:
- clean_latent: bfloat16 [8, 16, 1280], P(('grp', 'head'), 'seq'), parts along dimension 0
- decoded: bfloat16 [8, 32, 30720], P(('grp', 'head'), 'seq'), parts along dimension 0
There are 2 independent parts, one for each index of `grp`. A program takes and returns all parts, laid end to end along the dimension named above; an argument that names none is the same for every part. Nothing has to cross between parts.
All inputs are finite; a program needn't handle non-finite values.
Results may differ from a plain program's by a relative error of at most 0.013.
Values may be sent and summed in bfloat16 or wider, within the bound.
No kernel may reach another device: no remote copies, remote signals or barrier semaphores. Data moves between devices by JAX's collectives and lax.ppermute only.
A program may use at most 64 MiB of HBM per device.

v0:
```python
import jax
import jax.numpy as jnp
from jax import lax
from jax.sharding import PartitionSpec as P

NSTEPS = 16
CSLOTS = 2


SHIFT_FACTOR = 5.0
NORM_EPSILON = 1e-06


def shifted(array, axis, by):
    count = lax.axis_size(axis)
    pairs = [(i, i + by) for i in range(count) if 0 <= i + by < count]
    return lax.ppermute(array, axis, pairs)


def extended_2(cells, sides, width):
    for axis, dim in sides:
        count = lax.axis_size(axis)
        ends = count - 1
        head = lax.slice_in_dim(cells, 0, width, axis=dim)
        tail = lax.slice_in_dim(cells, cells.shape[dim] - width, cells.shape[dim], axis=dim)
        cells = jnp.concatenate(
            [
                lax.ppermute(tail, axis, [(i, (i + 1) % count) for i in range(ends)]),
                cells,
                lax.ppermute(head, axis, [((i + 1) % count, i) for i in range(ends)]),
            ],
            axis=dim,
        )
    return cells


def noise_level_of(step_index):
    fraction = 1.0 - step_index[0].astype(jnp.float32) / NSTEPS
    return SHIFT_FACTOR * fraction / (1.0 + (SHIFT_FACTOR - 1.0) * fraction)


def attend(query_rows, key_rows, value_rows):
    scale = 1.0 / key_rows.shape[-1] ** 0.5
    scores = jnp.dot(query_rows, key_rows.T, preferred_element_type=jnp.float32) * scale
    row_max = jnp.max(scores, axis=1, keepdims=True)
    exponent = jnp.exp(scores - row_max)
    accumulated = jnp.sum(exponent, axis=1, keepdims=True)
    weights = exponent.astype(jnp.bfloat16)
    blended = jnp.dot(weights, value_rows, preferred_element_type=jnp.float32)
    return (blended / accumulated).astype(jnp.bfloat16)


def velocity_of(attended, final_gain, out_weight):
    features = attended.astype(jnp.float32)
    mean_square = jnp.mean(features * features, axis=-1, keepdims=True)
    normed = features * lax.rsqrt(mean_square + NORM_EPSILON) * final_gain.astype(jnp.float32)
    return jnp.dot(normed, out_weight.astype(jnp.float32), precision=lax.Precision.HIGHEST)


def unpatch(patch_velocity):
    frame_count, row_count, col_count, patch_width = patch_velocity.shape
    channels = patch_width // 4
    grouped = patch_velocity.reshape(frame_count, row_count, col_count, 2, 2, channels)
    grouped = grouped.transpose(0, 1, 3, 2, 4, 5)
    return grouped.reshape(frame_count, 2 * row_count, 2 * col_count * channels)


def first_conv(extended, weight):
    channels = weight.shape[0] // 27
    frame_count = extended.shape[0] - 2
    row_count = extended.shape[1] - 2
    lattice = extended.reshape(frame_count + 2, row_count + 2, -1, channels)
    lattice = jnp.pad(lattice, ((0, 0), (0, 0), (1, 1), (0, 0)))
    col_count = lattice.shape[2] - 2
    shifted_taps = [
        lattice[
            step_t : step_t + frame_count, step_h : step_h + row_count, step_w : step_w + col_count
        ]
        for step_t in range(3)
        for step_h in range(3)
        for step_w in range(3)
    ]
    return jnp.dot(jnp.concatenate(shifted_taps, -1), weight, preferred_element_type=jnp.float32)


def activate(first_feat, first_gain):
    mean_square = jnp.mean(first_feat * first_feat, axis=-1, keepdims=True)
    normed = first_feat * lax.rsqrt(mean_square + NORM_EPSILON) * first_gain.astype(jnp.float32)
    return jax.nn.silu(normed).astype(jnp.bfloat16)


def upsample(activated):
    return jnp.repeat(jnp.repeat(activated, 2, axis=1), 2, axis=2)


def second_conv(lattice, weight):
    channels = lattice.shape[3]
    frame_count = lattice.shape[0] - 2
    row_count = lattice.shape[1] - 2
    col_count = lattice.shape[2] - 2
    accumulated = None
    for step_t in range(3):
        for step_h in range(3):
            layer_slab = lattice[step_t : step_t + frame_count, step_h : step_h + row_count]
            stacked = jnp.concatenate(
                [layer_slab[:, :, step_w : step_w + col_count] for step_w in range(3)], -1
            )
            first_row = (step_t * 3 + step_h) * 3 * channels
            weight_block = weight[first_row : first_row + 3 * channels]
            contribution = jnp.dot(stacked, weight_block, preferred_element_type=jnp.float32)
            accumulated = contribution if accumulated is None else accumulated + contribution
    return accumulated


def body(
    queries,
    keys,
    values,
    final_gain,
    out_weight,
    noisy_latent,
    step_index,
    span_index,
    cache_flags,
    latent_cache,
    feature_cache,
    first_weight,
    first_gain,
    second_weight,
):
    frame_count, row_count, col_count, head_size = queries.shape
    query_rows = queries.reshape(-1, head_size)
    key_rows = keys.reshape(-1, head_size)
    value_rows = values.reshape(-1, head_size)
    query_count = query_rows.shape[0]
    block_rows = 512 if query_count % 512 == 0 else query_count

    def attend_block(query_block):
        return attend(query_block, key_rows, value_rows)

    attended = lax.map(
        attend_block, query_rows.reshape(query_count // block_rows, block_rows, head_size)
    )
    attended = attended.reshape(frame_count, row_count, col_count, head_size)
    velocity = unpatch(
        velocity_of(
            lax.all_to_all(attended, "seq", split_axis=1, concat_axis=3, tiled=True),
            final_gain,
            out_weight,
        )
    )
    clean_latent = (
        noisy_latent.astype(jnp.float32) - noise_level_of(step_index) * velocity
    ).astype(jnp.bfloat16)
    is_first = lax.axis_index("head") == 0
    cache_slot = span_index[0] % CSLOTS
    flags_now = lax.dynamic_index_in_dim(cache_flags, cache_slot, 0, keepdims=False).astype(
        jnp.bfloat16
    )
    own_latent = lax.dynamic_index_in_dim(latent_cache, cache_slot, 0, keepdims=False)
    own_feature = lax.dynamic_index_in_dim(feature_cache, cache_slot, 0, keepdims=False)
    cached_latent, cached_feature = (
        lax.all_gather(own_latent, "head", axis=0, tiled=True),
        lax.all_gather(own_feature, "head", axis=0, tiled=True),
    )
    latent_rows = cached_latent.shape[1]
    flag_start = lax.axis_index("seq") * latent_rows
    local_flags = lax.dynamic_slice_in_dim(flags_now, flag_start, latent_rows, 1)
    fine_flags = jnp.repeat(local_flags, 2, axis=1)
    earlier = shifted(clean_latent, "head", 1)
    prior_latent = jnp.where(is_first, cached_latent * local_flags[:, :, None], earlier)
    frame_block = jnp.concatenate([prior_latent, clean_latent], 0)
    extended = extended_2(frame_block, (("seq", 1),), 2)
    activated = activate(first_conv(extended, first_weight), first_gain)
    coarse_count = activated.shape[1]
    row_ids = jnp.arange(coarse_count, dtype=jnp.int32)
    slab_index = lax.axis_index("seq")
    outside = (slab_index == 0) & (row_ids == 0) | (slab_index == lax.axis_size("seq") - 1) & (
        row_ids == coarse_count - 1
    )
    activated = jnp.where(outside[None, :, None, None], jnp.zeros_like(activated), activated)
    margin = 1
    fine = upsample(activated)
    upsampled = fine[:, margin : fine.shape[1] - margin]
    earlier_feature = shifted(upsampled, "head", 1)
    cached_feature = cached_feature * fine_flags[:, :, None]
    cached_rimmed = extended_2(cached_feature, (("seq", 1),), 1)
    cached_rimmed = cached_rimmed.reshape(earlier_feature.shape)
    prior_feature = jnp.where(is_first, cached_rimmed, earlier_feature)
    lattice = jnp.concatenate([prior_feature, upsampled], 0)
    frames_total = lattice.shape[0]
    up_rows = lattice.shape[1] - 2
    lattice = jnp.pad(lattice, ((0, 0), (0, 0), (1, 1), (0, 0)))
    decoded = second_conv(lattice, second_weight)
    return (clean_latent, decoded.astype(jnp.bfloat16).reshape(frames_total - 2, up_rows, -1))


def solution(mesh):
    in_specs = (
        P(("grp", "head"), None, None, "seq"),
        P("grp", None, None, "seq"),
        P("grp", None, None, "seq"),
        P(),
        P(),
        P(("grp", "head"), "seq", None),
        P("grp"),
        P("grp"),
        P("grp", None, None),
        P("grp", "head", "seq", None),
        P("grp", "head", "seq", None),
        P(),
        P(),
        P(),
    )
    out_specs = (P(("grp", "head"), "seq", None), P(("grp", "head"), "seq", None))
    return jax.shard_map(body, mesh=mesh, in_specs=in_specs, out_specs=out_specs, check_vma=False)
```

profile of v0, /device:TPU:17, one launch (start us, length us, event | category | flops | bytes accessed | tf_op | source)
XLA Modules:
  0.0 94.9 jit_solution(16637094723453344013)
XLA Ops:
  0.6 0.0 copy-start
  0.7 1.8 %fusion.135 = (f32[640]{0:T(1024)S(1)}, f32[640,1280]{1,0:T(8,128)S(1)}) fusion(bf16[640,128]{1,0:T(8,128)(2,1)} %bitcast.106, bf16[1280,128]{1,0:T(8,128)(2,1)} %bitcast.105), kind=kOutput, calls=%fused_computation.178 | convolution fusion | flops 211352960 | bytes 3770880 | tf_op jit(solution)/shard_map/while/body/eval_jaxpr/dot_general | solution.py:44
  2.5 0.6 fusion.54
  3.1 0.7 fusion.89
  3.8 0.7 copy.49
  4.5 5.6 %all-to-all-start = ((bf16[2,8,40,128]{3,2,0,1:T(8,128)(2,1)}), bf16[2,8,40,128]{3,2,0,1:T(8,128)(2,1)S(1)}, u32[]{:S(2)}, u32[]{:S(2)}) async-start(bf16[2,8,40,128]{3,2,0,1:T(8,128)(2,1)} %copy.49), calls=%async_computation | async-start | bytes 327680 | tf_op jit(solution)/shard_map/all_to_all | solution.py:147
  10.8 0.2 constant_dynamic-slice_fusion.2
  11.0 3.4 %all-gather = bf16[2,1,4,61440]{3,2,1,0:T(4,128)(2,1)S(1)} all-gather(bf16[1,1,4,61440]{3,2,1,0:T(4,128)(2,1)S(1)} %constant_dynamic-slice_fusion.2), channel_id=2, replica_groups=mesh['grp'=2,'seq'=8,'head'=2] {'head'}, dimensions={0}, use_global_device_ids=true | all-gather | bytes 1474560 | tf_op jit(solution)/shard_map/all_gather | solution.py:164
  14.4 0.1 fusion.121
  14.5 0.1 broadcast_in_dim.34
  14.5 0.1 mul.119
  14.6 0.5 bitcast_multiply_fusion
  15.1 1.0 %copy-done.2 = bf16[2,4,61440]{2,1,0:T(4,128)(2,1)} copy-done((bf16[2,4,61440]{2,1,0:T(4,128)(2,1)}, bf16[2,4,61440]{2,1,0:T(4,128)(2,1)S(1)}, u32[]{:S(2)}) %copy-start.2) | copy-done | bytes 983064
  16.1 1.6 %fusion.132 = (bf16[2,1,61440]{2,1,0:T(2,128)(2,1)}, bf16[2,1,61440]{2,1,0:T(2,128)(2,1)}) fusion(bf16[2,4,61440]{2,1,0:T(4,128)(2,1)S(1)} %bitcast_multiply_fusion), kind=kLoop, calls=%fused_computation.175 | loop fusion | bytes 983040 | tf_op jit(solution)/shard_map/slice | solution.py:25
  17.7 3.1 %collective-permute-start = (bf16[2,1,61440]{2,1,0:T(2,128)(2,1)}, bf16[2,1,61440]{2,1,0:T(2,128)(2,1)}, u32[]{:S(2)}, u32[]{:S(2)}) collective-permute-start(bf16[2,1,61440]{2,1,0:T(2,128)(2,1)} %get-tuple-element.44), channel_id=1, source_target_pairs={{0,2},{2,4},{4,6},{6,8},{8,10},{10,12},{12,14},{1,3},{3,5},{5,7},{... | collective-permute-start | bytes 737288 | tf_op jit(solution)/shard_map/ppermute | solution.py:28
  20.8 3.1 %collective-permute-start.1 = (bf16[2,1,61440]{2,1,0:T(2,128)(2,1)}, bf16[2,1,61440]{2,1,0:T(2,128)(2,1)}, u32[]{:S(2)}, u32[]{:S(2)}) collective-permute-start(bf16[2,1,61440]{2,1,0:T(2,128)(2,1)} %get-tuple-element.45), channel_id=1, source_target_pairs={{2,0},{4,2},{6,4},{8,6},{10,8},{12,10},{14,12},{3,1},{5,3},{7,5},{... | collective-permute-start | bytes 737288 | tf_op jit(solution)/shard_map/ppermute | solution.py:30
  24.6 0.1 fusion.117
  24.7 0.1 fusion.119
  24.9 0.1 copy.50
  25.0 0.1 reshape.126
  25.0 0.5 fusion.92
  25.5 0.1 copy.51
  25.7 0.2 mul.117
  25.9 0.0 copy-start.6
  25.9 1.3 %collective-permute-start.2 = (bf16[2,2,1280]{2,1,0:T(2,128)(2,1)S(1)}, bf16[2,2,1280]{2,1,0:T(2,128)(2,1)S(1)}, u32[]{:S(2)}, u32[]{:S(2)}) collective-permute-start(bf16[2,2,1280]{2,1,0:T(2,128)(2,1)S(1)} %subtract_convert_fusion), channel_id=1, source_target_pairs={{0,1},{2,3},{4,5},{6,7},{8,9},{10,11},{12,13},{14,15},{16,17},{18,... | collective-permute-start | bytes 30728 | tf_op jit(solution)/shard_map/ppermute | solution.py:17
  27.3 2.6 %all-gather.1 = bf16[2,1,2,1280]{3,2,1,0:T(2,128)(2,1)S(1)} all-gather(bf16[1,1,2,1280]{3,2,1,0:T(2,128)(2,1)S(1)} %constant_dynamic-slice_fusion), channel_id=3, replica_groups=mesh['grp'=2,'seq'=8,'head'=2] {'head'}, dimensions={0}, use_global_device_ids=true | all-gather | bytes 15360 | tf_op jit(solution)/shard_map/all_gather | solution.py:163
  29.9 0.1 broadcast_select_fusion.1
  30.0 2.2 %collective-permute-start.3 = (bf16[4,2,1280]{2,1,0:T(2,128)(2,1)S(1)}, bf16[4,2,1280]{2,1,0:T(2,128)(2,1)S(1)}, u32[]{:S(2)}, u32[]{:S(2)}) collective-permute-start(bf16[4,2,1280]{2,1,0:T(2,128)(2,1)S(1)} %pad_maximum_fusion.3), channel_id=1, source_target_pairs={{0,2},{2,4},{4,6},{6,8},{8,10},{10,12},{12,14},{1,3},{3,5},{5,7},{... | collective-permute-start | bytes 61448 | tf_op jit(solution)/shard_map/ppermute | solution.py:28
  32.2 4.0 %collective-permute-start.4 = (bf16[4,2,1280]{2,1,0:T(2,128)(2,1)S(1)}, bf16[4,2,1280]{2,1,0:T(2,128)(2,1)S(1)}, u32[]{:S(2)}, u32[]{:S(2)}) collective-permute-start(bf16[4,2,1280]{2,1,0:T(2,128)(2,1)S(1)} %pad_maximum_fusion.3), channel_id=1, source_target_pairs={{2,0},{4,2},{6,4},{8,6},{10,8},{12,10},{14,12},{3,1},{5,3},{7,5},{... | collective-permute-start | bytes 61448 | tf_op jit(solution)/shard_map/ppermute | solution.py:30
  36.2 6.4 %collective-permute-done.3 = bf16[4,2,1280]{2,1,0:T(2,128)(2,1)S(1)} collective-permute-done((bf16[4,2,1280]{2,1,0:T(2,128)(2,1)S(1)}, bf16[4,2,1280]{2,1,0:T(2,128)(2,1)S(1)}, u32[]{:S(2)}, u32[]{:S(2)}) %collective-permute-start.3) | collective-permute-done | bytes 20512 | tf_op jit(solution)/shard_map/ppermute | solution.py:28
  42.6 2.6 %collective-permute-done.4 = bf16[4,2,1280]{2,1,0:T(2,128)(2,1)S(1)} collective-permute-done((bf16[4,2,1280]{2,1,0:T(2,128)(2,1)S(1)}, bf16[4,2,1280]{2,1,0:T(2,128)(2,1)S(1)}, u32[]{:S(2)}, u32[]{:S(2)}) %collective-permute-start.4) | collective-permute-done | bytes 20512 | tf_op jit(solution)/shard_map/ppermute | solution.py:30
  45.2 0.1 pad_maximum_fusion.2
  45.3 0.4 reshape.140
  45.7 1.2 %fusion.133 = (bf16[2,4,80,16]{3,2,1,0:T(8,128)(2,1)S(1)}, bf16[2,4,80,16]{3,2,1,0:T(8,128)(2,1)}, bf16[2,4,80,16]{3,2,1,0:T(8,128)(2,1)}, bf16[2,4,80,16]{3,2,1...) fusion(bf16[4,6,80,16]{3,2,1,0:T(8,128)(2,1)S(1)} %reshape.140), kind=kLoop, calls=%fused_computation.176 | loop fusion | bytes 1208320 | tf_op jit(solution)/shard_map/slice | solution.py:76
  46.9 0.3 pad_slice_fusion.6
  47.3 0.1 fusion.134
  47.4 3.8 %concatenate.45 = bf16[2,4,80,432]{3,2,1,0:T(8,128)(2,1)S(1)} concatenate(bf16[2,4,80,16]{3,2,1,0:T(8,128)(2,1)S(1)} %get-tuple-element.72, bf16[2,4,80,16]{3,2,1,0:T(8,128)(2,1)S(1)} %get-tuple-element.71, bf16[2,4,80,16]{3,2,1,0:T(8,128)(2,1)S(1)} %get-tuple-element.47, bf16[2,4,80,16]{3,2,1,0:T(8,128)(2,1)S(1)} %get-tuple-element.48, ...), dimensions={3} | concatenate | bytes 1105920 | tf_op jit(solution)/shard_map/concatenate | solution.py:83
  51.2 1.6 %multiply_reduce_fusion = (f32[2,4,80]{2,1,0:T(4,128)S(1)}, f32[2,4,80,384]{3,2,1,0:T(8,128)S(1)}) fusion(bf16[2,4,80,432]{3,2,1,0:T(8,128)(2,1)S(1)} %concatenate.45, bf16[432,384]{1,0:T(8,128)(2,1)} %param.25), kind=kOutput, calls=%fused_computation.87 | convolution fusion | flops 212827520 | bytes 1870336 | tf_op jit(solution)/shard_map/dot_general | solution.py:83
  52.7 0.4 fusion.96
  53.1 0.1 broadcast_in_dim.37
  53.2 2.3 %broadcast_in_dim.38 = bf16[2,8,80,2,384]{4,3,2,1,0:T(2,128)(2,1)} broadcast(bf16[2,8,80,384]{3,2,1,0:T(8,128)(2,1)S(1)} %bitcast.104), dimensions={0,1,2,4} | broadcast | bytes 2949120 | tf_op jit(solution)/shard_map/broadcast_in_dim | solution.py:93
  55.5 4.3 %reshape.117 = bf16[2,8,160,384]{3,2,1,0:T(8,128)(2,1)S(1)} reshape(bf16[2,8,80,2,384]{4,3,2,1,0:T(2,128)(2,1)} %broadcast_in_dim.38) | data formatting | bytes 3932160 | tf_op jit(solution)/shard_map/reshape | solution.py:93
  59.8 0.1 slice.338
  60.0 1.6 %collective-permute-start.5 = (bf16[2,6,160,384]{3,2,1,0:T(8,128)(2,1)S(1)}, bf16[2,6,160,384]{3,2,1,0:T(8,128)(2,1)}, u32[]{:S(2)}, u32[]{:S(2)}) collective-permute-start(bf16[2,6,160,384]{3,2,1,0:T(8,128)(2,1)S(1)} %slice.338), channel_id=1, source_target_pairs={{0,1},{2,3},{4,5},{6,7},{8,9},{10,11},{12,13},{14,15},{16,17},{18,... | collective-permute-start | bytes 4423688 | tf_op jit(solution)/shard_map/ppermute | solution.py:17
  61.6 4.1 %pad_maximum_fusion.1 = bf16[2,6,61440]{2,1,0:T(8,128)(2,1)} fusion(bf16[2,1,61440]{2,1,0:T(2,128)(2,1)} %collective-permute-done.1, bf16[2,4,61440]{2,1,0:T(4,128)(2,1)S(1)} %copy-done.3, bf16[2,1,61440]{2,1,0:T(2,128)(2,1)} %collective-permute-done), kind=kLoop, calls=%fused_computation.65 | loop fusion | flops 4423680 | bytes 2949120 | tf_op jit(solution)/shard_map/concatenate | solution.py:26
  65.7 4.3 %reshape.139 = bf16[2,6,160,384]{3,2,1,0:T(8,128)(2,1)} reshape(bf16[2,6,61440]{2,1,0:T(8,128)(2,1)} %pad_maximum_fusion.1) | data formatting | bytes 2949120 | tf_op jit(solution)/shard_map/reshape | solution.py:188
  70.0 0.3 fusion.131
  70.3 1.0 %copy-done.4 = bf16[2,6,160,384]{3,2,1,0:T(8,128)(2,1)S(1)} copy-done((bf16[2,6,160,384]{3,2,1,0:T(8,128)(2,1)S(1)}, bf16[2,6,160,384]{3,2,1,0:T(8,128)(2,1)}, u32[]{:S(2)}) %copy-start.4) | copy-done | bytes 1474584
  71.4 1.5 %broadcast_select_fusion = bf16[2,6,160,384]{3,2,1,0:T(8,128)(2,1)S(1)} fusion(bf16[2,6,160,384]{3,2,1,0:T(8,128)(2,1)S(1)} %copy-done.4, bf16[2,6,160,384]{3,2,1,0:T(8,128)(2,1)} %collective-permute-done.5, pred[]{:T(512)S(6)} %eq.25), kind=kLoop, calls=%fused_computation.68 | loop fusion | flops 737280 | bytes 4423681 | tf_op jit(solution)/shard_map/jit(_where)/select_n | solution.py:189
  72.9 0.7 fusion.93
  73.7 0.3 pad_maximum_fusion
  74.0 4.2 %pad_slice_fusion.25 = (bf16[2,4,160,384]{3,2,1,0:T(8,128)(2,1)S(1)}, bf16[2,4,160,384]{3,2,1,0:T(8,128)(2,1)S(1)}, bf16[2,4,160,384]{3,2,1,0:T(8,128)(2,1)S(1)}...) fusion(bf16[4,6,160,384]{3,2,1,0:T(8,128)(2,1)S(1)} %pad_maximu, ...), kind=kLoop, calls=%fused_computation.157 | loop fusion | bytes 11796480 | tf_op jit(solution)/shard_map/slice | solution.py:106
  78.3 4.5 %pad_slice_fusion.24 = (bf16[2,4,160,384]{3,2,1,0:T(8,128)(2,1)S(1)}, bf16[2,4,160,384]{3,2,1,0:T(8,128)(2,1)S(1)}, bf16[2,4,160,384]{3,2,1,0:T(8,128)(2,1)S(1)}...) fusion(bf16[4,6,160,384]{3,2,1,0:T(8,128)(2,1)S(1)} %pad_maximu, ...), kind=kLoop, calls=%fused_computation.156 | loop fusion | bytes 11796480 | tf_op jit(solution)/shard_map/slice | solution.py:106
  82.8 1.0 %fusion.6 = f32[2,4,160,192]{3,2,1,0:T(8,128)S(1)} fusion(bf16[2,4,160,384]{3,2,1,0:T(8,128)(2,1)S(1)} %get-tuple-element.20, bf16[2,4,160,384]{3,2,1,0:T(8,128)(2,1)S(1)} %get-tuple-element.42, bf16[2,4,160,384]{3,2,1,0:T(8,128)(2,1)S(1)} %get-tuple-element.14, bf16[10368,192]{0,1:T(8,128)(2,1)S(1)} %copy-done.7), kind=kOutput, calls=%fused_computation.15 | convolution fusion | flops 575078400 | bytes 4374528 | tf_op jit(solution)/shard_map/dot_general | solution.py:110
  83.8 1.0 %fusion.12 = f32[2,4,160,192]{3,2,1,0:T(8,128)S(1)} fusion(bf16[2,4,160,384]{3,2,1,0:T(8,128)(2,1)S(1)} %get-tuple-element.22, bf16[2,4,160,384]{3,2,1,0:T(8,128)(2,1)S(1)} %get-tuple-element.43, bf16[2,4,160,384]{3,2,1,0:T(8,128)(2,1)S(1)} %get-tuple-element.21, bf16[10368,192]{0,1:T(8,128)(2,1)S(1)} %copy-done.7), kind=kOutput, calls=%fused_computation.21 | convolution fusion | flops 575078400 | bytes 4374528 | tf_op jit(solution)/shard_map/dot_general | solution.py:110
  84.9 1.0 %fusion.18 = f32[2,4,160,192]{3,2,1,0:T(8,128)S(1)} fusion(bf16[2,4,160,384]{3,2,1,0:T(8,128)(2,1)S(1)} %get-tuple-element.24, bf16[2,4,160,384]{3,2,1,0:T(8,128)(2,1)S(1)} %get-tuple-element.35, bf16[2,4,160,384]{3,2,1,0:T(8,128)(2,1)S(1)} %get-tuple-element.23, bf16[10368,192]{0,1:T(8,128)(2,1)S(1)} %copy-done.7), kind=kOutput, calls=%fused_computation.27 | convolution fusion | flops 575078400 | bytes 4374528 | tf_op jit(solution)/shard_map/dot_general | solution.py:110
  85.9 1.0 %fusion.24 = f32[2,4,160,192]{3,2,1,0:T(8,128)S(1)} fusion(bf16[2,4,160,384]{3,2,1,0:T(8,128)(2,1)S(1)} %get-tuple-element.27, bf16[2,4,160,384]{3,2,1,0:T(8,128)(2,1)S(1)} %get-tuple-element.36, bf16[2,4,160,384]{3,2,1,0:T(8,128)(2,1)S(1)} %get-tuple-element.25, bf16[10368,192]{0,1:T(8,128)(2,1)S(1)} %copy-done.7), kind=kOutput, calls=%fused_computation.33 | convolution fusion | flops 575078400 | bytes 4374528 | tf_op jit(solution)/shard_map/dot_general | solution.py:110
  86.9 1.0 %fusion.30 = f32[2,4,160,192]{3,2,1,0:T(8,128)S(1)} fusion(bf16[2,4,160,384]{3,2,1,0:T(8,128)(2,1)S(1)} %get-tuple-element.29, bf16[2,4,160,384]{3,2,1,0:T(8,128)(2,1)S(1)} %get-tuple-element.37, bf16[2,4,160,384]{3,2,1,0:T(8,128)(2,1)S(1)} %get-tuple-element.28, bf16[10368,192]{0,1:T(8,128)(2,1)S(1)} %copy-done.7), kind=kOutput, calls=%fused_computation.39 | convolution fusion | flops 575078400 | bytes 4374528 | tf_op jit(solution)/shard_map/dot_general | solution.py:110
  88.0 1.0 %fusion.36 = f32[2,4,160,192]{3,2,1,0:T(8,128)S(1)} fusion(bf16[2,4,160,384]{3,2,1,0:T(8,128)(2,1)S(1)} %get-tuple-element.31, bf16[2,4,160,384]{3,2,1,0:T(8,128)(2,1)S(1)} %get-tuple-element.40, bf16[2,4,160,384]{3,2,1,0:T(8,128)(2,1)S(1)} %get-tuple-element.30, bf16[10368,192]{0,1:T(8,128)(2,1)S(1)} %copy-done.7), kind=kOutput, calls=%fused_computation.45 | convolution fusion | flops 575078400 | bytes 4374528 | tf_op jit(solution)/shard_map/dot_general | solution.py:110
  89.0 1.1 %fusion.80 = f32[2,4,160,192]{3,2,1,0:T(8,128)S(1)} fusion(f32[2,4,160,192]{3,2,1,0:T(8,128)S(1)} %fusion.36, f32[2,4,160,192]{3,2,1,0:T(8,128)S(1)} %fusion.30, f32[2,4,160,192]{3,2,1,0:T(8,128)S(1)} %fusion.24, f32[2,4,160,192]{3,2,1,0:T(8,128)S(1)} %fusion.18, f32[2,4,160,192]{3,2,1,0:T(8,128)S(1)} %fusion.12, f32[2,4,160,192]{3,2,1,0:T(8,128)S(1)} %fusion.6, ...), kind=kOutput, calls=%fused_computation.76 | convolution fusion | flops 576552960 | bytes 12238848 | tf_op jit(solution)/shard_map/dot_general | solution.py:110
  90.1 1.0 %fusion.62 = f32[2,4,160,192]{3,2,1,0:T(8,128)S(1)} fusion(f32[2,4,160,192]{3,2,1,0:T(8,128)S(1)} %fusion.80, bf16[2,4,160,384]{3,2,1,0:T(8,128)(2,1)S(1)} %get-tuple-element.33, bf16[2,4,160,384]{3,2,1,0:T(8,128)(2,1)S(1)} %get-tuple-element.39, bf16[2,4,160,384]{3,2,1,0:T(8,128)(2,1)S(1)} %get-tuple-element.32, bf16[10368,192]{0,1:T(8,128)(2,1)S(1)} %copy-done.7), kind=kOutput, calls=%fused_computation.70 | convolution fusion | flops 575324160 | bytes 5685248 | tf_op jit(solution)/shard_map/dot_general | solution.py:110
  91.2 0.0 copy-start.1
  91.2 2.2 %fusion.83 = bf16[2,4,160,192]{3,2,1,0:T(8,128)(2,1)S(1)} fusion(f32[2,4,160,192]{3,2,1,0:T(8,128)S(1)} %fusion.62, bf16[2,4,160,384]{3,2,1,0:T(8,128)(2,1)S(1)} %get-tuple-element.26, bf16[2,4,160,384]{3,2,1,0:T(8,128)(2,1)S(1)} %get-tuple-element.38, bf16[2,4,160,384]{3,2,1,0:T(8,128)(2,1)S(1)} %get-tuple-element.12, bf16[10368,192]{0,1:T(8,128)(2,1)} %param.27), kind=kOutput, calls=%fused_computation.77 | convolution fusion | flops 575569920 | bytes 4866048 | tf_op jit(solution)/shard_map/dot_general | solution.py:110
  93.4 1.5 %reshape.118 = bf16[2,4,30720]{2,1,0:T(4,128)(2,1)} reshape(bf16[2,4,160,192]{3,2,1,0:T(8,128)(2,1)S(1)} %fusion.83) | data formatting | bytes 983040 | tf_op jit(solution)/shard_map/reshape | solution.py:195
  (37 shorter events, 0.2 us)
Async XLA Ops:
  0.6 10.2 %copy-start = (bf16[2,1,4,61440]{3,2,1,0:T(4,128)(2,1)S(1)}, bf16[2,1,4,61440]{3,2,1,0:T(4,128)(2,1)}, u32[]{:S(2)}) copy-start(bf16[2,1,4,61440]{3,2,1,0:T(4,128)(2,1)} %param.24) | copy-start | bytes 2949124
  0.6 2.5 %copy-start.13 = (bf16[4,8,40,128]{3,2,1,0:T(8,128)(2,1)S(1)}, bf16[4,8,40,128]{3,2,1,0:T(8,128)(2,1)}, u32[]{:S(2)}) copy-start(bf16[4,8,40,128]{3,2,1,0:T(8,128)(2,1)} %param.16) | copy-start | bytes 983044
  3.1 7.7 %copy-start.12 = (s32[2,2,16]{2,1,0:T(2,128)S(1)}, s32[2,2,16]{2,1,0:T(2,128)}, u32[]{:S(2)}) copy-start(s32[2,2,16]{2,1,0:T(2,128)} %param.22) | copy-start | bytes 772
  4.5 20.1 %all-to-all-start = ((bf16[2,8,40,128]{3,2,0,1:T(8,128)(2,1)}), bf16[2,8,40,128]{3,2,0,1:T(8,128)(2,1)S(1)}, u32[]{:S(2)}, u32[]{:S(2)}) async-start(bf16[2,8,40,128]{3,2,0,1:T(8,128)(2,1)} %copy.49), calls=%async_computation | async-start | bytes 327680 | tf_op jit(solution)/shard_map/all_to_all | solution.py:147
  11.0 13.6 %copy-start.10 = (bf16[1024]{0:T(1024)(128)(2,1)S(1)}, bf16[1024]{0:T(1024)(128)(2,1)}, u32[]{:S(2)}) copy-start(bf16[1024]{0:T(1024)(128)(2,1)} %param.17) | copy-start | bytes 6148
  14.6 10.4 %copy-start.5 = (bf16[1024,64]{0,1:T(8,128)(2,1)S(1)}, bf16[1024,64]{0,1:T(8,128)(2,1)}, u32[]{:S(2)}) copy-start(bf16[1024,64]{0,1:T(8,128)(2,1)} %param.18) | copy-start | bytes 393220
  14.6 11.3 %copy-start.8 = (bf16[2,2,1280]{2,1,0:T(2,128)(2,1)S(1)}, bf16[2,2,1280]{2,1,0:T(2,128)(2,1)}, u32[]{:S(2)}) copy-start(bf16[2,2,1280]{2,1,0:T(2,128)(2,1)} %param.19) | copy-start | bytes 30724
  15.1 1.0 %copy-start.2 = (bf16[2,4,61440]{2,1,0:T(4,128)(2,1)}, bf16[2,4,61440]{2,1,0:T(4,128)(2,1)S(1)}, u32[]{:S(2)}) copy-start(bf16[2,4,61440]{2,1,0:T(4,128)(2,1)S(1)} %bitcast_multiply_fusion) | copy-start | bytes 2949124
  16.1 11.2 %copy-start.9 = (bf16[2,1,2,1280]{3,2,1,0:T(2,128)(2,1)S(1)}, bf16[2,1,2,1280]{3,2,1,0:T(2,128)(2,1)}, u32[]{:S(2)}) copy-start(bf16[2,1,2,1280]{3,2,1,0:T(2,128)(2,1)} %param.23) | copy-start | bytes 30724
  16.1 20.2 %copy-start.11 = (bf16[384]{0:T(512)(128)(2,1)S(1)}, bf16[384]{0:T(512)(128)(2,1)}, u32[]{:S(2)}) copy-start(bf16[384]{0:T(512)(128)(2,1)} %param.26) | copy-start | bytes 2308
  17.7 43.9 %collective-permute-start = (bf16[2,1,61440]{2,1,0:T(2,128)(2,1)}, bf16[2,1,61440]{2,1,0:T(2,128)(2,1)}, u32[]{:S(2)}, u32[]{:S(2)}) collective-permute-start(bf16[2,1,61440]{2,1,0:T(2,128)(2,1)} %get-tuple-element.44), channel_id=1, source_target_pairs={{0,2},{2,4},{4,6},{6,8},{8,10},{10,12},{12,14},{1,3},{3,5},{5,7},{... | collective-permute-start | bytes 737288 | tf_op jit(solution)/shard_map/ppermute | solution.py:28
  20.8 40.8 %collective-permute-start.1 = (bf16[2,1,61440]{2,1,0:T(2,128)(2,1)}, bf16[2,1,61440]{2,1,0:T(2,128)(2,1)}, u32[]{:S(2)}, u32[]{:S(2)}) collective-permute-start(bf16[2,1,61440]{2,1,0:T(2,128)(2,1)} %get-tuple-element.45), channel_id=1, source_target_pairs={{2,0},{4,2},{6,4},{8,6},{10,8},{12,10},{14,12},{3,1},{5,3},{7,5},{... | collective-permute-start | bytes 737288 | tf_op jit(solution)/shard_map/ppermute | solution.py:30
  25.9 21.3 %copy-start.6 = (bf16[2,2,1280]{2,1,0:T(2,128)(2,1)}, bf16[2,2,1280]{2,1,0:T(2,128)(2,1)S(1)}, u32[]{:S(2)}) copy-start(bf16[2,2,1280]{2,1,0:T(2,128)(2,1)S(1)} %subtract_convert_fusion) | copy-start | bytes 30724
  25.9 4.0 %collective-permute-start.2 = (bf16[2,2,1280]{2,1,0:T(2,128)(2,1)S(1)}, bf16[2,2,1280]{2,1,0:T(2,128)(2,1)S(1)}, u32[]{:S(2)}, u32[]{:S(2)}) collective-permute-start(bf16[2,2,1280]{2,1,0:T(2,128)(2,1)S(1)} %subtract_convert_fusion), channel_id=1, source_target_pairs={{0,1},{2,3},{4,5},{6,7},{8,9},{10,11},{12,13},{14,15},{16,17},{18,... | collective-permute-start | bytes 30728 | tf_op jit(solution)/shard_map/ppermute | solution.py:17
  30.0 12.6 %collective-permute-start.3 = (bf16[4,2,1280]{2,1,0:T(2,128)(2,1)S(1)}, bf16[4,2,1280]{2,1,0:T(2,128)(2,1)S(1)}, u32[]{:S(2)}, u32[]{:S(2)}) collective-permute-start(bf16[4,2,1280]{2,1,0:T(2,128)(2,1)S(1)} %pad_maximum_fusion.3), channel_id=1, source_target_pairs={{0,2},{2,4},{4,6},{6,8},{8,10},{10,12},{12,14},{1,3},{3,5},{5,7},{... | collective-permute-start | bytes 61448 | tf_op jit(solution)/shard_map/ppermute | solution.py:28
  32.2 13.0 %collective-permute-start.4 = (bf16[4,2,1280]{2,1,0:T(2,128)(2,1)S(1)}, bf16[4,2,1280]{2,1,0:T(2,128)(2,1)S(1)}, u32[]{:S(2)}, u32[]{:S(2)}) collective-permute-start(bf16[4,2,1280]{2,1,0:T(2,128)(2,1)S(1)} %pad_maximum_fusion.3), channel_id=1, source_target_pairs={{2,0},{4,2},{6,4},{8,6},{10,8},{12,10},{14,12},{3,1},{5,3},{7,5},{... | collective-permute-start | bytes 61448 | tf_op jit(solution)/shard_map/ppermute | solution.py:30
  59.8 1.8 %copy-start.3 = (bf16[2,4,61440]{2,1,0:T(4,128)(2,1)S(1)}, bf16[2,4,61440]{2,1,0:T(4,128)(2,1)}, u32[]{:S(2)}) copy-start(bf16[2,4,61440]{2,1,0:T(4,128)(2,1)} %copy-done.2) | copy-start | bytes 2949124
  60.0 10.4 %collective-permute-start.5 = (bf16[2,6,160,384]{3,2,1,0:T(8,128)(2,1)S(1)}, bf16[2,6,160,384]{3,2,1,0:T(8,128)(2,1)}, u32[]{:S(2)}, u32[]{:S(2)}) collective-permute-start(bf16[2,6,160,384]{3,2,1,0:T(8,128)(2,1)S(1)} %slice.338), channel_id=1, source_target_pairs={{0,1},{2,3},{4,5},{6,7},{8,9},{10,11},{12,13},{14,15},{16,17},{18,... | collective-permute-start | bytes 4423688 | tf_op jit(solution)/shard_map/ppermute | solution.py:17
  70.0 1.4 %copy-start.4 = (bf16[2,6,160,384]{3,2,1,0:T(8,128)(2,1)S(1)}, bf16[2,6,160,384]{3,2,1,0:T(8,128)(2,1)}, u32[]{:S(2)}) copy-start(bf16[2,6,160,384]{3,2,1,0:T(8,128)(2,1)} %reshape.139) | copy-start | bytes 4423684
  78.3 4.5 %copy-start.7 = (bf16[10368,192]{0,1:T(8,128)(2,1)S(1)}, bf16[10368,192]{0,1:T(8,128)(2,1)}, u32[]{:S(2)}) copy-start(bf16[10368,192]{0,1:T(8,128)(2,1)} %param.27) | copy-start | bytes 11943940
  91.2 3.7 %copy-start.1 = (bf16[2,1,4,61440]{3,2,1,0:T(4,128)(2,1)S(1)}, bf16[2,1,4,61440]{3,2,1,0:T(4,128)(2,1)}, u32[]{:S(2)}) copy-start(bf16[2,1,4,61440]{3,2,1,0:T(4,128)(2,1)} %param.24) | copy-start | bytes 2949124
where the time goes:
time: 95.9 us; the launch traced here: 94.9 us
  local copies, waits for them, and re-layouts  32.8 us (34%)
  starting transfers between devices  20.9 us (22%)
  matrix products  15.1 us (16%)
  waiting for transfers between devices  9.01 us (9%)
  other arithmetic  8.65 us (9%)
  blocking collectives  5.97 us (6%)
  between operations  2.53 us (3%)
    dot_general x9, matrix products, second_conv(): jnp.dot(stacked, weight_block, preferred_element_type=jnp.float32)  10.5 us
    slice x3, local copies, waits for them, and re-layouts, second_conv(): layer_slab[:, :, step_w:step_w + col_count]  9.07 us
    ppermute x2, starting transfers between devices, extended_2(): lax.ppermute(head, axis, [((i + 1) % count, i) for i in range(ends)])  7.08 us
    ppermute x2, waiting for transfers between devices, extended_2(): lax.ppermute(tail, axis, [(i, (i + 1) % count) for i in range(ends)])  6.38 us
    all_to_all x1, starting transfers between devices, body(): lax.all_to_all(attended, 'seq', split_axis=1, concat_axis=3, tiled=True)  5.61 us
    ppermute x2, starting transfers between devices, extended_2(): lax.ppermute(tail, axis, [(i, (i + 1) % count) for i in range(ends)])  5.27 us
    reshape x1, local copies, waits for them, and re-layouts, body(): cached_rimmed = cached_rimmed.reshape(earlier_feature.shape)  4.32 us
    reshape x1, local copies, waits for them, and re-layouts, upsample(): return jnp.repeat(jnp.repeat(activated, 2, axis=1), 2, axis=2)  4.28 us
  transfers between devices with their start and end apart: 7, of which 2 were waited for; matrix products, arithmetic and copies ran while one was open for 29% of the time, Pallas kernels for 0%

commit v1 on v0

v1 whole, which is shorter than its diff:
```python
import jax
import jax.numpy as jnp
from jax import lax
from jax.experimental import pallas as pl
from jax.experimental.pallas import tpu as pltpu
from jax.sharding import PartitionSpec as P

NSTEPS = 16
CSLOTS = 2
SHIFT_FACTOR = 5.0
NORM_EPSILON = 1e-06
BF = jnp.bfloat16
F32 = jnp.float32
VMEM_LIMIT = 56 << 20


def params(dims=0):
    semantics = ("arbitrary",) * dims if dims else None
    return pltpu.CompilerParams(dimension_semantics=semantics, vmem_limit_bytes=VMEM_LIMIT)


def dot(left, right):
    return jnp.dot(left, right, preferred_element_type=F32)


def whole():
    return pl.BlockSpec(memory_space=pltpu.VMEM)


def smem():
    return pl.BlockSpec(memory_space=pltpu.SMEM)


def attention_kernel(q_ref, k_ref, v_ref, gain_ref, weight_ref, out_ref, *, cols, rows_total):
    frames, block, head_size = q_ref.shape
    rows = block // cols
    step = pl.program_id(0)
    if rows_total == rows:
        first = 0
    else:
        first = step * rows
    scale = 1.4426950408889634 / head_size**0.5
    keys = k_ref[...]
    values = jnp.concatenate([v_ref[...], jnp.ones_like(v_ref[...])], axis=1)
    gain = gain_ref[...].astype(F32)
    weight = weight_ref[...].astype(F32)
    none = jnp.zeros_like(weight)
    chosen = lax.broadcasted_iota(jnp.int32, (8, head_size), 0)
    total = None
    squares = []
    for f in range(frames):
        scores = lax.dot_general(
            q_ref[f], keys, (((1,), (1,)), ((), ())), preferred_element_type=F32
        )
        row_max = jnp.max(scores, axis=1, keepdims=True)
        weights = jnp.exp2((scores - row_max) * scale).astype(BF)
        blended = dot(weights, values)
        attended = (blended[:, :head_size] / blended[:, head_size:]).astype(BF).astype(F32)
        side = [none] * frames
        side[f] = weight
        wide = jnp.concatenate(side, axis=1).astype(BF)
        part = dot((attended * gain).astype(BF), wide)
        total = part if total is None else total + part
        squares.append(attended * attended)

    @pl.when(step == 0)
    def _():
        out_ref[0, 0] = jnp.zeros(out_ref.shape[2:], BF)
        out_ref[rows_total - 1, 2] = jnp.zeros(out_ref.shape[2:], BF)

    for r in range(rows):
        sums = None
        for f in range(frames):
            piece = squares[f][r * cols : (r + 1) * cols].astype(BF)
            line = lax.dot_general(
                (chosen == f).astype(F32).astype(BF),
                piece,
                (((1,), (1,)), ((), ())),
                preferred_element_type=F32,
            )
            sums = line if sums is None else sums + line
        lanes = total.shape[1]
        sums = jnp.concatenate([sums, jnp.zeros((8, lanes - cols), F32)], axis=1)
        unit = jnp.concatenate([total[r * cols : (r + 1) * cols], sums], axis=0).astype(BF)
        row = first + r
        out_ref[row, 1] = unit

        @pl.when(row + 1 < rows_total)
        def _():
            out_ref[jnp.minimum(row + 1, rows_total - 1), 0] = unit

        @pl.when(row > 0)
        def _():
            out_ref[jnp.maximum(row - 1, 0), 2] = unit


def attention(queries, keys, values, final_gain, out_weight, slab):
    frames, rows_total, cols, head_size = queries.shape
    q = queries.reshape(frames, rows_total * cols, head_size)
    k = keys.reshape(-1, head_size)
    v = values.reshape(-1, head_size)
    rows = 4 if rows_total % 4 == 0 else rows_total
    width = out_weight.shape[1]
    lanes = frames * width
    unit = cols + 8

    def kernel(slab_ref, *refs):
        attention_kernel(*refs, cols=cols, rows_total=rows_total)

    grid_spec = pltpu.PrefetchScalarGridSpec(
        num_scalar_prefetch=1,
        grid=(rows_total // rows,),
        in_specs=[
            pl.BlockSpec((frames, rows * cols, head_size), lambda i, s: (0, i, 0)),
            pl.BlockSpec(k.shape, lambda i, s: (0, 0)),
            pl.BlockSpec(v.shape, lambda i, s: (0, 0)),
            pl.BlockSpec((1, head_size), lambda i, s: (0, s[0])),
            pl.BlockSpec((head_size, width), lambda i, s: (s[0], 0)),
        ],
        out_specs=pl.BlockSpec((rows_total, 3, unit, lanes), lambda i, s: (0, 0, 0, 0)),
    )
    count = frames * rows_total * cols
    return pl.pallas_call(
        kernel,
        grid_spec=grid_spec,
        out_shape=jax.ShapeDtypeStruct((rows_total, 3, unit, lanes), BF),
        compiler_params=params(1),
        cost_estimate=pl.CostEstimate(
            flops=6 * count * k.shape[0] * head_size,
            bytes_accessed=2 * (q.size + k.size + v.size),
            transcendentals=count * k.shape[0],
        ),
        name="attention",
    )(slab, q, k, v, final_gain.reshape(1, -1), out_weight)


def prepare_kernel(span_ref, place_ref, flags_ref, cache_ref, small_ref, own_ref, up_ref, down_ref, scr):
    tiles, rows, lanes = cache_ref.shape[1:]
    cols, channels = own_ref.shape[2:]
    pieces = channels // lanes
    slot = lax.rem(span_ref[0], CSLOTS)
    coarse = rows // 2
    flags = [
        flags_ref[slot, place_ref[1], place_ref[0] * coarse + r].astype(F32) for r in range(coarse)
    ]

    def unpack(i, carry):
        for n in range(16):
            at = i * 16 + n
            scr[pl.ds(pl.multiple_of(at * rows, rows), rows), :] = cache_ref[0, at].astype(F32)
        return carry

    lax.fori_loop(0, tiles // 16, unpack, 0)
    for r in range(rows):
        for b in range(2):
            for q in range(pieces):
                start = (b * pieces + q) * rows + r
                piece = scr[pl.ds(start, cols, stride=2 * pieces * rows), :]
                piece = (piece * flags[r // 2]).astype(BF)
                own_ref[r, b, :, q * lanes : (q + 1) * lanes] = piece
                if r == 0:
                    up_ref[b * cols : (b + 1) * cols, q * lanes : (q + 1) * lanes] = piece
                if r == rows - 1:
                    down_ref[b * cols : (b + 1) * cols, q * lanes : (q + 1) * lanes] = piece
    extra = small_ref[...]
    up_ref[2 * cols :, :] = extra
    down_ref[2 * cols :, :] = extra


def prepare(span_index, place, cache_flags, feature_cache, small, channels):
    slots, _, rows, width = feature_cache.shape
    tiles = width // 128
    view = feature_cache.reshape(slots, rows, tiles, 128).transpose(0, 2, 1, 3)
    cols = width // channels // 2
    halo = 2 * cols + small.shape[0]
    grid_spec = pltpu.PrefetchScalarGridSpec(
        num_scalar_prefetch=3,
        grid=(1,),
        in_specs=[
            pl.BlockSpec((1, tiles, rows, 128), lambda i, s, p, f: (lax.rem(s[0], CSLOTS), 0, 0, 0)),
            pl.BlockSpec(small.shape, lambda i, s, p, f: (0, 0)),
        ],
        out_specs=[
            pl.BlockSpec((rows, 2, cols, channels), lambda i, s, p, f: (0, 0, 0, 0)),
            pl.BlockSpec((halo, channels), lambda i, s, p, f: (0, 0)),
            pl.BlockSpec((halo, channels), lambda i, s, p, f: (0, 0)),
        ],
        scratch_shapes=[pltpu.VMEM((tiles * rows, 128), F32)],
    )
    return pl.pallas_call(
        prepare_kernel,
        grid_spec=grid_spec,
        out_shape=[
            jax.ShapeDtypeStruct((rows, 2, cols, channels), BF),
            jax.ShapeDtypeStruct((halo, channels), BF),
            jax.ShapeDtypeStruct((halo, channels), BF),
        ],
        compiler_params=params(1),
        cost_estimate=pl.CostEstimate(
            flops=rows * width, bytes_accessed=6 * rows * width, transcendentals=0
        ),
        name="prepare",
    )(span_index, place, cache_flags, view, small)


def shift_down(array):
    moved = pltpu.roll(array, 1, axis=0)
    rows = lax.broadcasted_iota(jnp.int32, array.shape, 0)
    return jnp.where(rows == 0, 0.0, moved)


def shift_up(array):
    count = array.shape[0]
    moved = pltpu.roll(array, count - 1, axis=0)
    rows = lax.broadcasted_iota(jnp.int32, array.shape, 0)
    return jnp.where(rows == count - 1, 0.0, moved)


def cached_kernel(place_ref, own_ref, above_ref, below_ref, weight_ref, out_ref, var):
    rows, _, cols, channels = own_ref.shape
    for r in range(rows + 2):
        if r == 0:
            even, odd = above_ref[:cols], above_ref[cols : 2 * cols]
        elif r == rows + 1:
            even, odd = below_ref[:cols], below_ref[cols : 2 * cols]
        else:
            even, odd = own_ref[r - 1, 0], own_ref[r - 1, 1]
        var[0, r] = shift_down(odd.astype(F32)).astype(BF)
        var[1, r] = even
        var[2, r] = odd
        var[3, r] = shift_up(even.astype(F32)).astype(BF)

    def contribution(base):
        sides = []
        for b in range(2):
            total = None
            for h in range(3):
                left = jnp.concatenate(
                    [
                        var[b + w, h : h + rows].reshape(rows * cols, channels)
                        for w in range(3)
                    ],
                    axis=1,
                )
                start = pl.multiple_of(base + h * 3 * channels, channels)
                part = dot(left, weight_ref[pl.ds(start, 3 * channels), :])
                total = part if total is None else total + part
            sides.append(total)
        return jnp.concatenate(sides, axis=1)

    head = place_ref[1]
    first = contribution(head * (9 * channels))
    out_ref[0] = first.astype(BF).reshape(out_ref.shape[1:])

    @pl.when(head == 0)
    def _():
        out_ref[1] = jnp.zeros(out_ref.shape[1:], BF)

    @pl.when(head != 0)
    def _():
        out_ref[1] = contribution(0).astype(BF).reshape(out_ref.shape[1:])


def cached(place, own, above, below, weight):
    rows, _, cols, channels = own.shape
    return pl.pallas_call(
        cached_kernel,
        in_specs=[smem(), whole(), whole(), whole(), whole()],
        out_specs=whole(),
        out_shape=jax.ShapeDtypeStruct((2, rows, cols, 2 * weight.shape[1]), BF),
        scratch_shapes=[pltpu.VMEM((4, rows + 2, cols, channels), BF)],
        compiler_params=params(),
        cost_estimate=pl.CostEstimate(
            flops=2 * 2 * rows * 2 * cols * 9 * channels * weight.shape[1],
            bytes_accessed=2 * (own.size + weight.size),
            transcendentals=0,
        ),
        name="cached",
    )(place, own, above, below, weight)


def spread(source_ref, var):
    frames, coarse = source_ref.shape[:2]
    for f in range(frames):
        for r in range(coarse):
            plain = source_ref[f, r]
            wide = plain.astype(F32)
            var[0, f, r] = shift_down(wide).astype(BF)
            var[1, f, r] = plain
            var[2, f, r] = shift_up(wide).astype(BF)


def upsampled_part(var, weight_ref, frame, step_t, b):
    coarse, cols, channels = var.shape[2:]
    fine = 2 * (coarse - 2)
    total = None
    for h in range(3):
        lines = []
        for row in range(fine):
            at = (row + h - 1) // 2 + 1
            lines.append(
                jnp.concatenate(
                    [var[(b + w + 1) // 2, frame, at] for w in range(3)], axis=1
                )
            )
        start = (step_t * 3 + h) * 3 * channels
        part = dot(jnp.concatenate(lines, axis=0), weight_ref[start : start + 3 * channels, :])
        total = part if total is None else total + part
    return total


def own_kernel(source_ref, weight_ref, out_ref, var):
    spread(source_ref, var)
    width = weight_ref.shape[1]
    for f, pairs in ((0, ((0, 2),)), (1, ((0, 1), (1, 2)))):
        sides = []
        for b in range(2):
            total = None
            for frame, step_t in pairs:
                part = upsampled_part(var, weight_ref, frame, step_t, b)
                total = part if total is None else total + part
            sides.append(total)
        out_ref[f] = jnp.concatenate(sides, axis=1).reshape(out_ref.shape[1:])


def own_part(activated, weight):
    frames, coarse, cols, channels = activated.shape
    fine = 2 * (coarse - 2)
    return pl.pallas_call(
        own_kernel,
        in_specs=[whole(), whole()],
        out_specs=whole(),
        out_shape=jax.ShapeDtypeStruct((frames, fine, cols, 2 * weight.shape[1]), F32),
        scratch_shapes=[pltpu.VMEM((3, frames, coarse, cols, channels), BF)],
        compiler_params=params(),
        cost_estimate=pl.CostEstimate(
            flops=3 * 2 * fine * 2 * cols * 9 * channels * weight.shape[1],
            bytes_accessed=2 * (activated.size + weight.size),
            transcendentals=0,
        ),
        name="own_part",
    )(activated, weight)


def prior_kernel(place_ref, source_ref, cached_ref, own_ref, weight_ref, out_ref, var, total_ref, scr):
    frames, fine, cols, width = own_ref.shape
    head = place_ref[1]

    @pl.when(head == 0)
    def _():
        total_ref[...] = own_ref[...] + (
            cached_ref[...].astype(F32) + source_ref[...].astype(F32)
        )

    @pl.when(head != 0)
    def _():
        spread(source_ref, var)
        for f, pairs in ((0, ((0, 0), (1, 1))), (1, ((1, 0),))):
            sides = []
            for b in range(2):
                total = None
                for frame, step_t in pairs:
                    part = upsampled_part(var, weight_ref, frame, step_t, b)
                    total = part if total is None else total + part
                sides.append(total)
            both = jnp.concatenate(sides, axis=1).reshape(fine, cols, width)
            total_ref[f] = own_ref[f] + both

    pieces = width // 128
    for f in range(frames):
        for row in range(fine):
            for q in range(pieces):
                scr[pl.ds(q * fine + row, cols, stride=pieces * fine), :] = total_ref[
                    f, row, :, q * 128 : (q + 1) * 128
                ]

        def pack(i, carry):
            for n in range(16):
                at = i * 16 + n
                out_ref[f, at] = scr[pl.ds(pl.multiple_of(at * fine, fine), fine), :].astype(BF)
            return carry

        lax.fori_loop(0, out_ref.shape[1] // 16, pack, 0)


def prior_part(place, received, cached_sum, own_sum, weight):
    frames, coarse, cols, channels = received.shape
    _, fine, _, width = own_sum.shape
    tiles = cols * width // 128
    out = pl.pallas_call(
        prior_kernel,
        in_specs=[smem(), whole(), whole(), whole(), whole()],
        out_specs=whole(),
        out_shape=jax.ShapeDtypeStruct((frames, tiles, fine, 128), BF),
        scratch_shapes=[
            pltpu.VMEM((3, frames, coarse, cols, channels), BF),
            pltpu.VMEM(own_sum.shape, F32),
            pltpu.VMEM((tiles * fine, 128), F32),
        ],
        compiler_params=params(),
        cost_estimate=pl.CostEstimate(
            flops=3 * 2 * fine * 2 * cols * 9 * channels * weight.shape[1],
            bytes_accessed=2 * (received.size + weight.size),
            transcendentals=0,
        ),
        name="prior_part",
    )(place, received, cached_sum, own_sum, weight)
    return out.transpose(0, 2, 1, 3).reshape(frames, fine, cols * width)


def latent_kernel(step_ref, place_ref, parts_ref, own_ref, above_ref, below_ref, clean_ref, send_ref):
    sources, three, unit, lanes = parts_ref.shape
    cols = own_ref.shape[0]
    features = sources * 128
    fraction = 1.0 - step_ref[0].astype(F32) / NSTEPS
    fraction = jnp.full((1, lanes), fraction, F32)
    level = SHIFT_FACTOR * fraction / (1.0 + (SHIFT_FACTOR - 1.0) * fraction)
    total = parts_ref[0].astype(F32)
    for source in range(1, sources):
        total = total + parts_ref[source].astype(F32)
    half = lax.broadcasted_iota(jnp.int32, (cols, lanes), 1) < lanes // 2
    first_group = place_ref[1] == 0
    for k, small_ref in ((0, above_ref), (1, own_ref), (2, below_ref)):
        small = small_ref[...] if k == 1 else small_ref[small_ref.shape[0] - cols :]
        sums = jnp.transpose(total[k, cols:unit])[:cols]
        scale = lax.rsqrt(sums / features + NORM_EPSILON)
        scale = jnp.where(half, scale[:, 0:1], scale[:, 1:2])
        velocity = total[k, :cols] * scale
        clean = (small[:, :lanes].astype(F32) - level * velocity).astype(BF)
        clean_ref[k] = clean

        @pl.when(first_group)
        def _():
            send_ref[k] = clean

        @pl.when(jnp.logical_not(first_group))
        def _():
            send_ref[k] = small[:, lanes : 2 * lanes]


def latent(step_index, place, parts, own, above, below):
    sources, three, unit, lanes = parts.shape
    cols = own.shape[0]
    shape = jax.ShapeDtypeStruct((three, cols, lanes), BF)
    return pl.pallas_call(
        latent_kernel,
        in_specs=[smem(), smem(), whole(), whole(), whole(), whole()],
        out_specs=[whole(), whole()],
        out_shape=[shape, shape],
        compiler_params=params(),
        cost_estimate=pl.CostEstimate(
            flops=2 * parts.size, bytes_accessed=2 * parts.size, transcendentals=0
        ),
        name="latent",
    )(step_index, place, parts, own, above, below)


def first_kernel(
    place_ref, clean_ref, received_ref, own_ref, above_ref, below_ref, weight_ref, gain_ref, cached_ref, act_ref, send_ref, left, scr
):
    three, cols, lanes = clean_ref.shape
    frames, coarse = act_ref.shape[:2]
    channels = act_ref.shape[3]
    group = lanes // 4
    slot = lanes // 2
    part = group // 2
    head = place_ref[1]
    cached_old = jnp.concatenate(
        [
            above_ref[above_ref.shape[0] - cols :, lanes : 2 * lanes].astype(F32),
            own_ref[:, lanes : 2 * lanes].astype(F32),
            below_ref[below_ref.shape[0] - cols :, lanes : 2 * lanes].astype(F32),
        ],
        axis=0,
    )
    clean = jnp.concatenate([clean_ref[k].astype(F32) for k in range(three)], axis=0)
    arrived = jnp.concatenate([received_ref[k].astype(F32) for k in range(three)], axis=0)
    lane = lax.broadcasted_iota(jnp.int32, clean.shape, 1)
    line = lax.broadcasted_iota(jnp.int32, clean.shape, 0)
    at = lax.rem(line, cols)
    older = jnp.where(
        head == 0, jnp.where(lane < lanes // 2, cached_old, arrived), arrived
    )
    pieces = {}
    for source, x in enumerate((older, clean)):
        height = x.shape[0]
        before = jnp.where(at == 0, 0.0, pltpu.roll(x, 1, axis=0))
        after = jnp.where(at == cols - 1, 0.0, pltpu.roll(x, height - 1, axis=0))
        for f in range(2):
            for a in range(2):
                off = f * (lanes // 2) + a * group
                for side in range(2):
                    base = side * slot

                    def moved(array, shift):
                        shift = shift % lanes
                        return pltpu.roll(array, shift, axis=1) if shift else array

                    low = lane - base
                    even = jnp.where(
                        (low >= 0) & (low < part),
                        moved(before, base - off - part),
                        jnp.where(
                            (low >= part) & (low < 3 * part), moved(x, base + part - off), 0.0
                        ),
                    )
                    odd = jnp.where(
                        (low >= 0) & (low < 2 * part),
                        moved(x, base - off),
                        jnp.where(
                            (low >= 2 * part) & (low < 3 * part),
                            moved(after, base + 2 * part - off),
                            0.0,
                        ),
                    )
                    pieces[source * 2 + f, a, side, 0] = even
                    pieces[source * 2 + f, a, side, 1] = odd

    def piece(p, fo, ro, n):
        frame = fo + n // 3
        row = ro + n % 3
        k = row // 2
        return pieces[frame, row % 2, n % 2, p][k * cols : (k + 1) * cols]

    for p in range(2):
        for fo in range(frames):
            for ro in range(coarse):
                start = ((p * frames + fo) * coarse + ro) * cols
                for j in range(5):
                    block = piece(p, fo, ro, 2 * j)
                    if 2 * j + 1 < 9:
                        block = block + piece(p, fo, ro, 2 * j + 1)
                    left[start : start + cols, j * lanes : (j + 1) * lanes] = block.astype(BF)

    feat = dot(left[...], weight_ref[...])
    mean_square = jnp.mean(feat * feat, axis=-1, keepdims=True)
    normed = feat * lax.rsqrt(mean_square + NORM_EPSILON) * gain_ref[...].astype(F32)
    active = normed / (1.0 + jnp.exp(-normed))
    slab = place_ref[0]
    last = place_ref[2] - 1
    keep_first = jnp.where(slab == 0, 0.0, 1.0)
    keep_last = jnp.where(slab == last, 0.0, 1.0)
    for p in range(2):
        for fo in range(frames):
            for ro in range(coarse):
                start = ((p * frames + fo) * coarse + ro) * cols
                block = active[start : start + cols]
                if ro == 0:
                    block = block * keep_first
                if ro == coarse - 1:
                    block = block * keep_last
                to = (fo * coarse + ro) * 2 * cols + p
                for q in range(channels // 128):
                    scr[q, pl.ds(to, cols, stride=2), :] = block[:, q * 128 : (q + 1) * 128]
    for fo in range(frames):
        for ro in range(coarse):
            to = (fo * coarse + ro) * 2 * cols
            for q in range(channels // 128):
                act_ref[fo, ro, :, q * 128 : (q + 1) * 128] = scr[q, to : to + 2 * cols, :].astype(BF)

    @pl.when(head == 0)
    def _():
        send_ref[...] = act_ref[...]

    @pl.when(head != 0)
    def _():
        send_ref[...] = cached_ref[...]


def first(place, clean, received, own, above, below, weight, gain, cached_sum):
    three, cols, lanes = clean.shape
    shape = jax.ShapeDtypeStruct(cached_sum.shape, BF)
    frames, coarse, wide, channels = cached_sum.shape
    height = frames * coarse * wide
    return pl.pallas_call(
        first_kernel,
        in_specs=[smem()] + [whole()] * 8,
        out_specs=[whole(), whole()],
        out_shape=[shape, shape],
        scratch_shapes=[
            pltpu.VMEM((height, 5 * lanes), BF),
            pltpu.VMEM((channels // 128, height, 128), F32),
        ],
        compiler_params=params(),
        cost_estimate=pl.CostEstimate(
            flops=2 * height * weight.size, bytes_accessed=4 * cached_sum.size, transcendentals=height * channels
        ),
        name="first",
    )(place, clean, received, own, above, below, weight, gain, cached_sum)


def swapped(array, axis):
    return lax.ppermute(array, axis, [(0, 1), (1, 0)])


def body(
    queries,
    keys,
    values,
    final_gain,
    out_weight,
    noisy_latent,
    step_index,
    span_index,
    cache_flags,
    latent_cache,
    feature_cache,
    first_weight,
    first_gain,
    second_weight,
):
    frames, token_rows, cols, head_size = queries.shape
    channels = first_weight.shape[1]
    width = first_weight.shape[0] // 27
    slab = lax.axis_index("seq")
    slabs = lax.axis_size("seq")
    head = lax.axis_index("head")
    place = jnp.stack([slab, head, jnp.int32(slabs)]).astype(jnp.int32)

    slot = span_index[0] % CSLOTS
    own_latent = lax.dynamic_index_in_dim(latent_cache, slot, 0, keepdims=False)[0]
    rows = own_latent.shape[0]
    flags = lax.dynamic_slice(cache_flags, (slot, head, slab * rows), (1, 1, rows))[0, 0]
    own_latent = own_latent * flags[:, None].astype(BF)
    noisy_tokens = noisy_latent.reshape(frames, 2, cols, 2 * width).transpose(2, 0, 1, 3)
    noisy_tokens = noisy_tokens.reshape(cols, frames * 4 * width)
    old_tokens = own_latent.reshape(2, cols, 2 * width).transpose(1, 0, 2).reshape(cols, 4 * width)
    small = jnp.concatenate([noisy_tokens, old_tokens, old_tokens, jnp.zeros((cols, channels - 16 * width), BF)], 1)

    own_frame, up, down = prepare(span_index, place, cache_flags, feature_cache, small, channels)
    above = lax.ppermute(down, "seq", [(i, i + 1) for i in range(slabs - 1)])
    below = lax.ppermute(up, "seq", [(i + 1, i) for i in range(slabs - 1)])

    sent = attention(queries, keys, values, final_gain, out_weight, slab.reshape(1).astype(jnp.int32))
    parts = lax.all_to_all(sent, "seq", 0, 0, tiled=True)
    cached_sum = cached(place, own_frame, above, below, second_weight)

    clean, send = latent(step_index, place, parts, small, above, below)
    received = swapped(send, "head")
    spare = 64 - 3 * width
    padded = jnp.pad(first_weight.reshape(9, 3 * width, channels), ((0, 1), (0, spare), (0, 0)))
    padded = padded.reshape(640, channels)
    activated, send = first(
        place, clean, received, small, above, below, padded, first_gain.reshape(1, -1), cached_sum
    )
    arrived = swapped(send, "head")
    own_sum = own_part(activated, second_weight)
    decoded = prior_part(place, arrived, cached_sum, own_sum, second_weight)

    tokens = clean[1].reshape(cols, frames, 2, 2 * width).transpose(1, 2, 0, 3)
    return (tokens.reshape(frames, 2, 2 * cols * width), decoded)


def solution(mesh):
    in_specs = (
        P(("grp", "head"), None, None, "seq"),
        P("grp", None, None, "seq"),
        P("grp", None, None, "seq"),
        P(),
        P(),
        P(("grp", "head"), "seq", None),
        P("grp"),
        P("grp"),
        P("grp", None, None),
        P("grp", "head", "seq", None),
        P("grp", "head", "seq", None),
        P(),
        P(),
        P(),
    )
    out_specs = (P(("grp", "head"), "seq", None), P(("grp", "head"), "seq", None))
    return jax.shard_map(body, mesh=mesh, in_specs=in_specs, out_specs=out_specs, check_vma=False)
```

time: 95.9 us -> 74.3 us (0.77)
  Pallas kernels: 0 us -> 36.6 us
  matrix products: 15.1 us -> 0 us
  local copies, waits for them, and re-layouts: 32.8 us -> 18.9 us
  waiting for transfers between devices: 9.01 us -> 0.01 us
  starting transfers between devices: 20.9 us -> 13.6 us
  other arithmetic: 8.65 us -> 2.19 us
  blocking collectives: 5.97 us -> 0 us
    pallas_call x0 -> x7, Pallas kernels: none -> 36.6 us  [the longest x1 8.41 us: prior_part(): pl.pallas_call(prior_kernel, in_specs=[smem(), whole(), whole(), whole(),...]
    dot_general x13 -> x0, matrix products: 15.1 us -> none  [the longest x9 10.5 us: second_conv(): jnp.dot(stacked, weight_block, preferred_element_type=jnp.float32)]
    slice x8 -> x1, local copies, waits for them, and re-layouts: 12.5 us -> 0.7 us  [body(): tokens = clean[1].reshape(cols, frames, 2, 2 * width).transpose(1, 2, 0, 3)]
    unnamed x28 -> x14, local copies, waits for them, and re-layouts: 2.05 us -> 11.8 us
    ppermute x6 -> x4, waiting for transfers between devices: 9.01 us -> 0.01 us  [the longest x2 0.01 us: swapped(): return lax.ppermute(array, axis, [(0, 1), (1, 0)])]
    ppermute x6 -> x4, starting transfers between devices: 15.3 us -> 7.96 us  [the longest x1 3.09 us: body(): below = lax.ppermute(up, 'seq', [(i + 1, i) for i in range(slabs - 1)])]
    reshape x5 -> x6, local copies, waits for them, and re-layouts: 11.2 us -> 4.22 us  [the longest x1 1.28 us: attention(): final_gain.reshape(1, -1)]
    all_gather x2 -> x0, blocking collectives: 5.97 us -> none  [the longest x1 3.36 us: body(): lax.all_gather(own_feature, 'head', axis=0, tiled=True)]
  transfers between devices with their start and end apart: 7 -> 5, of which waited for: 2 -> 0; matrix products, arithmetic and copies ran while one was open for 29% -> 21% of each run, Pallas kernels for 0% -> 24%
where the time goes in v1:
time: 74.3 us; the launch traced here: 73.3 us
  Pallas kernels  36.6 us (49%)
  local copies, waits for them, and re-layouts  18.9 us (25%)
  starting transfers between devices  13.6 us (18%)
  other arithmetic  2.19 us (3%)
  between operations  2.07 us (3%)
    unnamed x14, local copies, waits for them, and re-layouts  11.8 us
    pallas_call x1, Pallas kernels, prior_part(): pl.pallas_call(prior_kernel, in_specs=[smem(), whole(), whole(), whole(),...  8.41 us
    pallas_call x1, Pallas kernels, own_part(): pl.pallas_call(own_kernel, in_specs=[whole(), whole()], out_specs=whole()...  7.7 us
    pallas_call x1, Pallas kernels, cached(): pl.pallas_call(cached_kernel, in_specs=[smem(), whole(), whole(), whole()...  6.65 us
    all_to_all x1, starting transfers between devices, body(): parts = lax.all_to_all(sent, 'seq', 0, 0, tiled=True)  5.61 us
    pallas_call x1, Pallas kernels, attention(): pl.pallas_call(kernel, grid_spec=grid_spec, out_shape=jax.ShapeDtypeStruc...  5.03 us
    pallas_call x1, Pallas kernels, first(): pl.pallas_call(first_kernel, in_specs=[smem()] + [whole()] * 8, out_specs...  3.59 us
    ppermute x1, starting transfers between devices, body(): below = lax.ppermute(up, 'seq', [(i + 1, i) for i in range(slabs - 1)])  3.09 us
  transfers between devices with their start and end apart: 5, of which 0 were waited for; matrix products, arithmetic and copies ran while one was open for 21% of the time, Pallas kernels for 24%

profile of v1, /device:TPU:17, one launch (start us, length us, event | category | flops | bytes accessed | tf_op | source)
XLA Modules:
  0.0 73.3 jit_solution(5828099694423901603)
XLA Ops:
  0.6 0.0 copy-start
  0.7 1.3 %reshape.63.refs_3_ = bf16[1,1024]{1,0:T(2,128)(2,1)} reshape(bf16[1024]{0:T(1024)(128)(2,1)} %param.17) | data formatting | bytes 4096 | tf_op jit(solution)/shard_map/reshape | solution.py:134
  1.9 1.7 %copy.22.refs_4_ = bf16[1024,64]{1,0:T(8,128)(2,1)} copy(bf16[1024,64]{0,1:T(8,128)(2,1)} %param.18) | data formatting | bytes 262144 | tf_op args[4]
  3.7 5.0 %attention.1 = bf16[8,3,48,128]{3,2,1,0:T(8,128)(2,1)} custom-call(s32[1]{0:T(128)} %bitcast.slab_ref, bf16[2,320,128]{2,1,0:T(8,128)(2,1)} %bitcast.34, bf16[1280,128]{1,0:T(8,128)(2,1)} %bitcast.32, bf16[1280,128]{1,0:T(8,128)(2,1)} %bitcast.33, bf16[1,1024]{1,0:T(2,128)(2,1)} %reshape.63.refs_3_, bf16[1024,64]{1,0:T(8,128)(2,1)} %copy.22.refs_4_), custom_call_target="tpu_custom_call" | custom-call | flops 629145600 | bytes 819200 | tf_op jit(solution)/shard_map/attention/pallas_call | solution.py:123
  8.7 5.6 %all-to-all-start = ((bf16[8,3,48,128]{3,2,1,0:T(8,128)(2,1)}), bf16[8,3,48,128]{3,2,1,0:T(8,128)(2,1)S(1)}, u32[]{:S(2)}, u32[]{:S(2)}) async-start(bf16[8,3,48,128]{3,2,1,0:T(8,128)(2,1)} %attention.1), calls=%async_computation | async-start | bytes 589824 | tf_op jit(solution)/shard_map/all_to_all | solution.py:635
  15.0 0.0 copy-done
  15.0 0.1 squeeze.9
  15.1 0.8 %convert_bitcast_fusion = bf16[2]{0:T(256)(128)(2,1)S(1)} fusion(s32[2,2,16]{2,1,0:T(2,128)} %flags_ref.1, s32[]{:T(128)S(6)} %select_n.19, s32[]{:T(128)S(6)} %select_n.20, s32[]{:T(128)S(6)} %select_n.21), kind=kLoop, calls=%fused_computation.3 | loop fusion | flops 2 | bytes 24 | tf_op jit(solution)/shard_map/convert_element_type | solution.py:624
  15.9 0.1 multiply_bitcast_fusion
  15.9 0.1 copy.24
  16.0 0.1 copy.25
  16.1 0.8 %reshape.64 = bf16[2,2,40,32]{3,2,1,0:T(8,128)(2,1)S(1)} reshape(bf16[2,2,1280]{2,1,0:T(2,128)(2,1)} %param.19) | data formatting | bytes 20480 | tf_op jit(solution)/shard_map/reshape | solution.py:625
  17.0 0.1 reshape.65
  17.1 0.7 pad_add_fusion.place_ref
  17.8 0.7 maximum_maximum_fusion.small_ref.own_ref
  18.5 3.0 %prepare.1 = (bf16[4,2,80,384]{3,2,1,0:T(8,128)(2,1)}, bf16[200,384]{1,0:T(8,128)(2,1)}, bf16[200,384]{1,0:T(8,128)(2,1)}) custom-call(s32[1]{0:T(128)} %copy.32.span_ref, s32[3]{0:T(128)} %pad_add_fusion.place_ref, s32[2,2,16]{2,1,0:T(2,128)} %flags_ref.1, bf16[2,480,4,128]{3,2,1,0:T(4,128)(2,1)} %bitcast.27, ...), custom_call_target="tpu_custom_call" | custom-call | flops 245760 | bytes 1474560 | tf_op jit(solution)/shard_map/prepare/pallas_call | solution.py:190
  21.4 3.1 %collective-permute-start = (bf16[200,384]{1,0:T(8,128)(2,1)}, bf16[200,384]{1,0:T(8,128)(2,1)S(1)}, u32[]{:S(2)}, u32[]{:S(2)}) collective-permute-start(bf16[200,384]{1,0:T(8,128)(2,1)} %get-tuple-element.9), channel_id=1, source_target_pairs={{0,2},{2,4},{4,6},{6,8},{8,10},{10,12},{12,14},{1,3},{3,5},{5,7},{... | collective-permute-start | bytes 460808 | tf_op jit(solution)/shard_map/ppermute | solution.py:631
  24.5 3.1 %collective-permute-start.1 = (bf16[200,384]{1,0:T(8,128)(2,1)}, bf16[200,384]{1,0:T(8,128)(2,1)S(1)}, u32[]{:S(2)}, u32[]{:S(2)}) collective-permute-start(bf16[200,384]{1,0:T(8,128)(2,1)} %get-tuple-element.10), channel_id=1, source_target_pairs={{2,0},{4,2},{6,4},{8,6},{10,8},{12,10},{14,12},{3,1},{5,3},{7,5},{... | collective-permute-start | bytes 460808 | tf_op jit(solution)/shard_map/ppermute | solution.py:632
  28.3 1.2 %reshape.71.gain_ref = bf16[1,384]{1,0:T(2,128)(2,1)} reshape(bf16[384]{0:T(512)(128)(2,1)} %param.26) | data formatting | bytes 1536 | tf_op jit(solution)/shard_map/reshape | solution.py:644
  29.5 1.8 %pad.4 = bf16[10,64,384]{2,1,0:T(8,128)(2,1)} pad(bf16[9,48,384]{2,1,0:T(8,128)(2,1)} %bitcast.28, bf16[]{:T(256)} %constant.32.clone.1), padding=0_1x0_16x0_0 | pad | bytes 823298 | tf_op jit(solution)/shard_map/jit(_pad)/pad | solution.py:641
  31.3 7.2 %copy.28.weight_ref = bf16[10368,192]{1,0:T(8,128)(2,1)} copy(bf16[10368,192]{0,1:T(8,128)(2,1)} %param.27) | data formatting | bytes 7962624 | tf_op args[13]
  38.6 0.0 collective-permute-done.above_ref
  38.6 0.0 copy-start.1
  38.6 0.0 collective-permute-done.1.below_ref
  38.6 0.0 copy-start.2
  38.6 0.0 all-to-all-done.parts_ref
  38.6 0.6 copy-done.1
  39.2 0.1 copy-done.2
  39.3 0.0 copy-start.3
  39.3 0.7 copy-done.3
  40.0 2.3 %latent.1 = (bf16[3,40,128]{2,1,0:T(8,128)(2,1)}, bf16[3,40,128]{2,1,0:T(8,128)(2,1)}) custom-call(s32[1]{0:T(128)S(6)} %copy.31.step_ref, s32[3]{0:T(128)} %pad_add_fusion.place_ref, bf16[8,3,48,128]{3,2,1,0:T(8,128)(2,1)} %copy-done.3, bf16[40,384]{1,0:T(8,128)(2,1)} %maximum_maximum_fusion.small_ref.own_ref, bf16[200,384]{1,0:T(8,128)(2,1)} %copy-done.1, ...), custom_call_target="tpu_custom_call" | custom-call | flops 294912 | bytes 294912 | tf_op jit(solution)/shard_map/latent/pallas_call | solution.py:445
  42.3 1.8 %collective-permute-start.2 = (bf16[3,40,128]{2,1,0:T(8,128)(2,1)}, bf16[3,40,128]{2,1,0:T(8,128)(2,1)S(1)}, u32[]{:S(2)}, u32[]{:S(2)}) collective-permute-start(bf16[3,40,128]{2,1,0:T(8,128)(2,1)} %get-tuple-element.12), channel_id=1, source_target_pairs={{0,1},{1,0},{2,3},{3,2},{4,5},{5,4},{6,7},{7,6},{8,9},{9,8},{10,11... | collective-permute-start | bytes 92168 | tf_op jit(solution)/shard_map/ppermute | solution.py:593
  44.1 6.6 %cached.1.cached_ref = bf16[2,4,80,384]{3,2,1,0:T(8,128)(2,1)} custom-call(s32[3]{0:T(128)} %pad_add_fusion.place_ref, bf16[4,2,80,384]{3,2,1,0:T(8,128)(2,1)} %get-tuple-element.13.own_ref, bf16[200,384]{1,0:T(8,128)(2,1)} %copy-done.1, bf16[200,384]{1,0:T(8,128)(2,1)} %copy-done.2, bf16[10368,192]{1,0:T(8,128)(2,1)} %copy.28.weight_ref), custom_call_target="tpu_custom_call" | custom-call | flops 1698693120 | bytes 4472832 | tf_op jit(solution)/shard_map/cached/pallas_call | solution.py:266
  50.7 0.0 collective-permute-done.2.received_ref
  50.7 0.0 copy-start.4
  50.7 0.6 copy-done.4
  51.3 3.6 %first.1 = (bf16[2,4,80,384]{3,2,1,0:T(8,128)(2,1)}, bf16[2,4,80,384]{3,2,1,0:T(8,128)(2,1)}) custom-call(s32[3]{0:T(128)} %pad_add_fusion.place_ref, bf16[3,40,128]{2,1,0:T(8,128)(2,1)} %get-tuple-element.11.clean_ref, bf16[3,40,128]{2,1,0:T(8,128)(2,1)} %copy-done.4, bf16[40,384]{1,0:T(8,128)(2,1)} %maximum_maximum_fusion.small_ref.own_ref, ...), custom_call_target="tpu_custom_call" | custom-call | flops 314572800 | bytes 983040 | tf_op jit(solution)/shard_map/first/pallas_call | solution.py:575
  54.9 0.0 collective-permute-start.3
  54.9 0.7 slice.3
  55.6 0.1 reshape_squeeze.3
  55.7 0.7 reshape.68
  56.4 7.7 %own_part.1.own_ref = f32[2,4,80,384]{3,2,1,0:T(8,128)} custom-call(bf16[2,4,80,384]{3,2,1,0:T(8,128)(2,1)} %get-tuple-element.15.source_ref, bf16[10368,192]{1,0:T(8,128)(2,1)} %copy.28.weight_ref), custom_call_target="tpu_custom_call" | custom-call | flops 2548039680 | bytes 4472832 | tf_op jit(solution)/shard_map/own_part/pallas_call | solution.py:329
  64.1 0.0 collective-permute-done.3.source_ref
  64.2 0.0 copy-start.5
  64.2 0.8 %copy-done.5 = bf16[2,4,80,384]{3,2,1,0:T(8,128)(2,1)} copy-done((bf16[2,4,80,384]{3,2,1,0:T(8,128)(2,1)}, bf16[2,4,80,384]{3,2,1,0:T(8,128)(2,1)S(1)}, u32[]{:S(2)}) %copy-start.5) | copy-done | bytes 491544
  64.9 8.4 %prior_part.1 = bf16[2,240,4,128]{3,2,1,0:T(4,128)(2,1)} custom-call(s32[3]{0:T(128)} %pad_add_fusion.place_ref, bf16[2,4,80,384]{3,2,1,0:T(8,128)(2,1)} %copy-done.5, bf16[2,4,80,384]{3,2,1,0:T(8,128)(2,1)} %cached.1.cached_ref, f32[2,4,80,384]{3,2,1,0:T(8,128)} %own_part.1.own_ref, bf16[10368,192]{1,0:T(8,128)(2,1)} %copy.28.weight_ref), custom_call_target="tpu_custom_call" | custom-call | flops 2548039680 | bytes 4472832 | tf_op jit(solution)/shard_map/prior_part/pallas_call | solution.py:390
  (5 shorter events, 0.1 us)
Async XLA Ops:
  0.6 14.4 %copy-start = (bf16[2,1,2,1280]{3,2,1,0:T(2,128)(2,1)S(1)}, bf16[2,1,2,1280]{3,2,1,0:T(2,128)(2,1)}, u32[]{:S(2)}) copy-start(bf16[2,1,2,1280]{3,2,1,0:T(2,128)(2,1)} %param.23) | copy-start | bytes 30724
  8.7 29.9 %all-to-all-start = ((bf16[8,3,48,128]{3,2,1,0:T(8,128)(2,1)}), bf16[8,3,48,128]{3,2,1,0:T(8,128)(2,1)S(1)}, u32[]{:S(2)}, u32[]{:S(2)}) async-start(bf16[8,3,48,128]{3,2,1,0:T(8,128)(2,1)} %attention.1), calls=%async_computation | async-start | bytes 589824 | tf_op jit(solution)/shard_map/all_to_all | solution.py:635
  21.4 17.2 %collective-permute-start = (bf16[200,384]{1,0:T(8,128)(2,1)}, bf16[200,384]{1,0:T(8,128)(2,1)S(1)}, u32[]{:S(2)}, u32[]{:S(2)}) collective-permute-start(bf16[200,384]{1,0:T(8,128)(2,1)} %get-tuple-element.9), channel_id=1, source_target_pairs={{0,2},{2,4},{4,6},{6,8},{8,10},{10,12},{12,14},{1,3},{3,5},{5,7},{... | collective-permute-start | bytes 460808 | tf_op jit(solution)/shard_map/ppermute | solution.py:631
  24.5 14.1 %collective-permute-start.1 = (bf16[200,384]{1,0:T(8,128)(2,1)}, bf16[200,384]{1,0:T(8,128)(2,1)S(1)}, u32[]{:S(2)}, u32[]{:S(2)}) collective-permute-start(bf16[200,384]{1,0:T(8,128)(2,1)} %get-tuple-element.10), channel_id=1, source_target_pairs={{2,0},{4,2},{6,4},{8,6},{10,8},{12,10},{14,12},{3,1},{5,3},{7,5},{... | collective-permute-start | bytes 460808 | tf_op jit(solution)/shard_map/ppermute | solution.py:632
  38.6 0.7 copy-start.1
  38.6 0.7 copy-start.2
  39.3 0.7 copy-start.3
  42.3 8.4 %collective-permute-start.2 = (bf16[3,40,128]{2,1,0:T(8,128)(2,1)}, bf16[3,40,128]{2,1,0:T(8,128)(2,1)S(1)}, u32[]{:S(2)}, u32[]{:S(2)}) collective-permute-start(bf16[3,40,128]{2,1,0:T(8,128)(2,1)} %get-tuple-element.12), channel_id=1, source_target_pairs={{0,1},{1,0},{2,3},{3,2},{4,5},{5,4},{6,7},{7,6},{8,9},{9,8},{10,11... | collective-permute-start | bytes 92168 | tf_op jit(solution)/shard_map/ppermute | solution.py:593
  50.7 0.6 copy-start.4
  54.9 9.2 %collective-permute-start.3 = (bf16[2,4,80,384]{3,2,1,0:T(8,128)(2,1)}, bf16[2,4,80,384]{3,2,1,0:T(8,128)(2,1)S(1)}, u32[]{:S(2)}, u32[]{:S(2)}) collective-permute-start(bf16[2,4,80,384]{3,2,1,0:T(8,128)(2,1)} %get-tuple-element.14), channel_id=1, source_target_pairs={{0,1},{1,0},{2,3},{3,2},{4,5},{5,4},{6,7},{7,6},{8,9},{9,8},{10,11... | collective-permute-start | bytes 1474568 | tf_op jit(solution)/shard_map/ppermute | solution.py:593
  64.2 0.8 %copy-start.5 = (bf16[2,4,80,384]{3,2,1,0:T(8,128)(2,1)}, bf16[2,4,80,384]{3,2,1,0:T(8,128)(2,1)S(1)}, u32[]{:S(2)}) copy-start(bf16[2,4,80,384]{3,2,1,0:T(8,128)(2,1)S(1)} %collective-permute-done.3.source_ref) | copy-start | bytes 1474564

commit v2 on v1

v2 whole, which is shorter than its diff:
```python
import jax
import jax.numpy as jnp
from jax import lax
from jax.experimental import pallas as pl
from jax.experimental.pallas import tpu as pltpu
from jax.sharding import PartitionSpec as P

NSTEPS = 16
CSLOTS = 2
SHIFT_FACTOR = 5.0
NORM_EPSILON = 1e-06
BF = jnp.bfloat16
F32 = jnp.float32
LAST = (((1,), (1,)), ((), ()))


def params(dims=0, mib=20):
    semantics = ("arbitrary",) * dims if dims else None
    return pltpu.CompilerParams(dimension_semantics=semantics, vmem_limit_bytes=mib << 20)


def dot(left, right):
    return jnp.dot(left, right, preferred_element_type=F32)


def dot_last(left, right):
    return lax.dot_general(left, right, LAST, preferred_element_type=F32)


def whole():
    return pl.BlockSpec(memory_space=pltpu.VMEM)


def smem():
    return pl.BlockSpec(memory_space=pltpu.SMEM)


def attention_kernel(q_ref, k_ref, v_ref, gain_ref, weight_ref, out_ref, *, cols, rows_total):
    frames, block, head_size = q_ref.shape
    rows = block // cols
    step = pl.program_id(0)
    slab = lax.axis_index("seq")
    scale = 1.4426950408889634 / head_size**0.5
    keys = k_ref[...]
    values = jnp.concatenate([v_ref[...], jnp.ones_like(v_ref[...])], axis=1)
    gains = gain_ref[...].astype(F32)
    chosen = lax.broadcasted_iota(jnp.int32, gains.shape, 0) == slab
    gain = jnp.sum(jnp.where(chosen, gains, 0.0), axis=0, keepdims=True)
    start = pl.multiple_of(slab * head_size, head_size)
    weight = weight_ref[:, pl.ds(start, head_size)]
    none = jnp.zeros_like(weight)
    line_of = lax.broadcasted_iota(jnp.int32, (8, head_size), 0)
    total = None
    squares = []
    for f in range(frames):
        scores = dot_last(q_ref[f], keys)
        row_max = jnp.max(scores, axis=1, keepdims=True)
        weights = jnp.exp2((scores - row_max) * scale).astype(BF)
        blended = dot(weights, values)
        attended = (blended[:, :head_size] / blended[:, head_size:]).astype(BF).astype(F32)
        side = [none] * frames
        side[f] = weight
        part = dot_last((attended * gain).astype(BF), jnp.concatenate(side, axis=0))
        total = part if total is None else total + part
        squares.append(attended * attended)

    @pl.when(step == 0)
    def _():
        out_ref[0, 0] = jnp.zeros(out_ref.shape[2:], BF)
        out_ref[rows_total - 1, 2] = jnp.zeros(out_ref.shape[2:], BF)

    for r in range(rows):
        sums = None
        for f in range(frames):
            piece = squares[f][r * cols : (r + 1) * cols].astype(BF)
            line = dot_last((line_of == f).astype(F32).astype(BF), piece)
            sums = line if sums is None else sums + line
        lanes = total.shape[1]
        sums = jnp.concatenate([sums, jnp.zeros((8, lanes - cols), F32)], axis=1)
        unit = jnp.concatenate([total[r * cols : (r + 1) * cols], sums], axis=0).astype(BF)
        row = step * rows + r
        out_ref[row, 1] = unit

        @pl.when(row + 1 < rows_total)
        def _():
            out_ref[jnp.minimum(row + 1, rows_total - 1), 0] = unit

        @pl.when(row > 0)
        def _():
            out_ref[jnp.maximum(row - 1, 0), 2] = unit


def attention(queries, keys, values, final_gain, out_weight):
    frames, rows_total, cols, head_size = queries.shape
    q = queries.reshape(frames, rows_total * cols, head_size)
    k = keys.reshape(-1, head_size)
    v = values.reshape(-1, head_size)
    gains = final_gain.reshape(-1, head_size)
    weight = out_weight.T
    rows = 4 if rows_total % 4 == 0 else rows_total
    lanes = frames * weight.shape[0]
    unit = cols + 8

    def kernel(*refs):
        attention_kernel(*refs, cols=cols, rows_total=rows_total)

    count = frames * rows_total * cols
    return pl.pallas_call(
        kernel,
        grid=(rows_total // rows,),
        in_specs=[
            pl.BlockSpec((frames, rows * cols, head_size), lambda i: (0, i, 0)),
            pl.BlockSpec(k.shape, lambda i: (0, 0)),
            pl.BlockSpec(v.shape, lambda i: (0, 0)),
            pl.BlockSpec(gains.shape, lambda i: (0, 0)),
            pl.BlockSpec(weight.shape, lambda i: (0, 0)),
        ],
        out_specs=pl.BlockSpec((rows_total, 3, unit, lanes), lambda i: (0, 0, 0, 0)),
        out_shape=jax.ShapeDtypeStruct((rows_total, 3, unit, lanes), BF),
        compiler_params=params(1, 40),
        cost_estimate=pl.CostEstimate(
            flops=6 * count * k.shape[0] * head_size,
            bytes_accessed=2 * (q.size + k.size + v.size),
            transcendentals=count * k.shape[0],
        ),
        name="attention",
    )(q, k, v, gains, weight)


def lane_groups(array, group):
    return lax.broadcasted_iota(jnp.int32, array.shape, 1) // group


def moved(array, shift):
    lanes = array.shape[1]
    shift = shift % lanes
    return pltpu.roll(array, shift, axis=1) if shift else array


def prepare_kernel(
    span_ref, flags_ref, cache_ref, noisy_ref, latent_ref, own_ref, up_ref, down_ref, small_ref, scr, lat
):
    tiles, rows, lanes = cache_ref.shape[1:]
    cols, channels = own_ref.shape[2:]
    pieces = channels // lanes
    slot = lax.rem(span_ref[0], CSLOTS)
    slab = lax.axis_index("seq")
    head = lax.axis_index("head")
    coarse = rows // 2
    flags = [flags_ref[slot, head, slab * coarse + r].astype(F32) for r in range(coarse)]

    frames, chunks, halves = noisy_ref.shape[:3]
    groups = frames * halves
    group = lanes // groups
    for f in range(frames + 1):
        for i in range(chunks):
            tile = latent_ref[0, i] if f == frames else noisy_ref[f, i]
            lat[pl.ds((f * chunks + i) * halves, halves), :] = tile.astype(F32)
    lines = [
        [lat[pl.ds(f * chunks * halves + a, chunks, stride=halves), :] for a in range(halves)]
        for f in range(frames + 1)
    ]
    noisy = [lines[f][a] for f in range(frames) for a in range(halves)]
    old = [lines[frames][a] * flags[a] for f in range(frames) for a in range(halves)]
    base = (frames + 1) * chunks * halves
    tokens = chunks * groups
    for n, parts in enumerate((noisy, old)):
        at = base + n * tokens
        for m in range(groups):
            total = None
            for g, part in enumerate(parts):
                term = jnp.where(lane_groups(part, group) == g, moved(part, group * (g - m)), 0.0)
                total = term if total is None else total + term
            lat[pl.ds(at + m, chunks, stride=groups), :] = total
        block = lat[at : at + tokens, :].astype(BF)
        small_ref[:, n * lanes : (n + 1) * lanes] = block
        up_ref[2 * cols :, n * lanes : (n + 1) * lanes] = block
        down_ref[2 * cols :, n * lanes : (n + 1) * lanes] = block
    rest = jnp.zeros((tokens, channels - 2 * lanes), BF)
    up_ref[2 * cols :, 2 * lanes :] = rest
    down_ref[2 * cols :, 2 * lanes :] = rest

    def unpack(i, carry):
        for n in range(16):
            at = i * 16 + n
            scr[pl.ds(pl.multiple_of(at * rows, rows), rows), :] = cache_ref[0, at].astype(F32)
        return carry

    lax.fori_loop(0, tiles // 16, unpack, 0)
    for r in range(rows):
        for b in range(2):
            for q in range(pieces):
                start = (b * pieces + q) * rows + r
                piece = scr[pl.ds(start, cols, stride=2 * pieces * rows), :]
                piece = (piece * flags[r // 2]).astype(BF)
                own_ref[r, b, :, q * lanes : (q + 1) * lanes] = piece
                if r == 0:
                    up_ref[b * cols : (b + 1) * cols, q * lanes : (q + 1) * lanes] = piece
                if r == rows - 1:
                    down_ref[b * cols : (b + 1) * cols, q * lanes : (q + 1) * lanes] = piece


def tiled(array):
    *lead, rows, width = array.shape
    count = len(lead)
    view = array.reshape(*lead, rows, width // 128, 128)
    return view.transpose(*range(count), count + 1, count, count + 2)


def prepare(span_index, cache_flags, feature_cache, noisy_latent, latent_cache, channels):
    slots, _, rows, width = feature_cache.shape
    tiles = width // 128
    cols = width // channels // 2
    noisy = tiled(noisy_latent)
    frames, chunks, halves = noisy.shape[:3]
    tokens = chunks * frames * halves
    halo = 2 * cols + tokens
    grid_spec = pltpu.PrefetchScalarGridSpec(
        num_scalar_prefetch=2,
        grid=(1,),
        in_specs=[
            pl.BlockSpec((1, tiles, rows, 128), lambda i, s, f: (lax.rem(s[0], CSLOTS), 0, 0, 0)),
            pl.BlockSpec(noisy.shape, lambda i, s, f: (0, 0, 0, 0)),
            pl.BlockSpec((1, chunks, halves, 128), lambda i, s, f: (lax.rem(s[0], CSLOTS), 0, 0, 0)),
        ],
        out_specs=[
            pl.BlockSpec((rows, 2, cols, channels), lambda i, s, f: (0, 0, 0, 0)),
            pl.BlockSpec((halo, channels), lambda i, s, f: (0, 0)),
            pl.BlockSpec((halo, channels), lambda i, s, f: (0, 0)),
            pl.BlockSpec((tokens, 256), lambda i, s, f: (0, 0)),
        ],
        scratch_shapes=[
            pltpu.VMEM((tiles * rows, 128), F32),
            pltpu.VMEM(((frames + 1) * chunks * halves + 2 * tokens, 128), F32),
        ],
    )
    return pl.pallas_call(
        prepare_kernel,
        grid_spec=grid_spec,
        out_shape=[
            jax.ShapeDtypeStruct((rows, 2, cols, channels), BF),
            jax.ShapeDtypeStruct((halo, channels), BF),
            jax.ShapeDtypeStruct((halo, channels), BF),
            jax.ShapeDtypeStruct((tokens, 256), BF),
        ],
        compiler_params=params(1),
        cost_estimate=pl.CostEstimate(
            flops=rows * width, bytes_accessed=6 * rows * width, transcendentals=0
        ),
        name="prepare",
    )(span_index, cache_flags, tiled(feature_cache[:, 0]), noisy, tiled(latent_cache[:, 0]))


def shift_down(array):
    moved_rows = pltpu.roll(array, 1, axis=0)
    rows = lax.broadcasted_iota(jnp.int32, array.shape, 0)
    return jnp.where(rows == 0, 0.0, moved_rows)


def shift_up(array):
    count = array.shape[0]
    moved_rows = pltpu.roll(array, count - 1, axis=0)
    rows = lax.broadcasted_iota(jnp.int32, array.shape, 0)
    return jnp.where(rows == count - 1, 0.0, moved_rows)


def cached_kernel(own_ref, above_ref, below_ref, weight_ref, out_ref, var):
    rows, _, cols, channels = own_ref.shape
    for r in range(rows + 2):
        if r == 0:
            even, odd = above_ref[:cols], above_ref[cols : 2 * cols]
        elif r == rows + 1:
            even, odd = below_ref[:cols], below_ref[cols : 2 * cols]
        else:
            even, odd = own_ref[r - 1, 0], own_ref[r - 1, 1]
        var[0, r] = shift_down(odd.astype(F32)).astype(BF)
        var[1, r] = even
        var[2, r] = odd
        var[3, r] = shift_up(even.astype(F32)).astype(BF)

    def contribute(f, base):
        for r in range(0, rows, 2):
            sides = []
            for b in range(2):
                total = None
                for h in range(3):
                    left = jnp.concatenate(
                        [
                            var[b + w, r + h : r + h + 2].reshape(2 * cols, channels)
                            for w in range(3)
                        ],
                        axis=1,
                    )
                    start = pl.multiple_of(base + h * 3 * channels, 128)
                    part = dot_last(left, weight_ref[:, pl.ds(start, 3 * channels)])
                    total = part if total is None else total + part
                sides.append(total)
            both = jnp.concatenate(sides, axis=1).astype(BF)
            out_ref[f, r : r + 2] = both.reshape(2, cols, both.shape[1])

    head = lax.axis_index("head")
    contribute(0, head * (9 * channels))

    @pl.when(head == 0)
    def _():
        out_ref[1] = jnp.zeros(out_ref.shape[1:], BF)

    @pl.when(head != 0)
    def _():
        contribute(1, 0)


def cached(own, above, below, weight):
    rows, _, cols, channels = own.shape
    return pl.pallas_call(
        cached_kernel,
        in_specs=[whole()] * 4,
        out_specs=whole(),
        out_shape=jax.ShapeDtypeStruct((2, rows, cols, 2 * weight.shape[0]), BF),
        scratch_shapes=[pltpu.VMEM((4, rows + 2, cols, channels), BF)],
        compiler_params=params(),
        cost_estimate=pl.CostEstimate(
            flops=2 * 2 * rows * 2 * cols * 9 * channels * weight.shape[0],
            bytes_accessed=2 * (own.size + weight.size),
            transcendentals=0,
        ),
        name="cached",
    )(own, above, below, weight)


def mix_kernel(weight_ref, out_ref):
    channels = weight_ref.shape[1] // 9

    def tap(h, w):
        start = (h * 3 + w) * channels
        return weight_ref[:, start : start + channels].astype(F32)

    lines = {}
    for w in range(3):
        top, middle, bottom = tap(0, w), tap(1, w), tap(2, w)
        lines[0, 0, w] = top
        lines[0, 1, w] = middle + bottom
        lines[1, 0, w] = top + middle
        lines[1, 1, w] = bottom
    for a in range(2):
        for u in range(2):
            left, centre, right = [lines[a, u, w] for w in range(3)]
            mixed = ((left, centre + right), (left + centre, right))
            for b in range(2):
                for v in range(2):
                    start = (u * 2 + v) * channels
                    out_ref[0, a * 2 + b, :, start : start + channels] = mixed[b][v].astype(BF)


def mix(weight):
    out, height = weight.shape
    third = height // 3
    shape = (3, 4, out, third // 9 * 4)
    return pl.pallas_call(
        mix_kernel,
        grid=(3,),
        in_specs=[pl.BlockSpec((out, third), lambda t: (0, t))],
        out_specs=pl.BlockSpec((1,) + shape[1:], lambda t: (t, 0, 0, 0)),
        out_shape=jax.ShapeDtypeStruct(shape, BF),
        compiler_params=params(1),
        cost_estimate=pl.CostEstimate(
            flops=4 * weight.size, bytes_accessed=6 * weight.size, transcendentals=0
        ),
        name="mix",
    )(weight)


def spread(source_ref, var):
    frames, coarse = source_ref.shape[:2]
    for f in range(frames):
        for r in range(coarse):
            plain = source_ref[f, r]
            wide = plain.astype(F32)
            var[0, f, r] = shift_down(wide).astype(BF)
            var[1, f, r] = plain
            var[2, f, r] = shift_up(wide).astype(BF)


def taps(var, frames, a, b):
    coarse = var.shape[2]
    lines = []
    for frame in frames:
        for r in range(coarse - 2):
            lines.append(
                jnp.concatenate(
                    [var[b + v, frame, r + a + u] for u in range(2) for v in range(2)], axis=1
                )
            )
    return jnp.concatenate(lines, axis=0)


def own_kernel(source_ref, old_ref, new_ref, out_ref, var):
    step = pl.program_id(0)
    a = step // 2
    b = step % 2

    @pl.when(step == 0)
    def _():
        spread(source_ref, var)

    both = dot_last(taps(var, (0, 1), a, b), new_ref[0, 0])
    more = dot_last(taps(var, (0,), a, b), old_ref[0, 0])
    height = more.shape[0]
    shape = out_ref.shape[2:]
    out_ref[0, 0] = both[:height].reshape(shape)
    out_ref[0, 1] = (both[height:] + more).reshape(shape)


def own_part(activated, mixed):
    frames, coarse, cols, channels = activated.shape
    _, parities, width, depth = mixed.shape
    block = (1, 1, width, depth)
    shape = (parities, frames, coarse - 2, cols, width)
    return pl.pallas_call(
        own_kernel,
        grid=(parities,),
        in_specs=[
            pl.BlockSpec(activated.shape, lambda i: (0, 0, 0, 0)),
            pl.BlockSpec(block, lambda i: (1, i, 0, 0)),
            pl.BlockSpec(block, lambda i: (2, i, 0, 0)),
        ],
        out_specs=pl.BlockSpec((1,) + shape[1:], lambda i: (i, 0, 0, 0, 0)),
        out_shape=jax.ShapeDtypeStruct(shape, F32),
        scratch_shapes=[pltpu.VMEM((3, frames, coarse, cols, channels), BF)],
        compiler_params=params(1),
        cost_estimate=pl.CostEstimate(
            flops=2 * 3 * 2 * cols * depth * width * parities,
            bytes_accessed=2 * (activated.size + 2 * parities * width * depth),
            transcendentals=0,
        ),
        name="own_part",
    )(activated, mixed, mixed)


def prior_kernel(source_ref, cached_ref, own_ref, old_ref, new_ref, out_ref, var, total_ref, scr):
    parities, frames, coarse_rows, cols, width = total_ref.shape
    head = lax.axis_index("head")
    step = pl.program_id(0)
    a = step // 2
    b = step % 2

    @pl.when(head == 0)
    def _():
        total_ref[step] = own_ref[0]

    @pl.when(head != 0)
    def _():
        @pl.when(step == 0)
        def _():
            spread(source_ref, var)

        both = dot_last(taps(var, (0, 1), a, b), old_ref[0, 0])
        more = dot_last(taps(var, (1,), a, b), new_ref[0, 0])
        height = more.shape[0]
        shape = total_ref.shape[2:]
        total_ref[step, 0] = own_ref[0, 0] + (both[:height] + more).reshape(shape)
        total_ref[step, 1] = own_ref[0, 1] + both[height:].reshape(shape)

    @pl.when(step == parities - 1)
    def _():
        fine = 2 * coarse_rows
        pieces = 2 * width // 128
        keep = jnp.where(head == 0, 1.0, 0.0)
        for f in range(frames):
            for row in range(fine):
                side = (row % 2) * 2
                sides = [total_ref[side + n, f, row // 2] for n in range(2)]
                line = jnp.concatenate(sides, axis=1)
                extra = cached_ref[f, row].astype(F32) + source_ref[f, row].astype(F32)
                line = line + keep * extra
                for q in range(pieces):
                    scr[pl.ds(q * fine + row, cols, stride=pieces * fine), :] = line[
                        :, q * 128 : (q + 1) * 128
                    ]

            def pack(i, carry):
                for n in range(16):
                    at = i * 16 + n
                    tile = scr[pl.ds(pl.multiple_of(at * fine, fine), fine), :]
                    out_ref[f, at] = tile.astype(BF)
                return carry

            lax.fori_loop(0, out_ref.shape[1] // 16, pack, 0)


def prior_part(received, cached_sum, own_sum, mixed):
    frames, coarse, cols, channels = received.shape
    _, parities, width, depth = mixed.shape
    fine = 2 * (coarse - 2)
    tiles = cols * 2 * width // 128
    block = (1, 1, width, depth)
    out = pl.pallas_call(
        prior_kernel,
        grid=(parities,),
        in_specs=[
            pl.BlockSpec(received.shape, lambda i: (0, 0, 0, 0)),
            pl.BlockSpec(cached_sum.shape, lambda i: (0, 0, 0, 0)),
            pl.BlockSpec((1,) + own_sum.shape[1:], lambda i: (i, 0, 0, 0, 0)),
            pl.BlockSpec(block, lambda i: (0, i, 0, 0)),
            pl.BlockSpec(block, lambda i: (1, i, 0, 0)),
        ],
        out_specs=pl.BlockSpec((frames, tiles, fine, 128), lambda i: (0, 0, 0, 0)),
        out_shape=jax.ShapeDtypeStruct((frames, tiles, fine, 128), BF),
        scratch_shapes=[
            pltpu.VMEM((3, frames, coarse, cols, channels), BF),
            pltpu.VMEM(own_sum.shape, F32),
            pltpu.VMEM((tiles * fine, 128), F32),
        ],
        compiler_params=params(1),
        cost_estimate=pl.CostEstimate(
            flops=2 * 3 * 2 * cols * depth * width * parities,
            bytes_accessed=2 * (received.size + 2 * parities * width * depth),
            transcendentals=0,
        ),
        name="prior_part",
    )(received, cached_sum, own_sum, mixed, mixed)
    return out.transpose(0, 2, 1, 3).reshape(frames, fine, tiles * 128)


def latent_kernel(step_ref, parts_ref, own_ref, above_ref, below_ref, clean_ref, send_ref, out_ref, scr):
    sources, three, unit, lanes = parts_ref.shape
    cols = own_ref.shape[0]
    frames, chunks, halves = out_ref.shape[:3]
    groups = frames * halves
    group = lanes // groups
    features = sources * 128
    fraction = 1.0 - step_ref[0].astype(F32) / NSTEPS
    fraction = jnp.full((1, lanes), fraction, F32)
    level = SHIFT_FACTOR * fraction / (1.0 + (SHIFT_FACTOR - 1.0) * fraction)
    total = parts_ref[0].astype(F32)
    for source in range(1, sources):
        total = total + parts_ref[source].astype(F32)
    half = lax.broadcasted_iota(jnp.int32, (cols, lanes), 1) < lanes // 2
    first_group = lax.axis_index("head") == 0
    for k, small_ref in ((0, above_ref), (1, own_ref), (2, below_ref)):
        small = small_ref[...] if k == 1 else small_ref[small_ref.shape[0] - cols :]
        sums = jnp.transpose(total[k, cols:unit])[:cols]
        scale = lax.rsqrt(sums / features + NORM_EPSILON)
        scale = jnp.where(half, scale[:, 0:1], scale[:, 1:2])
        velocity = total[k, :cols] * scale
        clean = (small[:, :lanes].astype(F32) - level * velocity).astype(BF)
        clean_ref[k] = clean
        if k == 1:
            scr[:cols, :] = clean.astype(F32)

        @pl.when(first_group)
        def _():
            send_ref[k] = clean

        @pl.when(jnp.logical_not(first_group))
        def _():
            send_ref[k] = small[:, lanes : 2 * lanes]

    parts = [scr[pl.ds(m, chunks, stride=groups), :] for m in range(groups)]
    for g in range(groups):
        total_line = None
        for m, part in enumerate(parts):
            term = jnp.where(lane_groups(part, group) == m, moved(part, group * (m - g)), 0.0)
            total_line = term if total_line is None else total_line + term
        f, a = g // halves, g % halves
        scr[pl.ds(cols + f * chunks * halves + a, chunks, stride=halves), :] = total_line
    for f in range(frames):
        for i in range(chunks):
            at = cols + (f * chunks + i) * halves
            out_ref[f, i] = scr[at : at + halves, :].astype(BF)


def latent(step_index, parts, own, above, below, frames, halves, chunks):
    sources, three, unit, lanes = parts.shape
    cols = own.shape[0]
    shape = jax.ShapeDtypeStruct((three, cols, lanes), BF)
    return pl.pallas_call(
        latent_kernel,
        in_specs=[smem(), whole(), whole(), whole(), whole()],
        out_specs=[whole(), whole(), whole()],
        out_shape=[shape, shape, jax.ShapeDtypeStruct((frames, chunks, halves, 128), BF)],
        scratch_shapes=[pltpu.VMEM((cols + frames * chunks * halves, lanes), F32)],
        compiler_params=params(0, 8),
        cost_estimate=pl.CostEstimate(
            flops=2 * parts.size, bytes_accessed=2 * parts.size, transcendentals=0
        ),
        name="latent",
    )(step_index, parts, own, above, below)


def first_kernel(
    clean_ref, received_ref, own_ref, above_ref, below_ref, weight_ref, gain_ref, cached_ref, act_ref, send_ref, left, padded, scr
):
    three, cols, lanes = clean_ref.shape
    frames, coarse = act_ref.shape[:2]
    channels = act_ref.shape[3]
    group = lanes // 4
    slot = lanes // 2
    part = group // 2
    head = lax.axis_index("head")
    three_taps = weight_ref.shape[0] // 9
    gap = jnp.zeros((slot - three_taps, channels), BF)
    for n in range(9):
        padded[n * slot : n * slot + three_taps, :] = weight_ref[
            n * three_taps : (n + 1) * three_taps, :
        ]
        padded[n * slot + three_taps : (n + 1) * slot, :] = gap
    padded[9 * slot :, :] = jnp.zeros((slot, channels), BF)
    gains = gain_ref[...].astype(F32)
    gain = jnp.concatenate([gains[q : q + 1] for q in range(gains.shape[0])], axis=1)
    cached_old = jnp.concatenate(
        [
            above_ref[above_ref.shape[0] - cols :, lanes : 2 * lanes].astype(F32),
            own_ref[:, lanes : 2 * lanes].astype(F32),
            below_ref[below_ref.shape[0] - cols :, lanes : 2 * lanes].astype(F32),
        ],
        axis=0,
    )
    clean = jnp.concatenate([clean_ref[k].astype(F32) for k in range(three)], axis=0)
    arrived = jnp.concatenate([received_ref[k].astype(F32) for k in range(three)], axis=0)
    lane = lax.broadcasted_iota(jnp.int32, clean.shape, 1)
    line = lax.broadcasted_iota(jnp.int32, clean.shape, 0)
    at = lax.rem(line, cols)
    older = jnp.where(
        head == 0, jnp.where(lane < lanes // 2, cached_old, arrived), arrived
    )
    pieces = {}
    for source, x in enumerate((older, clean)):
        height = x.shape[0]
        before = jnp.where(at == 0, 0.0, pltpu.roll(x, 1, axis=0))
        after = jnp.where(at == cols - 1, 0.0, pltpu.roll(x, height - 1, axis=0))
        for f in range(2):
            for a in range(2):
                off = f * (lanes // 2) + a * group
                for side in range(2):
                    base = side * slot

                    low = lane - base
                    even = jnp.where(
                        (low >= 0) & (low < part),
                        moved(before, base - off - part),
                        jnp.where(
                            (low >= part) & (low < 3 * part), moved(x, base + part - off), 0.0
                        ),
                    )
                    odd = jnp.where(
                        (low >= 0) & (low < 2 * part),
                        moved(x, base - off),
                        jnp.where(
                            (low >= 2 * part) & (low < 3 * part),
                            moved(after, base + 2 * part - off),
                            0.0,
                        ),
                    )
                    pieces[source * 2 + f, a, side, 0] = even
                    pieces[source * 2 + f, a, side, 1] = odd

    def piece(p, fo, ro, n):
        frame = fo + n // 3
        row = ro + n % 3
        k = row // 2
        return pieces[frame, row % 2, n % 2, p][k * cols : (k + 1) * cols]

    for p in range(2):
        for fo in range(frames):
            for ro in range(coarse):
                start = ((p * frames + fo) * coarse + ro) * cols
                for j in range(5):
                    block = piece(p, fo, ro, 2 * j)
                    if 2 * j + 1 < 9:
                        block = block + piece(p, fo, ro, 2 * j + 1)
                    left[start : start + cols, j * lanes : (j + 1) * lanes] = block.astype(BF)

    feat = dot(left[...], padded[...])
    mean_square = jnp.mean(feat * feat, axis=-1, keepdims=True)
    normed = feat * lax.rsqrt(mean_square + NORM_EPSILON) * gain
    active = normed / (1.0 + jnp.exp(-normed))
    slab = lax.axis_index("seq")
    last = lax.axis_size("seq") - 1
    keep_first = jnp.where(slab == 0, 0.0, 1.0)
    keep_last = jnp.where(slab == last, 0.0, 1.0)
    for p in range(2):
        for fo in range(frames):
            for ro in range(coarse):
                start = ((p * frames + fo) * coarse + ro) * cols
                block = active[start : start + cols]
                if ro == 0:
                    block = block * keep_first
                if ro == coarse - 1:
                    block = block * keep_last
                to = (fo * coarse + ro) * 2 * cols + p
                for q in range(channels // 128):
                    scr[q, pl.ds(to, cols, stride=2), :] = block[:, q * 128 : (q + 1) * 128]
    for fo in range(frames):
        for ro in range(coarse):
            to = (fo * coarse + ro) * 2 * cols
            for q in range(channels // 128):
                act_ref[fo, ro, :, q * 128 : (q + 1) * 128] = scr[q, to : to + 2 * cols, :].astype(BF)

    @pl.when(head == 0)
    def _():
        send_ref[...] = act_ref[...]

    @pl.when(head != 0)
    def _():
        send_ref[...] = cached_ref[...]


def first(clean, received, own, above, below, weight, gain, cached_sum):
    three, cols, lanes = clean.shape
    shape = jax.ShapeDtypeStruct(cached_sum.shape, BF)
    frames, coarse, wide, channels = cached_sum.shape
    height = frames * coarse * wide
    return pl.pallas_call(
        first_kernel,
        in_specs=[whole()] * 8,
        out_specs=[whole(), whole()],
        out_shape=[shape, shape],
        scratch_shapes=[
            pltpu.VMEM((height, 5 * lanes), BF),
            pltpu.VMEM((5 * lanes, channels), BF),
            pltpu.VMEM((channels // 128, height, 128), F32),
        ],
        compiler_params=params(),
        cost_estimate=pl.CostEstimate(
            flops=2 * height * weight.size, bytes_accessed=4 * cached_sum.size, transcendentals=height * channels
        ),
        name="first",
    )(clean, received, own, above, below, weight, gain, cached_sum)


def swapped(array, axis):
    return lax.ppermute(array, axis, [(0, 1), (1, 0)])


def body(
    queries,
    keys,
    values,
    final_gain,
    out_weight,
    noisy_latent,
    step_index,
    span_index,
    cache_flags,
    latent_cache,
    feature_cache,
    first_weight,
    first_gain,
    second_weight,
):
    channels = first_weight.shape[1]
    slabs = lax.axis_size("seq")
    frames, halves, width = noisy_latent.shape
    second = second_weight.T

    own_frame, up, down, small = prepare(
        span_index, cache_flags, feature_cache, noisy_latent, latent_cache, channels
    )
    above = lax.ppermute(down, "seq", [(i, i + 1) for i in range(slabs - 1)])
    below = lax.ppermute(up, "seq", [(i + 1, i) for i in range(slabs - 1)])

    sent = attention(queries, keys, values, final_gain, out_weight)
    parts = lax.all_to_all(sent, "seq", 0, 0, tiled=True)
    mixed = mix(second)
    cached_sum = cached(own_frame, above, below, second)

    clean, send, out = latent(step_index, parts, small, above, below, frames, halves, width // 128)
    received = swapped(send, "head")
    activated, send = first(
        clean, received, small, above, below, first_weight, first_gain.reshape(-1, 128), cached_sum
    )
    arrived = swapped(send, "head")
    own_sum = own_part(activated, mixed)
    decoded = prior_part(arrived, cached_sum, own_sum, mixed)
    return (out.transpose(0, 2, 1, 3).reshape(frames, halves, width), decoded)


def solution(mesh):
    in_specs = (
        P(("grp", "head"), None, None, "seq"),
        P("grp", None, None, "seq"),
        P("grp", None, None, "seq"),
        P(),
        P(),
        P(("grp", "head"), "seq", None),
        P("grp"),
        P("grp"),
        P("grp", None, None),
        P("grp", "head", "seq", None),
        P("grp", "head", "seq", None),
        P(),
        P(),
        P(),
    )
    out_specs = (P(("grp", "head"), "seq", None), P(("grp", "head"), "seq", None))
    return jax.shard_map(body, mesh=mesh, in_specs=in_specs, out_specs=out_specs, check_vma=False)
```

time: 74.3 us -> 50.8 us (0.68)
  Pallas kernels: 36.6 us -> 20.3 us
  local copies, waits for them, and re-layouts: 18.9 us -> 9.86 us
  waiting for transfers between devices: 0.01 us -> 4.39 us
  other arithmetic: 2.19 us -> 0 us
    pallas_call x6 -> x7, Pallas kernels: 33.6 us -> 19.2 us  [the longest x1 4.12 us: prior_part(): pl.pallas_call(prior_kernel, grid=(parities,), in_specs=[pl.BlockSpec(rec...]
    ppermute x1, waiting for transfers between devices: 0.01 us -> 4.37 us  [body(): below = lax.ppermute(up, 'seq', [(i + 1, i) for i in range(slabs - 1)])]
    reshape x6 -> x0, local copies, waits for them, and re-layouts: 4.22 us -> none  [the longest x1 1.28 us: attention(): final_gain.reshape(1, -1)]
    unnamed x14 -> x26, local copies, waits for them, and re-layouts: 11.8 us -> 9.86 us
    pallas_call x1, Pallas kernels: 2.97 us -> 1.09 us  [prepare(): pl.pallas_call(prepare_kernel, grid_spec=grid_spec, out_shape=[jax.ShapeD...]
    pad x1 -> x0, local copies, waits for them, and re-layouts: 1.84 us -> none  [body(): jnp.pad(first_weight.reshape(9, 3 * width, channels), ((0, 1), (0, spare)...]
    convert_element_type x1 -> x0, other arithmetic: 0.76 us -> none  [body(): own_latent = own_latent * flags[:, None].astype(BF)]
  transfers between devices with their start and end apart: 5 -> 5, of which waited for: 0 -> 1; matrix products, arithmetic and copies ran while one was open for 21% -> 0% of each run, Pallas kernels for 24% -> 20%
where the time goes in v2:
time: 50.8 us; the launch traced here: 49.9 us
  Pallas kernels  20.3 us (40%)
  starting transfers between devices  13.3 us (26%)
  local copies, waits for them, and re-layouts  9.86 us (19%)
  waiting for transfers between devices  4.39 us (9%)
  between operations  2.08 us (4%)
    unnamed x26, local copies, waits for them, and re-layouts  9.86 us
    all_to_all x1, starting transfers between devices, body(): parts = lax.all_to_all(sent, 'seq', 0, 0, tiled=True)  5.74 us
    ppermute x1, waiting for transfers between devices, body(): below = lax.ppermute(up, 'seq', [(i + 1, i) for i in range(slabs - 1)])  4.37 us
    pallas_call x1, Pallas kernels, prior_part(): pl.pallas_call(prior_kernel, grid=(parities,), in_specs=[pl.BlockSpec(rec...  4.12 us
    pallas_call x1, Pallas kernels, cached(): pl.pallas_call(cached_kernel, in_specs=[whole()] * 4, out_specs=whole(),...  4.11 us
    pallas_call x1, Pallas kernels, attention(): pl.pallas_call(kernel, grid=(rows_total // rows,), in_specs=[pl.BlockSpec...  3.92 us
    ppermute x1, starting transfers between devices, body(): above = lax.ppermute(down, 'seq', [(i, i + 1) for i in range(slabs - 1)])  3.09 us
    ppermute x1, starting transfers between devices, body(): below = lax.ppermute(up, 'seq', [(i + 1, i) for i in range(slabs - 1)])  3.09 us
  transfers between devices with their start and end apart: 5, of which 1 were waited for; matrix products, arithmetic and copies ran while one was open for 0% of the time, Pallas kernels for 20%

profile of v2, /device:TPU:17, one launch (start us, length us, event | category | flops | bytes accessed | tf_op | source)
XLA Modules:
  0.0 49.9 jit_solution(16244210804965038584)
XLA Ops:
  0.6 0.0 copy-start.8
  0.6 1.0 %copy-done.8 = bf16[4,8,40,128]{3,2,1,0:T(8,128)(2,1)S(1)} copy-done((bf16[4,8,40,128]{3,2,1,0:T(8,128)(2,1)S(1)}, bf16[4,8,40,128]{3,2,1,0:T(8,128)(2,1)}, u32[]{:S(2)}) %copy-start.8) | copy-done | bytes 327704
  1.6 0.0 copy-start.9
  1.6 1.0 %copy-done.9 = bf16[4,8,40,128]{3,2,1,0:T(8,128)(2,1)S(1)} copy-done((bf16[4,8,40,128]{3,2,1,0:T(8,128)(2,1)S(1)}, bf16[4,8,40,128]{3,2,1,0:T(8,128)(2,1)}, u32[]{:S(2)}) %copy-start.9) | copy-done | bytes 327704
  2.6 0.0 copy-start.10
  2.6 0.9 %copy-done.10 = bf16[2,8,40,128]{3,2,1,0:T(8,128)(2,1)S(1)} copy-done((bf16[2,8,40,128]{3,2,1,0:T(8,128)(2,1)S(1)}, bf16[2,8,40,128]{3,2,1,0:T(8,128)(2,1)}, u32[]{:S(2)}) %copy-start.10) | copy-done | bytes 163864
  3.5 0.0 copy-start.11
  3.5 0.9 %copy-done.11 = bf16[1024,64]{0,1:T(8,128)(2,1)S(1)} copy-done((bf16[1024,64]{0,1:T(8,128)(2,1)S(1)}, bf16[1024,64]{0,1:T(8,128)(2,1)}, u32[]{:S(2)}) %copy-start.11) | copy-done | bytes 131096
  4.4 0.0 copy-start.12
  4.4 0.7 %copy-done.12 = bf16[1024]{0:T(1024)(128)(2,1)S(1)} copy-done((bf16[1024]{0:T(1024)(128)(2,1)S(1)}, bf16[1024]{0:T(1024)(128)(2,1)}, u32[]{:S(2)}) %copy-start.12) | copy-done | bytes 2072
  5.1 3.9 %attention.1 = bf16[8,3,48,128]{3,2,1,0:T(8,128)(2,1)} custom-call(bf16[2,320,128]{2,1,0:T(8,128)(2,1)S(1)} %bitcast.30, bf16[1280,128]{1,0:T(8,128)(2,1)S(1)} %bitcast.28, bf16[1280,128]{1,0:T(8,128)(2,1)S(1)} %bitcast.29, bf16[8,128]{1,0:T(8,128)(2,1)S(1)} %bitcast.32, bf16[64,1024]{1,0:T(8,128)(2,1)S(1)} %bitcast.31), custom_call_target="tpu_custom_call" | custom-call | flops 629145600 | bytes 819200 | tf_op jit(solution)/shard_map/attention/pallas_call | solution.py:108
  9.0 0.0 copy-start.3
  9.0 5.7 %all-to-all-start = ((bf16[8,3,48,128]{3,2,1,0:T(8,128)(2,1)}), bf16[8,3,48,128]{3,2,1,0:T(8,128)(2,1)S(1)}, u32[]{:S(2)}, u32[]{:S(2)}) async-start(bf16[8,3,48,128]{3,2,1,0:T(8,128)(2,1)} %attention.1), calls=%async_computation | async-start | bytes 589824 | tf_op jit(solution)/shard_map/all_to_all | solution.py:764
  14.7 0.0 copy-start.7
  15.4 0.0 copy-start.2
  15.4 1.2 %copy-done.2 = bf16[2,1,4,61440]{3,2,1,0:T(4,128)(2,1)S(1)} copy-done((bf16[2,1,4,61440]{3,2,1,0:T(4,128)(2,1)S(1)}, bf16[2,1,4,61440]{3,2,1,0:T(4,128)(2,1)}, u32[]{:S(2)}) %copy-start.2) | copy-done | bytes 983064
  16.6 0.0 copy-start.4
  16.6 0.7 %copy-done.4 = bf16[2,2,1280]{2,1,0:T(2,128)(2,1)S(1)} copy-done((bf16[2,2,1280]{2,1,0:T(2,128)(2,1)S(1)}, bf16[2,2,1280]{2,1,0:T(2,128)(2,1)}, u32[]{:S(2)}) %copy-start.4) | copy-done | bytes 10264
  17.3 0.0 copy-start.5
  17.3 0.7 %copy-done.5 = bf16[2,1,2,1280]{3,2,1,0:T(2,128)(2,1)S(1)} copy-done((bf16[2,1,2,1280]{3,2,1,0:T(2,128)(2,1)S(1)}, bf16[2,1,2,1280]{3,2,1,0:T(2,128)(2,1)}, u32[]{:S(2)}) %copy-start.5) | copy-done | bytes 10264
  18.0 0.0 copy-start.6
  18.0 0.7 %copy-done.6 = s32[2,2,16]{2,1,0:T(2,128)S(1)} copy-done((s32[2,2,16]{2,1,0:T(2,128)S(1)}, s32[2,2,16]{2,1,0:T(2,128)}, u32[]{:S(2)}) %copy-start.6) | copy-done | bytes 280
  18.7 1.1 %prepare.1 = (bf16[4,2,80,384]{3,2,1,0:T(8,128)(2,1)S(1)}, bf16[200,384]{1,0:T(8,128)(2,1)S(1)}, bf16[200,384]{1,0:T(8,128)(2,1)S(1)}, bf16[40,256]{1,0:T(8,128)(2,1)S(1)}) custom-call(s32[1]{0:T(128)S(6)} %copy.17.span_ref, s32[2,2,16]{2,1,0:T(2,128)S(1)} %copy-done.6, bf16[2,480,4,128]{3,2,1,0:T(4,128)(2,1)S(1)} %bitcast.24, ...), custom_call_target="tpu_custom_call" | custom-call | flops 245760 | bytes 1474560 | tf_op jit(solution)/shard_map/prepare/pallas_call | solution.py:237
  19.8 3.1 %collective-permute-start = (bf16[200,384]{1,0:T(8,128)(2,1)S(1)}, bf16[200,384]{1,0:T(8,128)(2,1)S(1)}, u32[]{:S(2)}, u32[]{:S(2)}) collective-permute-start(bf16[200,384]{1,0:T(8,128)(2,1)S(1)} %get-tuple-element.12), channel_id=1, source_target_pairs={{0,2},{2,4},{4,6},{6,8},{8,10},{10,12},{12,14},{1,3},{3,5},{5,7},{... | collective-permute-start | bytes 460808 | tf_op jit(solution)/shard_map/ppermute | solution.py:760
  22.9 3.1 %collective-permute-start.1 = (bf16[200,384]{1,0:T(8,128)(2,1)S(1)}, bf16[200,384]{1,0:T(8,128)(2,1)S(1)}, u32[]{:S(2)}, u32[]{:S(2)}) collective-permute-start(bf16[200,384]{1,0:T(8,128)(2,1)S(1)} %get-tuple-element.13), channel_id=1, source_target_pairs={{2,0},{4,2},{6,4},{8,6},{10,8},{12,10},{14,12},{3,1},{5,3},{7,5},{... | collective-permute-start | bytes 460808 | tf_op jit(solution)/shard_map/ppermute | solution.py:761
  26.7 0.0 collective-permute-done.above_ref
  26.7 4.4 %collective-permute-done.1.below_ref = bf16[200,384]{1,0:T(8,128)(2,1)S(1)} collective-permute-done((bf16[200,384]{1,0:T(8,128)(2,1)S(1)}, bf16[200,384]{1,0:T(8,128)(2,1)S(1)}, u32[]{:S(2)}, u32[]{:S(2)}) %collective-permute-start.1) | collective-permute-done | bytes 153632 | tf_op jit(solution)/shard_map/ppermute | solution.py:761
  31.0 0.0 all-to-all-done.parts_ref
  31.0 1.2 %latent.1 = (bf16[3,40,128]{2,1,0:T(8,128)(2,1)S(1)}, bf16[3,40,128]{2,1,0:T(8,128)(2,1)S(1)}, bf16[2,10,2,128]{3,2,1,0:T(2,128)(2,1)}) custom-call(s32[1]{0:T(128)S(6)} %copy.16.step_ref, bf16[8,3,48,128]{3,2,1,0:T(8,128)(2,1)S(1)} %all-to-all-done.parts_ref, bf16[40,256]{1,0:T(8,128)(2,1)S(1)} %get-tuple-element.11.own_ref, ...), custom_call_target="tpu_custom_call" | custom-call | flops 294912 | bytes 294912 | tf_op jit(solution)/shard_map/latent/pallas_call | solution.py:577
  32.3 1.3 %collective-permute-start.2 = (bf16[3,40,128]{2,1,0:T(8,128)(2,1)S(1)}, bf16[3,40,128]{2,1,0:T(8,128)(2,1)S(1)}, u32[]{:S(2)}, u32[]{:S(2)}) collective-permute-start(bf16[3,40,128]{2,1,0:T(8,128)(2,1)S(1)} %get-tuple-element.16), channel_id=1, source_target_pairs={{0,1},{1,0},{2,3},{3,2},{4,5},{5,4},{6,7},{7,6},{8,9},{9,8},{10,11... | collective-permute-start | bytes 92168 | tf_op jit(solution)/shard_map/ppermute | solution.py:733
  33.6 0.0 copy-start
  33.6 2.1 %copy-done = bf16[10368,192]{0,1:T(8,128)(2,1)S(1)} copy-done((bf16[10368,192]{0,1:T(8,128)(2,1)S(1)}, bf16[10368,192]{0,1:T(8,128)(2,1)}, u32[]{:S(2)}) %copy-start) | copy-done | bytes 3981336
  35.7 0.0 copy-start.1
  35.7 4.1 %cached.1.cached_ref = bf16[2,4,80,384]{3,2,1,0:T(8,128)(2,1)S(1)} custom-call(bf16[4,2,80,384]{3,2,1,0:T(8,128)(2,1)S(1)} %get-tuple-element.17.own_ref, bf16[200,384]{1,0:T(8,128)(2,1)S(1)} %collective-permute-done.above_ref, bf16[200,384]{1,0:T(8,128)(2,1)S(1)} %collective-permute-done.1.below_ref, bf16[192,10368]{1,0:T(8,128)(2,1)S(1)} %bitcast.22), custom_call_target="tpu_custom_call" | custom-call | flops 1698693120 | bytes 4472832 | tf_op jit(solution)/shard_map/cached/pallas_call | solution.py:315
  39.8 0.0 collective-permute-done.2.received_ref
  39.8 0.0 copy-done.3
  39.8 0.0 copy-done.7
  39.8 1.3 %first.1 = (bf16[2,4,80,384]{3,2,1,0:T(8,128)(2,1)S(1)}, bf16[2,4,80,384]{3,2,1,0:T(8,128)(2,1)S(1)}) custom-call(bf16[3,40,128]{2,1,0:T(8,128)(2,1)S(1)} %get-tuple-element.15.clean_ref, bf16[3,40,128]{2,1,0:T(8,128)(2,1)S(1)} %collective-permute-done.2.received_ref, bf16[40,256]{1,0:T(8,128)(2,1)S(1)} %get-tuple-element.11.own_ref, ...), custom_call_target="tpu_custom_call" | custom-call | flops 212336640 | bytes 983040 | tf_op jit(solution)/shard_map/first/pallas_call | solution.py:714
  41.1 0.1 collective-permute-start.3
  41.2 0.0 copy-done.1
  41.2 1.9 %mix.1.old_ref.new_ref = bf16[3,4,192,1536]{3,2,1,0:T(8,128)(2,1)S(1)} custom-call(bf16[192,10368]{1,0:T(8,128)(2,1)S(1)} %bitcast.23), custom_call_target="tpu_custom_call" | custom-call | flops 7962624 | bytes 11943936 | tf_op jit(solution)/shard_map/mix/pallas_call | solution.py:359
  43.1 2.7 %own_part.1.own_ref = f32[4,2,2,80,192]{4,3,2,1,0:T(8,128)S(1)} custom-call(bf16[2,4,80,384]{3,2,1,0:T(8,128)(2,1)S(1)} %get-tuple-element.19.source_ref, bf16[3,4,192,1536]{3,2,1,0:T(8,128)(2,1)S(1)} %mix.1.old_ref.new_ref, bf16[3,4,192,1536]{3,2,1,0:T(8,128)(2,1)S(1)} %mix.1.old_ref.new_ref), custom_call_target="tpu_custom_call" | custom-call | flops 1132462080 | bytes 5210112 | tf_op jit(solution)/shard_map/own_part/pallas_call | solution.py:419
  45.8 0.0 collective-permute-done.3.source_ref
  45.8 4.1 %prior_part.1 = bf16[2,240,4,128]{3,2,1,0:T(4,128)(2,1)} custom-call(bf16[2,4,80,384]{3,2,1,0:T(8,128)(2,1)S(1)} %collective-permute-done.3.source_ref, bf16[2,4,80,384]{3,2,1,0:T(8,128)(2,1)S(1)} %cached.1.cached_ref, f32[4,2,2,80,192]{4,3,2,1,0:T(8,128)S(1)} %own_part.1.own_ref, bf16[3,4,192,1536]{3,2,1,0:T(8,128)(2,1)S(1)} %mix.1.old_ref.new_ref, ...), custom_call_target="tpu_custom_call" | custom-call | flops 1132462080 | bytes 5210112 | tf_op jit(solution)/shard_map/prior_part/pallas_call | solution.py:497
Async XLA Ops:
  0.6 1.0 %copy-start.8 = (bf16[4,8,40,128]{3,2,1,0:T(8,128)(2,1)S(1)}, bf16[4,8,40,128]{3,2,1,0:T(8,128)(2,1)}, u32[]{:S(2)}) copy-start(bf16[4,8,40,128]{3,2,1,0:T(8,128)(2,1)} %param.15) | copy-start | bytes 983044
  1.6 1.0 %copy-start.9 = (bf16[4,8,40,128]{3,2,1,0:T(8,128)(2,1)S(1)}, bf16[4,8,40,128]{3,2,1,0:T(8,128)(2,1)}, u32[]{:S(2)}) copy-start(bf16[4,8,40,128]{3,2,1,0:T(8,128)(2,1)} %param.16) | copy-start | bytes 983044
  2.6 0.9 %copy-start.10 = (bf16[2,8,40,128]{3,2,1,0:T(8,128)(2,1)S(1)}, bf16[2,8,40,128]{3,2,1,0:T(8,128)(2,1)}, u32[]{:S(2)}) copy-start(bf16[2,8,40,128]{3,2,1,0:T(8,128)(2,1)} %param.14) | copy-start | bytes 491524
  3.5 0.9 %copy-start.11 = (bf16[1024,64]{0,1:T(8,128)(2,1)S(1)}, bf16[1024,64]{0,1:T(8,128)(2,1)}, u32[]{:S(2)}) copy-start(bf16[1024,64]{0,1:T(8,128)(2,1)} %param.18) | copy-start | bytes 393220
  4.4 0.7 %copy-start.12 = (bf16[1024]{0:T(1024)(128)(2,1)S(1)}, bf16[1024]{0:T(1024)(128)(2,1)}, u32[]{:S(2)}) copy-start(bf16[1024]{0:T(1024)(128)(2,1)} %param.17) | copy-start | bytes 6148
  9.0 30.8 %copy-start.3 = (bf16[432,384]{1,0:T(8,128)(2,1)S(1)}, bf16[432,384]{1,0:T(8,128)(2,1)}, u32[]{:S(2)}) copy-start(bf16[432,384]{1,0:T(8,128)(2,1)} %weight_ref.1) | copy-start | bytes 995332
  9.0 22.0 %all-to-all-start = ((bf16[8,3,48,128]{3,2,1,0:T(8,128)(2,1)}), bf16[8,3,48,128]{3,2,1,0:T(8,128)(2,1)S(1)}, u32[]{:S(2)}, u32[]{:S(2)}) async-start(bf16[8,3,48,128]{3,2,1,0:T(8,128)(2,1)} %attention.1), calls=%async_computation | async-start | bytes 589824 | tf_op jit(solution)/shard_map/all_to_all | solution.py:764
  14.7 25.1 %copy-start.7 = (bf16[384]{0:T(512)(128)(2,1)S(1)}, bf16[384]{0:T(512)(128)(2,1)}, u32[]{:S(2)}) copy-start(bf16[384]{0:T(512)(128)(2,1)} %param.26) | copy-start | bytes 2308
  15.4 1.2 %copy-start.2 = (bf16[2,1,4,61440]{3,2,1,0:T(4,128)(2,1)S(1)}, bf16[2,1,4,61440]{3,2,1,0:T(4,128)(2,1)}, u32[]{:S(2)}) copy-start(bf16[2,1,4,61440]{3,2,1,0:T(4,128)(2,1)} %param.24) | copy-start | bytes 2949124
  16.6 0.7 %copy-start.4 = (bf16[2,2,1280]{2,1,0:T(2,128)(2,1)S(1)}, bf16[2,2,1280]{2,1,0:T(2,128)(2,1)}, u32[]{:S(2)}) copy-start(bf16[2,2,1280]{2,1,0:T(2,128)(2,1)} %param.19) | copy-start | bytes 30724
  17.3 0.7 %copy-start.5 = (bf16[2,1,2,1280]{3,2,1,0:T(2,128)(2,1)S(1)}, bf16[2,1,2,1280]{3,2,1,0:T(2,128)(2,1)}, u32[]{:S(2)}) copy-start(bf16[2,1,2,1280]{3,2,1,0:T(2,128)(2,1)} %param.23) | copy-start | bytes 30724
  18.0 0.7 %copy-start.6 = (s32[2,2,16]{2,1,0:T(2,128)S(1)}, s32[2,2,16]{2,1,0:T(2,128)}, u32[]{:S(2)}) copy-start(s32[2,2,16]{2,1,0:T(2,128)} %flags_ref.1) | copy-start | bytes 772
  19.8 6.9 %collective-permute-start = (bf16[200,384]{1,0:T(8,128)(2,1)S(1)}, bf16[200,384]{1,0:T(8,128)(2,1)S(1)}, u32[]{:S(2)}, u32[]{:S(2)}) collective-permute-start(bf16[200,384]{1,0:T(8,128)(2,1)S(1)} %get-tuple-element.12), channel_id=1, source_target_pairs={{0,2},{2,4},{4,6},{6,8},{8,10},{10,12},{12,14},{1,3},{3,5},{5,7},{... | collective-permute-start | bytes 460808 | tf_op jit(solution)/shard_map/ppermute | solution.py:760
  22.9 8.1 %collective-permute-start.1 = (bf16[200,384]{1,0:T(8,128)(2,1)S(1)}, bf16[200,384]{1,0:T(8,128)(2,1)S(1)}, u32[]{:S(2)}, u32[]{:S(2)}) collective-permute-start(bf16[200,384]{1,0:T(8,128)(2,1)S(1)} %get-tuple-element.13), channel_id=1, source_target_pairs={{2,0},{4,2},{6,4},{8,6},{10,8},{12,10},{14,12},{3,1},{5,3},{7,5},{... | collective-permute-start | bytes 460808 | tf_op jit(solution)/shard_map/ppermute | solution.py:761
  32.3 7.5 %collective-permute-start.2 = (bf16[3,40,128]{2,1,0:T(8,128)(2,1)S(1)}, bf16[3,40,128]{2,1,0:T(8,128)(2,1)S(1)}, u32[]{:S(2)}, u32[]{:S(2)}) collective-permute-start(bf16[3,40,128]{2,1,0:T(8,128)(2,1)S(1)} %get-tuple-element.16), channel_id=1, source_target_pairs={{0,1},{1,0},{2,3},{3,2},{4,5},{5,4},{6,7},{7,6},{8,9},{9,8},{10,11... | collective-permute-start | bytes 92168 | tf_op jit(solution)/shard_map/ppermute | solution.py:733
  33.6 2.1 %copy-start = (bf16[10368,192]{0,1:T(8,128)(2,1)S(1)}, bf16[10368,192]{0,1:T(8,128)(2,1)}, u32[]{:S(2)}) copy-start(bf16[10368,192]{0,1:T(8,128)(2,1)} %param.27) | copy-start | bytes 11943940
  35.7 5.5 %copy-start.1 = (bf16[10368,192]{0,1:T(8,128)(2,1)S(1)}, bf16[10368,192]{0,1:T(8,128)(2,1)}, u32[]{:S(2)}) copy-start(bf16[10368,192]{0,1:T(8,128)(2,1)} %param.27) | copy-start | bytes 11943940
  41.1 4.7 %collective-permute-start.3 = (bf16[2,4,80,384]{3,2,1,0:T(8,128)(2,1)S(1)}, bf16[2,4,80,384]{3,2,1,0:T(8,128)(2,1)S(1)}, u32[]{:S(2)}, u32[]{:S(2)}) collective-permute-start(bf16[2,4,80,384]{3,2,1,0:T(8,128)(2,1)S(1)} %get-tuple-element.18), channel_id=1, source_target_pairs={{0,1},{1,0},{2,3},{3,2},{4,5},{5,4},{6,7},{7,6},{8,9},{9,8},{10,11... | collective-permute-start | bytes 1474568 | tf_op jit(solution)/shard_map/ppermute | solution.py:733

commit v3 on v2

--- a/solution.py
+++ b/solution.py
@@ -14,7 +14,7 @@
 LAST = (((1,), (1,)), ((), ()))
 
 
-def params(dims=0, mib=20):
+def params(dims=0, mib=12):
     semantics = ("arbitrary",) * dims if dims else None
     return pltpu.CompilerParams(dimension_semantics=semantics, vmem_limit_bytes=mib << 20)
 
@@ -27,19 +27,72 @@
     return lax.dot_general(left, right, LAST, preferred_element_type=F32)
 
 
+def far(array):
+    return pltpu.with_memory_space_constraint(array, pltpu.HBM)
+
+
+def far_spec():
+    return pl.BlockSpec(memory_space=pltpu.HBM)
+
+
 def whole():
     return pl.BlockSpec(memory_space=pltpu.VMEM)
 
 
-def smem():
-    return pl.BlockSpec(memory_space=pltpu.SMEM)
-
-
-def attention_kernel(q_ref, k_ref, v_ref, gain_ref, weight_ref, out_ref, *, cols, rows_total):
-    frames, block, head_size = q_ref.shape
-    rows = block // cols
-    step = pl.program_id(0)
+def attention_kernel(
+    code_ref,
+    flags_hbm,
+    q_hbm,
+    k_hbm,
+    v_hbm,
+    gain_hbm,
+    weight_hbm,
+    cache_hbm,
+    noisy_hbm,
+    latent_hbm,
+    out_ref,
+    facts_ref,
+    cache_ref,
+    noisy_ref,
+    latent_ref,
+    flags_ref,
+    q_ref,
+    k_ref,
+    v_ref,
+    gain_ref,
+    weight_ref,
+    sems,
+    *,
+    cols,
+    rows,
+):
     slab = lax.axis_index("seq")
+    head = lax.axis_index("head")
+    frames, query_count, head_size = q_ref.shape
+    rows_total = query_count // cols
+    count = [0]
+
+    def load(source, target):
+        copy = pltpu.make_async_copy(source, target, sems.at[count[0]])
+        count[0] += 1
+        copy.start()
+        return copy
+
+    slot = lax.rem(code_ref[0] // NSTEPS, CSLOTS)
+    key_copies = [load(q_hbm, q_ref), load(k_hbm, k_ref)]
+    value_copies = [load(v_hbm, v_ref), load(gain_hbm, gain_ref), load(weight_hbm, weight_ref)]
+    later = [
+        load(flags_hbm, flags_ref),
+        load(cache_hbm.at[slot], cache_ref),
+        load(latent_hbm.at[slot], latent_ref),
+        load(noisy_hbm, noisy_ref),
+    ]
+    edge = jnp.zeros(out_ref.shape[2:], BF)
+    out_ref[0, 0] = edge
+    out_ref[rows_total - 1, 2] = edge
+    for copy in key_copies + value_copies:
+        copy.wait()
+
     scale = 1.4426950408889634 / head_size**0.5
     keys = k_ref[...]
     values = jnp.concatenate([v_ref[...], jnp.ones_like(v_ref[...])], axis=1)
@@ -50,47 +103,85 @@
     weight = weight_ref[:, pl.ds(start, head_size)]
     none = jnp.zeros_like(weight)
     line_of = lax.broadcasted_iota(jnp.int32, (8, head_size), 0)
-    total = None
-    squares = []
-    for f in range(frames):
-        scores = dot_last(q_ref[f], keys)
-        row_max = jnp.max(scores, axis=1, keepdims=True)
-        weights = jnp.exp2((scores - row_max) * scale).astype(BF)
-        blended = dot(weights, values)
-        attended = (blended[:, :head_size] / blended[:, head_size:]).astype(BF).astype(F32)
-        side = [none] * frames
-        side[f] = weight
-        part = dot_last((attended * gain).astype(BF), jnp.concatenate(side, axis=0))
-        total = part if total is None else total + part
-        squares.append(attended * attended)
-
-    @pl.when(step == 0)
-    def _():
-        out_ref[0, 0] = jnp.zeros(out_ref.shape[2:], BF)
-        out_ref[rows_total - 1, 2] = jnp.zeros(out_ref.shape[2:], BF)
-
-    for r in range(rows):
-        sums = None
+
+    def block(step):
+        total = None
+        squares = []
         for f in range(frames):
-            piece = squares[f][r * cols : (r + 1) * cols].astype(BF)
-            line = dot_last((line_of == f).astype(F32).astype(BF), piece)
-            sums = line if sums is None else sums + line
-        lanes = total.shape[1]
-        sums = jnp.concatenate([sums, jnp.zeros((8, lanes - cols), F32)], axis=1)
-        unit = jnp.concatenate([total[r * cols : (r + 1) * cols], sums], axis=0).astype(BF)
-        row = step * rows + r
-        out_ref[row, 1] = unit
-
-        @pl.when(row + 1 < rows_total)
-        def _():
-            out_ref[jnp.minimum(row + 1, rows_total - 1), 0] = unit
-
-        @pl.when(row > 0)
-        def _():
-            out_ref[jnp.maximum(row - 1, 0), 2] = unit
-
-
-def attention(queries, keys, values, final_gain, out_weight):
+            at = step * (rows * cols)
+            if not isinstance(step, int):
+                at = pl.multiple_of(at, 16)
+            scores = dot_last(q_ref[f, pl.ds(at, rows * cols), :], keys)
+            row_max = jnp.max(scores, axis=1, keepdims=True)
+            weights = jnp.exp2((scores - row_max) * scale).astype(BF)
+            blended = dot(weights, values)
+            attended = (blended[:, :head_size] / blended[:, head_size:]).astype(BF).astype(F32)
+            side = [none] * frames
+            side[f] = weight
+            part = dot_last((attended * gain).astype(BF), jnp.concatenate(side, axis=0))
+            total = part if total is None else total + part
+            squares.append(attended * attended)
+        for r in range(rows):
+            sums = None
+            for f in range(frames):
+                piece = squares[f][r * cols : (r + 1) * cols].astype(BF)
+                line = dot_last((line_of == f).astype(F32).astype(BF), piece)
+                sums = line if sums is None else sums + line
+            lanes = total.shape[1]
+            sums = jnp.concatenate([sums, jnp.zeros((8, lanes - cols), F32)], axis=1)
+            unit = jnp.concatenate([total[r * cols : (r + 1) * cols], sums], axis=0).astype(BF)
+            row = step * rows + r
+            out_ref[row, 1] = unit
+            if isinstance(step, int):
+                if row + 1 < rows_total:
+                    out_ref[row + 1, 0] = unit
+                if row > 0:
+                    out_ref[row - 1, 2] = unit
+            else:
+
+                @pl.when(row + 1 < rows_total)
+                def _():
+                    out_ref[jnp.minimum(row + 1, rows_total - 1), 0] = unit
+
+                @pl.when(row > 0)
+                def _():
+                    out_ref[jnp.maximum(row - 1, 0), 2] = unit
+
+    steps = rows_total // rows
+    if steps <= 2:
+        for step in range(steps):
+            block(step)
+    else:
+
+        def one(step, carry):
+            block(step)
+            return carry
+
+        lax.fori_loop(0, steps, one, 0)
+
+    for copy in later:
+        copy.wait()
+    fraction = 1.0 - lax.rem(code_ref[0], NSTEPS).astype(F32) / NSTEPS
+    fraction = jnp.full((1, 128), fraction, F32)
+    facts_ref[0:1, :] = SHIFT_FACTOR * fraction / (1.0 + (SHIFT_FACTOR - 1.0) * fraction)
+    coarse = noisy_ref.shape[2]
+    for r in range(coarse):
+        flag = flags_ref[slot, head, slab * coarse + r].astype(F32)
+        facts_ref[1 + r : 2 + r, :] = jnp.full((1, 128), flag, F32)
+
+
+def attention(
+    queries,
+    keys,
+    values,
+    final_gain,
+    out_weight,
+    code,
+    cache_flags,
+    feature_cache,
+    noisy_latent,
+    latent_cache,
+):
     frames, rows_total, cols, head_size = queries.shape
     q = queries.reshape(frames, rows_total * cols, head_size)
     k = keys.reshape(-1, head_size)
@@ -100,31 +191,60 @@
     rows = 4 if rows_total % 4 == 0 else rows_total
     lanes = frames * weight.shape[0]
     unit = cols + 8
+    cache = tiled(feature_cache[:, 0])
+    noisy = tiled(noisy_latent)
+    latents = tiled(latent_cache[:, 0])
 
     def kernel(*refs):
-        attention_kernel(*refs, cols=cols, rows_total=rows_total)
+        attention_kernel(*refs, cols=cols, rows=rows)
 
     count = frames * rows_total * cols
+    shapes = [
+        ((rows_total, 3, unit, lanes), BF),
+        ((8, 128), F32),
+        (cache.shape[1:], BF),
+        (noisy.shape, BF),
+        (latents.shape[1:], BF),
+    ]
     return pl.pallas_call(
         kernel,
-        grid=(rows_total // rows,),
-        in_specs=[
-            pl.BlockSpec((frames, rows * cols, head_size), lambda i: (0, i, 0)),
-            pl.BlockSpec(k.shape, lambda i: (0, 0)),
-            pl.BlockSpec(v.shape, lambda i: (0, 0)),
-            pl.BlockSpec(gains.shape, lambda i: (0, 0)),
-            pl.BlockSpec(weight.shape, lambda i: (0, 0)),
-        ],
-        out_specs=pl.BlockSpec((rows_total, 3, unit, lanes), lambda i: (0, 0, 0, 0)),
-        out_shape=jax.ShapeDtypeStruct((rows_total, 3, unit, lanes), BF),
-        compiler_params=params(1, 40),
+        in_specs=[pl.BlockSpec(memory_space=pltpu.SMEM)]
+        + [far_spec()] * 9,
+        out_specs=[whole()] * len(shapes),
+        out_shape=[pltpu.VMEM(shape, kind) for shape, kind in shapes],
+        scratch_shapes=[
+            pltpu.SMEM(cache_flags.shape, jnp.int32),
+            pltpu.VMEM(q.shape, BF),
+            pltpu.VMEM(k.shape, BF),
+            pltpu.VMEM(v.shape, BF),
+            pltpu.VMEM(gains.shape, BF),
+            pltpu.VMEM(weight.shape, BF),
+            pltpu.SemaphoreType.DMA((9,)),
+        ],
+        compiler_params=params(0, 16),
         cost_estimate=pl.CostEstimate(
             flops=6 * count * k.shape[0] * head_size,
             bytes_accessed=2 * (q.size + k.size + v.size),
             transcendentals=count * k.shape[0],
         ),
         name="attention",
-    )(q, k, v, gains, weight)
+    )(
+        code,
+        *[
+            far(array)
+            for array in (
+                cache_flags,
+                q,
+                k,
+                v,
+                gains,
+                weight,
+                cache,
+                noisy,
+                latents,
+            )
+        ]
+    )
 
 
 def lane_groups(array, group):
@@ -137,24 +257,20 @@
     return pltpu.roll(array, shift, axis=1) if shift else array
 
 
-def prepare_kernel(
-    span_ref, flags_ref, cache_ref, noisy_ref, latent_ref, own_ref, up_ref, down_ref, small_ref, scr, lat
-):
-    tiles, rows, lanes = cache_ref.shape[1:]
+def prepare_kernel(facts_ref, cache_ref, noisy_ref, latent_ref, own_ref, up_ref, down_ref, small_ref, scr, lat):
+    tiles, rows, lanes = cache_ref.shape
     cols, channels = own_ref.shape[2:]
     pieces = channels // lanes
-    slot = lax.rem(span_ref[0], CSLOTS)
-    slab = lax.axis_index("seq")
-    head = lax.axis_index("head")
     coarse = rows // 2
-    flags = [flags_ref[slot, head, slab * coarse + r].astype(F32) for r in range(coarse)]
+    flags = [facts_ref[1 + r : 2 + r, :] for r in range(coarse)]
+    whole_column = 2 * pieces * rows
 
     frames, chunks, halves = noisy_ref.shape[:3]
     groups = frames * halves
     group = lanes // groups
     for f in range(frames + 1):
         for i in range(chunks):
-            tile = latent_ref[0, i] if f == frames else noisy_ref[f, i]
+            tile = latent_ref[i] if f == frames else noisy_ref[f, i]
             lat[pl.ds((f * chunks + i) * halves, halves), :] = tile.astype(F32)
     lines = [
         [lat[pl.ds(f * chunks * halves + a, chunks, stride=halves), :] for a in range(halves)]
@@ -180,24 +296,32 @@
     up_ref[2 * cols :, 2 * lanes :] = rest
     down_ref[2 * cols :, 2 * lanes :] = rest
 
+    pad = jnp.zeros((whole_column, lanes), F32)
+    scr[:whole_column, :] = pad
+    scr[whole_column + tiles * rows :, :] = pad
+
     def unpack(i, carry):
         for n in range(16):
             at = i * 16 + n
-            scr[pl.ds(pl.multiple_of(at * rows, rows), rows), :] = cache_ref[0, at].astype(F32)
+            to = pl.multiple_of(whole_column + at * rows, rows)
+            scr[pl.ds(to, rows), :] = cache_ref[at].astype(F32)
         return carry
 
     lax.fori_loop(0, tiles // 16, unpack, 0)
     for r in range(rows):
-        for b in range(2):
+        for n in range(4):
             for q in range(pieces):
-                start = (b * pieces + q) * rows + r
-                piece = scr[pl.ds(start, cols, stride=2 * pieces * rows), :]
+                column = whole_column * ((n + 1) // 2) + ((n + 1) % 2) * pieces * rows
+                start = column + q * rows + r
+                piece = scr[pl.ds(start, cols, stride=whole_column), :]
                 piece = (piece * flags[r // 2]).astype(BF)
-                own_ref[r, b, :, q * lanes : (q + 1) * lanes] = piece
-                if r == 0:
-                    up_ref[b * cols : (b + 1) * cols, q * lanes : (q + 1) * lanes] = piece
-                if r == rows - 1:
-                    down_ref[b * cols : (b + 1) * cols, q * lanes : (q + 1) * lanes] = piece
+                own_ref[n, r, :, q * lanes : (q + 1) * lanes] = piece
+                if n in (1, 2):
+                    to = slice((n - 1) * cols, n * cols)
+                    if r == 0:
+                        up_ref[to, q * lanes : (q + 1) * lanes] = piece
+                    if r == rows - 1:
+                        down_ref[to, q * lanes : (q + 1) * lanes] = piece
 
 
 def tiled(array):
@@ -207,48 +331,32 @@
     return view.transpose(*range(count), count + 1, count, count + 2)
 
 
-def prepare(span_index, cache_flags, feature_cache, noisy_latent, latent_cache, channels):
-    slots, _, rows, width = feature_cache.shape
-    tiles = width // 128
-    cols = width // channels // 2
-    noisy = tiled(noisy_latent)
+def prepare(facts, cache, noisy, latents, channels):
+    tiles, rows, lanes = cache.shape
+    cols = tiles * lanes // channels // 2
     frames, chunks, halves = noisy.shape[:3]
     tokens = chunks * frames * halves
     halo = 2 * cols + tokens
-    grid_spec = pltpu.PrefetchScalarGridSpec(
-        num_scalar_prefetch=2,
-        grid=(1,),
-        in_specs=[
-            pl.BlockSpec((1, tiles, rows, 128), lambda i, s, f: (lax.rem(s[0], CSLOTS), 0, 0, 0)),
-            pl.BlockSpec(noisy.shape, lambda i, s, f: (0, 0, 0, 0)),
-            pl.BlockSpec((1, chunks, halves, 128), lambda i, s, f: (lax.rem(s[0], CSLOTS), 0, 0, 0)),
-        ],
-        out_specs=[
-            pl.BlockSpec((rows, 2, cols, channels), lambda i, s, f: (0, 0, 0, 0)),
-            pl.BlockSpec((halo, channels), lambda i, s, f: (0, 0)),
-            pl.BlockSpec((halo, channels), lambda i, s, f: (0, 0)),
-            pl.BlockSpec((tokens, 256), lambda i, s, f: (0, 0)),
-        ],
-        scratch_shapes=[
-            pltpu.VMEM((tiles * rows, 128), F32),
-            pltpu.VMEM(((frames + 1) * chunks * halves + 2 * tokens, 128), F32),
-        ],
-    )
     return pl.pallas_call(
         prepare_kernel,
-        grid_spec=grid_spec,
+        in_specs=[whole()] * 4,
+        out_specs=[whole()] * 4,
         out_shape=[
-            jax.ShapeDtypeStruct((rows, 2, cols, channels), BF),
+            jax.ShapeDtypeStruct((4, rows, cols, channels), BF),
             jax.ShapeDtypeStruct((halo, channels), BF),
             jax.ShapeDtypeStruct((halo, channels), BF),
             jax.ShapeDtypeStruct((tokens, 256), BF),
         ],
-        compiler_params=params(1),
+        scratch_shapes=[
+            pltpu.VMEM((tiles * rows + 4 * channels // lanes * rows, lanes), F32),
+            pltpu.VMEM(((frames + 1) * chunks * halves + 2 * tokens, lanes), F32),
+        ],
+        compiler_params=params(),
         cost_estimate=pl.CostEstimate(
-            flops=rows * width, bytes_accessed=6 * rows * width, transcendentals=0
+            flops=cache.size, bytes_accessed=6 * cache.size, transcendentals=0
         ),
         name="prepare",
-    )(span_index, cache_flags, tiled(feature_cache[:, 0]), noisy, tiled(latent_cache[:, 0]))
+    )(facts, cache, noisy, latents)
 
 
 def shift_down(array):
@@ -264,76 +372,35 @@
     return jnp.where(rows == count - 1, 0.0, moved_rows)
 
 
-def cached_kernel(own_ref, above_ref, below_ref, weight_ref, out_ref, var):
-    rows, _, cols, channels = own_ref.shape
-    for r in range(rows + 2):
-        if r == 0:
-            even, odd = above_ref[:cols], above_ref[cols : 2 * cols]
-        elif r == rows + 1:
-            even, odd = below_ref[:cols], below_ref[cols : 2 * cols]
-        else:
-            even, odd = own_ref[r - 1, 0], own_ref[r - 1, 1]
-        var[0, r] = shift_down(odd.astype(F32)).astype(BF)
-        var[1, r] = even
-        var[2, r] = odd
-        var[3, r] = shift_up(even.astype(F32)).astype(BF)
-
-    def contribute(f, base):
-        for r in range(0, rows, 2):
-            sides = []
-            for b in range(2):
-                total = None
-                for h in range(3):
-                    left = jnp.concatenate(
-                        [
-                            var[b + w, r + h : r + h + 2].reshape(2 * cols, channels)
-                            for w in range(3)
-                        ],
-                        axis=1,
-                    )
-                    start = pl.multiple_of(base + h * 3 * channels, 128)
-                    part = dot_last(left, weight_ref[:, pl.ds(start, 3 * channels)])
-                    total = part if total is None else total + part
-                sides.append(total)
-            both = jnp.concatenate(sides, axis=1).astype(BF)
-            out_ref[f, r : r + 2] = both.reshape(2, cols, both.shape[1])
-
-    head = lax.axis_index("head")
-    contribute(0, head * (9 * channels))
-
-    @pl.when(head == 0)
-    def _():
-        out_ref[1] = jnp.zeros(out_ref.shape[1:], BF)
-
-    @pl.when(head != 0)
-    def _():
-        contribute(1, 0)
-
-
-def cached(own, above, below, weight):
-    rows, _, cols, channels = own.shape
-    return pl.pallas_call(
-        cached_kernel,
-        in_specs=[whole()] * 4,
-        out_specs=whole(),
-        out_shape=jax.ShapeDtypeStruct((2, rows, cols, 2 * weight.shape[0]), BF),
-        scratch_shapes=[pltpu.VMEM((4, rows + 2, cols, channels), BF)],
-        compiler_params=params(),
-        cost_estimate=pl.CostEstimate(
-            flops=2 * 2 * rows * 2 * cols * 9 * channels * weight.shape[0],
-            bytes_accessed=2 * (own.size + weight.size),
-            transcendentals=0,
-        ),
-        name="cached",
-    )(own, above, below, weight)
-
-
-def mix_kernel(weight_ref, out_ref):
-    channels = weight_ref.shape[1] // 9
+def cached_sum(line, rows, weight):
+    lines = []
+    for b in range(2):
+        for r in rows:
+            lines.append(
+                jnp.concatenate(
+                    [line(b + w, r + h - 1) for h in range(3) for w in range(3)], axis=1
+                )
+            )
+    total = dot_last(jnp.concatenate(lines, axis=0), weight)
+    half = total.shape[0] // 2
+    return jnp.concatenate([total[:half], total[half:]], axis=1).astype(BF)
+
+
+def slices(weight_hbm, weight_ref, sems, count):
+    depth = weight_ref.shape[2]
+    copies = []
+    for t in range(count):
+        source = weight_hbm.at[:, pl.ds(t * depth, depth)]
+        copies.append(pltpu.make_async_copy(source, weight_ref.at[t], sems.at[t]))
+    return copies
+
+
+def mix_third(weight_ref, out_ref, t):
+    channels = weight_ref.shape[2] // 9
 
     def tap(h, w):
         start = (h * 3 + w) * channels
-        return weight_ref[:, start : start + channels].astype(F32)
+        return weight_ref[t, :, start : start + channels].astype(F32)
 
     lines = {}
     for w in range(3):
@@ -349,25 +416,135 @@
             for b in range(2):
                 for v in range(2):
                     start = (u * 2 + v) * channels
-                    out_ref[0, a * 2 + b, :, start : start + channels] = mixed[b][v].astype(BF)
-
-
-def mix(weight):
+                    out_ref[t, a * 2 + b, :, start : start + channels] = mixed[b][v].astype(BF)
+
+
+def mix_kernel(own_ref, weight_hbm, mixed_hbm, middle_ref, weight_ref, mixed_ref, sems, out_sems):
+    rows = own_ref.shape[1]
+    head = lax.axis_index("head")
+    inner = range(1, rows - 1)
+    copies = slices(weight_hbm, weight_ref, sems, 3)
+    for copy in copies:
+        copy.start()
+
+    def line(n, r):
+        return own_ref[n, r]
+
+    outs = [pltpu.make_async_copy(mixed_ref.at[t], mixed_hbm.at[t], out_sems.at[t]) for t in range(3)]
+    shape = middle_ref.shape[1:]
+    for t in range(3):
+        copies[t].wait()
+        mix_third(weight_ref, mixed_ref, t)
+        outs[t].start()
+        if t == 0:
+
+            @pl.when(head == 0)
+            def _():
+                middle_ref[0] = cached_sum(line, inner, weight_ref[0]).reshape(shape)
+                middle_ref[1] = jnp.zeros(shape, BF)
+
+            @pl.when(head != 0)
+            def _():
+                middle_ref[1] = cached_sum(line, inner, weight_ref[0]).reshape(shape)
+
+        if t == 1:
+
+            @pl.when(head != 0)
+            def _():
+                middle_ref[0] = cached_sum(line, inner, weight_ref[1]).reshape(shape)
+
+    for copy in outs:
+        copy.wait()
+
+
+def mix(own, weight):
+    _, rows, cols, channels = own.shape
     out, height = weight.shape
     third = height // 3
     shape = (3, 4, out, third // 9 * 4)
     return pl.pallas_call(
         mix_kernel,
-        grid=(3,),
-        in_specs=[pl.BlockSpec((out, third), lambda t: (0, t))],
-        out_specs=pl.BlockSpec((1,) + shape[1:], lambda t: (t, 0, 0, 0)),
-        out_shape=jax.ShapeDtypeStruct(shape, BF),
-        compiler_params=params(1),
+        in_specs=[whole(), far_spec()],
+        out_specs=[far_spec(), whole()],
+        out_shape=[
+            pltpu.HBM(shape, BF),
+            jax.ShapeDtypeStruct((2, rows - 2, cols, 2 * out), BF),
+        ],
+        scratch_shapes=[
+            pltpu.VMEM((3, out, third), BF),
+            pltpu.VMEM(shape, BF),
+            pltpu.SemaphoreType.DMA((3,)),
+            pltpu.SemaphoreType.DMA((3,)),
+        ],
+        compiler_params=params(0, 24),
         cost_estimate=pl.CostEstimate(
-            flops=4 * weight.size, bytes_accessed=6 * weight.size, transcendentals=0
+            flops=2 * 2 * 2 * 2 * cols * third * out,
+            bytes_accessed=6 * weight.size,
+            transcendentals=0,
         ),
         name="mix",
-    )(weight)
+    )(own, far(weight))
+
+
+def edge_kernel(own_ref, above_ref, below_ref, weight_hbm, out_ref, var, weight_ref, sems):
+    _, rows, cols, channels = own_ref.shape
+    head = lax.axis_index("head")
+    first_copy, second_copy = slices(weight_hbm, weight_ref, sems, 2)
+    first_copy.start()
+
+    @pl.when(head != 0)
+    def _():
+        second_copy.start()
+
+    for n, rim in enumerate((above_ref, below_ref)):
+        even, odd = rim[:cols], rim[cols : 2 * cols]
+        var[n, 0] = shift_down(odd.astype(F32)).astype(BF)
+        var[n, 1] = even
+        var[n, 2] = odd
+        var[n, 3] = shift_up(even.astype(F32)).astype(BF)
+
+    def line(n, r):
+        if r < 0:
+            return var[0, n]
+        return var[1, n] if r == rows else own_ref[n, r]
+
+    outer = (0, rows - 1)
+    shape = out_ref.shape[1:]
+    first_copy.wait()
+
+    @pl.when(head == 0)
+    def _():
+        out_ref[0] = cached_sum(line, outer, weight_ref[0]).reshape(shape)
+        out_ref[1] = jnp.zeros(shape, BF)
+
+    @pl.when(head != 0)
+    def _():
+        out_ref[1] = cached_sum(line, outer, weight_ref[0]).reshape(shape)
+        second_copy.wait()
+        out_ref[0] = cached_sum(line, outer, weight_ref[1]).reshape(shape)
+
+
+def edges(own, above, below, weight):
+    _, rows, cols, channels = own.shape
+    out, height = weight.shape
+    return pl.pallas_call(
+        edge_kernel,
+        in_specs=[whole(), whole(), whole(), far_spec()],
+        out_specs=whole(),
+        out_shape=jax.ShapeDtypeStruct((2, 2, cols, 2 * out), BF),
+        scratch_shapes=[
+            pltpu.VMEM((2, 4, cols, channels), BF),
+            pltpu.VMEM((2, out, height // 3), BF),
+            pltpu.SemaphoreType.DMA((2,)),
+        ],
+        compiler_params=params(),
+        cost_estimate=pl.CostEstimate(
+            flops=2 * 2 * 2 * 2 * cols * 9 * channels * out,
+            bytes_accessed=2 * (own.size + weight.size),
+            transcendentals=0,
+        ),
+        name="edge",
+    )(own, above, below, far(weight))
 
 
 def spread(source_ref, var):
@@ -434,10 +611,10 @@
             transcendentals=0,
         ),
         name="own_part",
-    )(activated, mixed, mixed)
-
-
-def prior_kernel(source_ref, cached_ref, own_ref, old_ref, new_ref, out_ref, var, total_ref, scr):
+    )(activated, far(mixed), far(mixed))
+
+
+def prior_kernel(source_ref, middle_ref, edge_ref, own_ref, old_ref, new_ref, out_ref, var, total_ref, scr):
     parities, frames, coarse_rows, cols, width = total_ref.shape
     head = lax.axis_index("head")
     step = pl.program_id(0)
@@ -471,7 +648,11 @@
                 side = (row % 2) * 2
                 sides = [total_ref[side + n, f, row // 2] for n in range(2)]
                 line = jnp.concatenate(sides, axis=1)
-                extra = cached_ref[f, row].astype(F32) + source_ref[f, row].astype(F32)
+                if row in (0, fine - 1):
+                    mine = edge_ref[f, min(row, 1)]
+                else:
+                    mine = middle_ref[f, row - 1]
+                extra = mine.astype(F32) + source_ref[f, row].astype(F32)
                 line = line + keep * extra
                 for q in range(pieces):
                     scr[pl.ds(q * fine + row, cols, stride=pieces * fine), :] = line[
@@ -488,7 +669,7 @@
             lax.fori_loop(0, out_ref.shape[1] // 16, pack, 0)
 
 
-def prior_part(received, cached_sum, own_sum, mixed):
+def prior_part(received, middle, edge, own_sum, mixed):
     frames, coarse, cols, channels = received.shape
     _, parities, width, depth = mixed.shape
     fine = 2 * (coarse - 2)
@@ -499,7 +680,8 @@
         grid=(parities,),
         in_specs=[
             pl.BlockSpec(received.shape, lambda i: (0, 0, 0, 0)),
-            pl.BlockSpec(cached_sum.shape, lambda i: (0, 0, 0, 0)),
+            pl.BlockSpec(middle.shape, lambda i: (0, 0, 0, 0)),
+            pl.BlockSpec(edge.shape, lambda i: (0, 0, 0, 0)),
             pl.BlockSpec((1,) + own_sum.shape[1:], lambda i: (i, 0, 0, 0, 0)),
             pl.BlockSpec(block, lambda i: (0, i, 0, 0)),
             pl.BlockSpec(block, lambda i: (1, i, 0, 0)),
@@ -518,20 +700,18 @@
             transcendentals=0,
         ),
         name="prior_part",
-    )(received, cached_sum, own_sum, mixed, mixed)
+    )(received, middle, edge, own_sum, far(mixed), far(mixed))
     return out.transpose(0, 2, 1, 3).reshape(frames, fine, tiles * 128)
 
 
-def latent_kernel(step_ref, parts_ref, own_ref, above_ref, below_ref, clean_ref, send_ref, out_ref, scr):
+def latent_kernel(facts_ref, parts_ref, own_ref, above_ref, below_ref, clean_ref, send_ref, out_ref, scr):
     sources, three, unit, lanes = parts_ref.shape
     cols = own_ref.shape[0]
     frames, chunks, halves = out_ref.shape[:3]
     groups = frames * halves
     group = lanes // groups
     features = sources * 128
-    fraction = 1.0 - step_ref[0].astype(F32) / NSTEPS
-    fraction = jnp.full((1, lanes), fraction, F32)
-    level = SHIFT_FACTOR * fraction / (1.0 + (SHIFT_FACTOR - 1.0) * fraction)
+    level = facts_ref[0:1, :]
     total = parts_ref[0].astype(F32)
     for source in range(1, sources):
         total = total + parts_ref[source].astype(F32)
@@ -570,13 +750,13 @@
             out_ref[f, i] = scr[at : at + halves, :].astype(BF)
 
 
-def latent(step_index, parts, own, above, below, frames, halves, chunks):
+def latent(facts, parts, own, above, below, frames, halves, chunks):
     sources, three, unit, lanes = parts.shape
     cols = own.shape[0]
     shape = jax.ShapeDtypeStruct((three, cols, lanes), BF)
     return pl.pallas_call(
         latent_kernel,
-        in_specs=[smem(), whole(), whole(), whole(), whole()],
+        in_specs=[whole()] * 5,
         out_specs=[whole(), whole(), whole()],
         out_shape=[shape, shape, jax.ShapeDtypeStruct((frames, chunks, halves, 128), BF)],
         scratch_shapes=[pltpu.VMEM((cols + frames * chunks * halves, lanes), F32)],
@@ -585,11 +765,11 @@
             flops=2 * parts.size, bytes_accessed=2 * parts.size, transcendentals=0
         ),
         name="latent",
-    )(step_index, parts, own, above, below)
+    )(facts, parts, own, above, below)
 
 
 def first_kernel(
-    clean_ref, received_ref, own_ref, above_ref, below_ref, weight_ref, gain_ref, cached_ref, act_ref, send_ref, left, padded, scr
+    clean_ref, received_ref, own_ref, above_ref, below_ref, weight_ref, gain_ref, middle_ref, edge_ref, act_ref, send_ref, left, padded, scr
 ):
     three, cols, lanes = clean_ref.shape
     frames, coarse = act_ref.shape[:2]
@@ -703,17 +883,22 @@
 
     @pl.when(head != 0)
     def _():
-        send_ref[...] = cached_ref[...]
-
-
-def first(clean, received, own, above, below, weight, gain, cached_sum):
+        for fo in range(frames):
+            send_ref[fo, 0] = edge_ref[fo, 0]
+            send_ref[fo, coarse - 1] = edge_ref[fo, 1]
+            for ro in range(1, coarse - 1):
+                send_ref[fo, ro] = middle_ref[fo, ro - 1]
+
+
+def first(clean, received, own, above, below, weight, gain, middle, edge):
     three, cols, lanes = clean.shape
-    shape = jax.ShapeDtypeStruct(cached_sum.shape, BF)
-    frames, coarse, wide, channels = cached_sum.shape
+    frames, inner, wide, channels = middle.shape
+    coarse = inner + 2
+    shape = jax.ShapeDtypeStruct((frames, coarse, wide, channels), BF)
     height = frames * coarse * wide
     return pl.pallas_call(
         first_kernel,
-        in_specs=[whole()] * 8,
+        in_specs=[whole()] * 9,
         out_specs=[whole(), whole()],
         out_shape=[shape, shape],
         scratch_shapes=[
@@ -723,10 +908,10 @@
         ],
         compiler_params=params(),
         cost_estimate=pl.CostEstimate(
-            flops=2 * height * weight.size, bytes_accessed=4 * cached_sum.size, transcendentals=height * channels
+            flops=2 * height * weight.size, bytes_accessed=8 * middle.size, transcendentals=height * channels
         ),
         name="first",
-    )(clean, received, own, above, below, weight, gain, cached_sum)
+    )(clean, received, own, above, below, weight, gain, middle, edge)
 
 
 def swapped(array, axis):
@@ -754,25 +939,34 @@
     frames, halves, width = noisy_latent.shape
     second = second_weight.T
 
-    own_frame, up, down, small = prepare(
-        span_index, cache_flags, feature_cache, noisy_latent, latent_cache, channels
+    sent, facts, cache, noisy, latents = attention(
+        queries,
+        keys,
+        values,
+        final_gain,
+        out_weight,
+        span_index * NSTEPS + step_index,
+        cache_flags,
+        feature_cache,
+        noisy_latent,
+        latent_cache,
     )
+    parts = lax.all_to_all(sent, "seq", 0, 0, tiled=True)
+    own_frame, up, down, small = prepare(facts, cache, noisy, latents, channels)
     above = lax.ppermute(down, "seq", [(i, i + 1) for i in range(slabs - 1)])
     below = lax.ppermute(up, "seq", [(i + 1, i) for i in range(slabs - 1)])
-
-    sent = attention(queries, keys, values, final_gain, out_weight)
-    parts = lax.all_to_all(sent, "seq", 0, 0, tiled=True)
-    mixed = mix(second)
-    cached_sum = cached(own_frame, above, below, second)
-
-    clean, send, out = latent(step_index, parts, small, above, below, frames, halves, width // 128)
+    mixed, middle = mix(own_frame, second)
+    above, below, middle = lax.optimization_barrier((above, below, middle))
+
+    clean, send, out = latent(facts, parts, small, above, below, frames, halves, width // 128)
+    edge = edges(own_frame, above, below, second)
     received = swapped(send, "head")
     activated, send = first(
-        clean, received, small, above, below, first_weight, first_gain.reshape(-1, 128), cached_sum
+        clean, received, small, above, below, first_weight, first_gain.reshape(-1, 128), middle, edge
     )
     arrived = swapped(send, "head")
     own_sum = own_part(activated, mixed)
-    decoded = prior_part(arrived, cached_sum, own_sum, mixed)
+    decoded = prior_part(arrived, middle, edge, own_sum, mixed)
     return (out.transpose(0, 2, 1, 3).reshape(frames, halves, width), decoded)
 
 

time: 50.8 us -> 45.2 us (0.89)
  local copies, waits for them, and re-layouts: 9.86 us -> 0.01 us
  Pallas kernels: 20.3 us -> 28.4 us
  waiting for transfers between devices: 4.39 us -> 1.48 us
    unnamed x26 -> x4, local copies, waits for them, and re-layouts: 9.86 us -> 0.01 us
    pallas_call x6, Pallas kernels: 13.5 us -> 17.7 us  [the longest x1 6.13 us: mix(): pl.pallas_call(mix_kernel, in_specs=[whole(), far_spec()], out_specs=[far...]
    ppermute x1, waiting for transfers between devices: 4.37 us -> 1.47 us  [body(): below = lax.ppermute(up, 'seq', [(i + 1, i) for i in range(slabs - 1)])]
    pallas_call x1, Pallas kernels: 2.68 us -> 4.63 us  [own_part(): pl.pallas_call(own_kernel, grid=(parities,), in_specs=[pl.BlockSpec(activ...]
    pallas_call x1, Pallas kernels: 4.12 us -> 6.04 us  [prior_part(): pl.pallas_call(prior_kernel, grid=(parities,), in_specs=[pl.BlockSpec(rec...]
  transfers between devices with their start and end apart: 5 -> 5, of which waited for: 1 -> 1; matrix products, arithmetic and copies ran while one was open for 0% -> 0% of each run, Pallas kernels for 20% -> 35%
where the time goes in v3:
time: 45.2 us; the launch traced here: 44.8 us
  Pallas kernels  28.4 us (63%)
  starting transfers between devices  12.8 us (28%)
  between operations  2.05 us (5%)
  waiting for transfers between devices  1.48 us (3%)
    pallas_call x1, Pallas kernels, mix(): pl.pallas_call(mix_kernel, in_specs=[whole(), far_spec()], out_specs=[far...  6.13 us
    pallas_call x1, Pallas kernels, prior_part(): pl.pallas_call(prior_kernel, grid=(parities,), in_specs=[pl.BlockSpec(rec...  6.04 us
    all_to_all x1, starting transfers between devices, body(): parts = lax.all_to_all(sent, 'seq', 0, 0, tiled=True)  5.62 us
    pallas_call x1, Pallas kernels, own_part(): pl.pallas_call(own_kernel, grid=(parities,), in_specs=[pl.BlockSpec(activ...  4.63 us
    pallas_call x1, Pallas kernels, attention(): pl.pallas_call(kernel, in_specs=[pl.BlockSpec(memory_space=pltpu.SMEM)] +...  4.2 us
    pallas_call x1, Pallas kernels, edges(): pl.pallas_call(edge_kernel, in_specs=[whole(), whole(), whole(), far_spec...  4.17 us
    ppermute x1, starting transfers between devices, body(): above = lax.ppermute(down, 'seq', [(i, i + 1) for i in range(slabs - 1)])  3.09 us
    ppermute x1, starting transfers between devices, body(): below = lax.ppermute(up, 'seq', [(i + 1, i) for i in range(slabs - 1)])  3.09 us
  transfers between devices with their start and end apart: 5, of which 1 were waited for; matrix products, arithmetic and copies ran while one was open for 0% of the time, Pallas kernels for 35%

profile of v3, /device:TPU:17, one launch (start us, length us, event | category | flops | bytes accessed | tf_op | source)
XLA Modules:
  0.0 44.8 jit_solution(12853696009073152912)
XLA Ops:
  1.9 4.2 %attention.1 = (bf16[8,3,48,128]{3,2,1,0:T(8,128)(2,1)}, f32[8,128]{1,0:T(8,128)S(1)}, bf16[480,4,128]{2,1,0:T(4,128)(2,1)S(1)}, bf16[2,10,2,128]{3,2,1,0:T(2,128)(2,1)S(1)}, bf16[10,2,128]{2,1,0:T(2,128)(2,1)S(1)}) custom-call(s32[1]{0:T(128)S(6)} %add.3.refs_0_, s32[2,2,16]{2,1,0:T(2,128)} %refs_1_.1, bf16[2,320,128]{2,1,0:T(8,128)(2,1)} %bitcast.29, ...), custom_call_target="tpu_custom_call" | custom-call | flops 629145600 | bytes 819200 | tf_op jit(solution)/shard_map/attention/pallas_call | solution.py:209
  6.1 5.6 %all-to-all-start = ((bf16[8,3,48,128]{3,2,1,0:T(8,128)(2,1)}), bf16[8,3,48,128]{3,2,1,0:T(8,128)(2,1)S(1)}, u32[]{:S(2)}, u32[]{:S(2)}) async-start(bf16[8,3,48,128]{3,2,1,0:T(8,128)(2,1)} %get-tuple-element.22), calls=%async_computation | async-start | bytes 589824 | tf_op jit(solution)/shard_map/all_to_all | solution.py:954
  11.8 0.7 %prepare.1 = (bf16[4,4,80,384]{3,2,1,0:T(8,128)(2,1)S(1)}, bf16[200,384]{1,0:T(8,128)(2,1)S(1)}, bf16[200,384]{1,0:T(8,128)(2,1)S(1)}, bf16[40,256]{1,0:T(8,128)(2,1)S(1)}) custom-call(f32[8,128]{1,0:T(8,128)S(1)} %get-tuple-element.21.facts_ref, bf16[480,4,128]{2,1,0:T(4,128)(2,1)S(1)} %get-tuple-element.23.cache_ref, ...), custom_call_target="tpu_custom_call" | custom-call | flops 245760 | bytes 1474560 | tf_op jit(solution)/shard_map/prepare/pallas_call | solution.py:340
  12.5 3.1 %collective-permute-start = (bf16[200,384]{1,0:T(8,128)(2,1)S(1)}, bf16[200,384]{1,0:T(8,128)(2,1)S(1)}, u32[]{:S(2)}, u32[]{:S(2)}) collective-permute-start(bf16[200,384]{1,0:T(8,128)(2,1)S(1)} %get-tuple-element.27), channel_id=1, source_target_pairs={{0,2},{2,4},{4,6},{6,8},{8,10},{10,12},{12,14},{1,3},{3,5},{5,7},{... | collective-permute-start | bytes 460808 | tf_op jit(solution)/shard_map/ppermute | solution.py:956
  15.6 3.1 %collective-permute-start.1 = (bf16[200,384]{1,0:T(8,128)(2,1)S(1)}, bf16[200,384]{1,0:T(8,128)(2,1)S(1)}, u32[]{:S(2)}, u32[]{:S(2)}) collective-permute-start(bf16[200,384]{1,0:T(8,128)(2,1)S(1)} %get-tuple-element.28), channel_id=1, source_target_pairs={{2,0},{4,2},{6,4},{8,6},{10,8},{12,10},{14,12},{3,1},{5,3},{7,5},{... | collective-permute-start | bytes 460808 | tf_op jit(solution)/shard_map/ppermute | solution.py:957
  18.7 6.1 %mix.1 = (bf16[3,4,192,1536]{3,2,1,0:T(8,128)(2,1)}, bf16[2,2,80,384]{3,2,1,0:T(8,128)(2,1)S(1)}) custom-call(bf16[4,4,80,384]{3,2,1,0:T(8,128)(2,1)S(1)} %get-tuple-element.29.own_ref, bf16[192,10368]{1,0:T(8,128)(2,1)} %bitcast.23), custom_call_target="tpu_custom_call" | custom-call | flops 849346560 | bytes 11943936 | tf_op jit(solution)/shard_map/mix/pallas_call | solution.py:465
  24.8 0.0 copy-start
  24.8 0.0 copy-start.1
  24.8 0.0 collective-permute-done.above_ref
  24.8 1.5 %collective-permute-done.1.below_ref = bf16[200,384]{1,0:T(8,128)(2,1)S(1)} collective-permute-done((bf16[200,384]{1,0:T(8,128)(2,1)S(1)}, bf16[200,384]{1,0:T(8,128)(2,1)S(1)}, u32[]{:S(2)}, u32[]{:S(2)}) %collective-permute-start.1) | collective-permute-done | bytes 153632 | tf_op jit(solution)/shard_map/ppermute | solution.py:957
  26.3 0.0 all-to-all-done.parts_ref
  26.3 1.2 %latent.1 = (bf16[3,40,128]{2,1,0:T(8,128)(2,1)S(1)}, bf16[3,40,128]{2,1,0:T(8,128)(2,1)S(1)}, bf16[2,10,2,128]{3,2,1,0:T(2,128)(2,1)}) custom-call(f32[8,128]{1,0:T(8,128)S(1)} %get-tuple-element.21.facts_ref, bf16[8,3,48,128]{3,2,1,0:T(8,128)(2,1)S(1)} %all-to-all-done.parts_ref, bf16[40,256]{1,0:T(8,128)(2,1)S(1)} %get-tuple-element.26.own_ref, ...), custom_call_target="tpu_custom_call" | custom-call | flops 294912 | bytes 294912 | tf_op jit(solution)/shard_map/latent/pallas_call | solution.py:757
  27.5 0.9 %collective-permute-start.2 = (bf16[3,40,128]{2,1,0:T(8,128)(2,1)S(1)}, bf16[3,40,128]{2,1,0:T(8,128)(2,1)S(1)}, u32[]{:S(2)}, u32[]{:S(2)}) collective-permute-start(bf16[3,40,128]{2,1,0:T(8,128)(2,1)S(1)} %get-tuple-element.35), channel_id=1, source_target_pairs={{0,1},{1,0},{2,3},{3,2},{4,5},{5,4},{6,7},{7,6},{8,9},{9,8},{10,11... | collective-permute-start | bytes 92168 | tf_op jit(solution)/shard_map/ppermute | solution.py:918
  28.5 4.2 %edge.1.edge_ref = bf16[2,2,80,384]{3,2,1,0:T(8,128)(2,1)S(1)} custom-call(bf16[4,4,80,384]{3,2,1,0:T(8,128)(2,1)S(1)} %get-tuple-element.29.own_ref, bf16[200,384]{1,0:T(8,128)(2,1)S(1)} %collective-permute-done.above_ref, bf16[200,384]{1,0:T(8,128)(2,1)S(1)} %collective-permute-done.1.below_ref, bf16[192,10368]{1,0:T(8,128)(2,1)} %bitcast.24), custom_call_target="tpu_custom_call" | custom-call | flops 849346560 | bytes 4964352 | tf_op jit(solution)/shard_map/edge/pallas_call | solution.py:530
  32.7 0.0 collective-permute-done.2.received_ref
  32.7 0.0 copy-done
  32.7 0.0 copy-done.1
  32.7 1.3 %first.1 = (bf16[2,4,80,384]{3,2,1,0:T(8,128)(2,1)S(1)}, bf16[2,4,80,384]{3,2,1,0:T(8,128)(2,1)S(1)}) custom-call(bf16[3,40,128]{2,1,0:T(8,128)(2,1)S(1)} %get-tuple-element.34.clean_ref, bf16[3,40,128]{2,1,0:T(8,128)(2,1)S(1)} %collective-permute-done.2.received_ref, bf16[40,256]{1,0:T(8,128)(2,1)S(1)} %get-tuple-element.26.own_ref, ...), custom_call_target="tpu_custom_call" | custom-call | flops 212336640 | bytes 983040 | tf_op jit(solution)/shard_map/first/pallas_call | solution.py:899
  34.0 0.1 collective-permute-start.3
  34.1 4.6 %own_part.1.own_ref = f32[4,2,2,80,192]{4,3,2,1,0:T(8,128)S(1)} custom-call(bf16[2,4,80,384]{3,2,1,0:T(8,128)(2,1)S(1)} %get-tuple-element.38.source_ref, bf16[3,4,192,1536]{3,2,1,0:T(8,128)(2,1)} %get-tuple-element.39.old_ref.new_ref, bf16[3,4,192,1536]{3,2,1,0:T(8,128)(2,1)} %get-tuple-element.39.old_ref.new_ref), custom_call_target="tpu_custom_call" | custom-call | flops 1132462080 | bytes 5210112 | tf_op jit(solution)/shard_map/own_part/pallas_call | solution.py:596
  38.7 0.0 collective-permute-done.3.source_ref
  38.7 6.0 %prior_part.1 = bf16[2,240,4,128]{3,2,1,0:T(4,128)(2,1)} custom-call(bf16[2,4,80,384]{3,2,1,0:T(8,128)(2,1)S(1)} %collective-permute-done.3.source_ref, bf16[2,2,80,384]{3,2,1,0:T(8,128)(2,1)S(1)} %get-tuple-element.36.middle_ref, bf16[2,2,80,384]{3,2,1,0:T(8,128)(2,1)S(1)} %edge.1.edge_ref, f32[4,2,2,80,192]{4,3,2,1,0:T(8,128)S(1)} %own_part.1.own_ref, ...), custom_call_target="tpu_custom_call" | custom-call | flops 1132462080 | bytes 5210112 | tf_op jit(solution)/shard_map/prior_part/pallas_call | solution.py:678
Async XLA Ops:
  6.1 20.2 %all-to-all-start = ((bf16[8,3,48,128]{3,2,1,0:T(8,128)(2,1)}), bf16[8,3,48,128]{3,2,1,0:T(8,128)(2,1)S(1)}, u32[]{:S(2)}, u32[]{:S(2)}) async-start(bf16[8,3,48,128]{3,2,1,0:T(8,128)(2,1)} %get-tuple-element.22), calls=%async_computation | async-start | bytes 589824 | tf_op jit(solution)/shard_map/all_to_all | solution.py:954
  12.5 12.4 %collective-permute-start = (bf16[200,384]{1,0:T(8,128)(2,1)S(1)}, bf16[200,384]{1,0:T(8,128)(2,1)S(1)}, u32[]{:S(2)}, u32[]{:S(2)}) collective-permute-start(bf16[200,384]{1,0:T(8,128)(2,1)S(1)} %get-tuple-element.27), channel_id=1, source_target_pairs={{0,2},{2,4},{4,6},{6,8},{8,10},{10,12},{12,14},{1,3},{3,5},{5,7},{... | collective-permute-start | bytes 460808 | tf_op jit(solution)/shard_map/ppermute | solution.py:956
  15.6 10.7 %collective-permute-start.1 = (bf16[200,384]{1,0:T(8,128)(2,1)S(1)}, bf16[200,384]{1,0:T(8,128)(2,1)S(1)}, u32[]{:S(2)}, u32[]{:S(2)}) collective-permute-start(bf16[200,384]{1,0:T(8,128)(2,1)S(1)} %get-tuple-element.28), channel_id=1, source_target_pairs={{2,0},{4,2},{6,4},{8,6},{10,8},{12,10},{14,12},{3,1},{5,3},{7,5},{... | collective-permute-start | bytes 460808 | tf_op jit(solution)/shard_map/ppermute | solution.py:957
  24.8 7.9 %copy-start = (bf16[432,384]{1,0:T(8,128)(2,1)S(1)}, bf16[432,384]{1,0:T(8,128)(2,1)}, u32[]{:S(2)}) copy-start(bf16[432,384]{1,0:T(8,128)(2,1)} %weight_ref.1) | copy-start | bytes 995332
  24.8 7.9 %copy-start.1 = (bf16[384]{0:T(512)(128)(2,1)S(1)}, bf16[384]{0:T(512)(128)(2,1)}, u32[]{:S(2)}) copy-start(bf16[384]{0:T(512)(128)(2,1)} %param.26) | copy-start | bytes 2308
  27.5 5.1 %collective-permute-start.2 = (bf16[3,40,128]{2,1,0:T(8,128)(2,1)S(1)}, bf16[3,40,128]{2,1,0:T(8,128)(2,1)S(1)}, u32[]{:S(2)}, u32[]{:S(2)}) collective-permute-start(bf16[3,40,128]{2,1,0:T(8,128)(2,1)S(1)} %get-tuple-element.35), channel_id=1, source_target_pairs={{0,1},{1,0},{2,3},{3,2},{4,5},{5,4},{6,7},{7,6},{8,9},{9,8},{10,11... | collective-permute-start | bytes 92168 | tf_op jit(solution)/shard_map/ppermute | solution.py:918
  34.0 4.7 %collective-permute-start.3 = (bf16[2,4,80,384]{3,2,1,0:T(8,128)(2,1)S(1)}, bf16[2,4,80,384]{3,2,1,0:T(8,128)(2,1)S(1)}, u32[]{:S(2)}, u32[]{:S(2)}) collective-permute-start(bf16[2,4,80,384]{3,2,1,0:T(8,128)(2,1)S(1)} %get-tuple-element.37), channel_id=1, source_target_pairs={{0,1},{1,0},{2,3},{3,2},{4,5},{5,4},{6,7},{7,6},{8,9},{9,8},{10,11... | collective-permute-start | bytes 1474568 | tf_op jit(solution)/shard_map/ppermute | solution.py:918

commit v4 on v3

--- a/solution.py
+++ b/solution.py
@@ -27,6 +27,10 @@
     return lax.dot_general(left, right, LAST, preferred_element_type=F32)
 
 
+def smem():
+    return pl.BlockSpec(memory_space=pltpu.SMEM)
+
+
 def far(array):
     return pltpu.with_memory_space_constraint(array, pltpu.HBM)
 
@@ -40,7 +44,6 @@
 
 
 def attention_kernel(
-    code_ref,
     flags_hbm,
     q_hbm,
     k_hbm,
@@ -78,13 +81,12 @@
         copy.start()
         return copy
 
-    slot = lax.rem(code_ref[0] // NSTEPS, CSLOTS)
     key_copies = [load(q_hbm, q_ref), load(k_hbm, k_ref)]
     value_copies = [load(v_hbm, v_ref), load(gain_hbm, gain_ref), load(weight_hbm, weight_ref)]
     later = [
         load(flags_hbm, flags_ref),
-        load(cache_hbm.at[slot], cache_ref),
-        load(latent_hbm.at[slot], latent_ref),
+        load(cache_hbm, cache_ref),
+        load(latent_hbm, latent_ref),
         load(noisy_hbm, noisy_ref),
     ]
     edge = jnp.zeros(out_ref.shape[2:], BF)
@@ -161,13 +163,12 @@
 
     for copy in later:
         copy.wait()
-    fraction = 1.0 - lax.rem(code_ref[0], NSTEPS).astype(F32) / NSTEPS
-    fraction = jnp.full((1, 128), fraction, F32)
-    facts_ref[0:1, :] = SHIFT_FACTOR * fraction / (1.0 + (SHIFT_FACTOR - 1.0) * fraction)
-    coarse = noisy_ref.shape[2]
-    for r in range(coarse):
-        flag = flags_ref[slot, head, slab * coarse + r].astype(F32)
-        facts_ref[1 + r : 2 + r, :] = jnp.full((1, 128), flag, F32)
+    slots, _, coarse, _ = latent_ref.shape
+    for slot in range(slots):
+        for r in range(coarse):
+            flag = flags_ref[slot, head, slab * coarse + r].astype(F32)
+            at = slot * coarse + r
+            facts_ref[at : at + 1, :] = jnp.full((1, 128), flag, F32)
 
 
 def attention(
@@ -176,7 +177,6 @@
     values,
     final_gain,
     out_weight,
-    code,
     cache_flags,
     feature_cache,
     noisy_latent,
@@ -202,14 +202,13 @@
     shapes = [
         ((rows_total, 3, unit, lanes), BF),
         ((8, 128), F32),
-        (cache.shape[1:], BF),
+        (cache.shape, BF),
         (noisy.shape, BF),
-        (latents.shape[1:], BF),
+        (latents.shape, BF),
     ]
     return pl.pallas_call(
         kernel,
-        in_specs=[pl.BlockSpec(memory_space=pltpu.SMEM)]
-        + [far_spec()] * 9,
+        in_specs=[far_spec()] * 9,
         out_specs=[whole()] * len(shapes),
         out_shape=[pltpu.VMEM(shape, kind) for shape, kind in shapes],
         scratch_shapes=[
@@ -229,7 +228,6 @@
         ),
         name="attention",
     )(
-        code,
         *[
             far(array)
             for array in (
@@ -257,12 +255,13 @@
     return pltpu.roll(array, shift, axis=1) if shift else array
 
 
-def prepare_kernel(facts_ref, cache_ref, noisy_ref, latent_ref, own_ref, up_ref, down_ref, small_ref, scr, lat):
-    tiles, rows, lanes = cache_ref.shape
+def prepare_kernel(span_ref, facts_ref, cache_ref, noisy_ref, latent_ref, own_ref, up_ref, down_ref, small_ref, scr, lat):
+    _, tiles, rows, lanes = cache_ref.shape
     cols, channels = own_ref.shape[2:]
     pieces = channels // lanes
     coarse = rows // 2
-    flags = [facts_ref[1 + r : 2 + r, :] for r in range(coarse)]
+    slot = lax.rem(span_ref[0], CSLOTS)
+    flags = [facts_ref[pl.ds(slot * coarse + r, 1), :] for r in range(coarse)]
     whole_column = 2 * pieces * rows
 
     frames, chunks, halves = noisy_ref.shape[:3]
@@ -270,7 +269,7 @@
     group = lanes // groups
     for f in range(frames + 1):
         for i in range(chunks):
-            tile = latent_ref[i] if f == frames else noisy_ref[f, i]
+            tile = latent_ref[slot, i] if f == frames else noisy_ref[f, i]
             lat[pl.ds((f * chunks + i) * halves, halves), :] = tile.astype(F32)
     lines = [
         [lat[pl.ds(f * chunks * halves + a, chunks, stride=halves), :] for a in range(halves)]
@@ -304,7 +303,7 @@
         for n in range(16):
             at = i * 16 + n
             to = pl.multiple_of(whole_column + at * rows, rows)
-            scr[pl.ds(to, rows), :] = cache_ref[at].astype(F32)
+            scr[pl.ds(to, rows), :] = cache_ref[slot, at].astype(F32)
         return carry
 
     lax.fori_loop(0, tiles // 16, unpack, 0)
@@ -331,15 +330,15 @@
     return view.transpose(*range(count), count + 1, count, count + 2)
 
 
-def prepare(facts, cache, noisy, latents, channels):
-    tiles, rows, lanes = cache.shape
+def prepare(span_index, facts, cache, noisy, latents, channels):
+    _, tiles, rows, lanes = cache.shape
     cols = tiles * lanes // channels // 2
     frames, chunks, halves = noisy.shape[:3]
     tokens = chunks * frames * halves
     halo = 2 * cols + tokens
     return pl.pallas_call(
         prepare_kernel,
-        in_specs=[whole()] * 4,
+        in_specs=[smem()] + [whole()] * 4,
         out_specs=[whole()] * 4,
         out_shape=[
             jax.ShapeDtypeStruct((4, rows, cols, channels), BF),
@@ -356,7 +355,7 @@
             flops=cache.size, bytes_accessed=6 * cache.size, transcendentals=0
         ),
         name="prepare",
-    )(facts, cache, noisy, latents)
+    )(span_index, facts, cache, noisy, latents)
 
 
 def shift_down(array):
@@ -372,35 +371,157 @@
     return jnp.where(rows == count - 1, 0.0, moved_rows)
 
 
-def cached_sum(line, rows, weight):
+def tap_sum(line, rows, steps, weight):
     lines = []
     for b in range(2):
         for r in rows:
             lines.append(
                 jnp.concatenate(
-                    [line(b + w, r + h - 1) for h in range(3) for w in range(3)], axis=1
+                    [line(b + w, r + h - 1) for h in steps for w in range(3)], axis=1
                 )
             )
     total = dot_last(jnp.concatenate(lines, axis=0), weight)
     half = total.shape[0] // 2
-    return jnp.concatenate([total[:half], total[half:]], axis=1).astype(BF)
-
-
-def slices(weight_hbm, weight_ref, sems, count):
+    return jnp.concatenate([total[:half], total[half:]], axis=1)
+
+
+def middle_kernel(own_ref, weight_hbm, out_ref, rim_ref, weight_ref, sems):
+    rows = own_ref.shape[1]
     depth = weight_ref.shape[2]
-    copies = []
-    for t in range(count):
-        source = weight_hbm.at[:, pl.ds(t * depth, depth)]
-        copies.append(pltpu.make_async_copy(source, weight_ref.at[t], sems.at[t]))
-    return copies
-
-
-def mix_third(weight_ref, out_ref, t):
-    channels = weight_ref.shape[2] // 9
+    third = depth // 3
+    head = lax.axis_index("head")
+    copies = [
+        pltpu.make_async_copy(
+            weight_hbm.at[:, pl.ds(t * depth, depth)], weight_ref.at[t], sems.at[t]
+        )
+        for t in range(2)
+    ]
+    for copy in copies:
+        copy.start()
+
+    def line(n, r):
+        return own_ref[n, r]
+
+    def contribute(f, t):
+        weight = weight_ref[t]
+        inner = tap_sum(line, range(1, rows - 1), range(3), weight).astype(BF)
+        out_ref[f] = inner.reshape(out_ref.shape[1:])
+        rim_ref[f, 0] = tap_sum(line, (0,), (1, 2), weight[:, third:])
+        rim_ref[f, 1] = tap_sum(line, (rows - 1,), (0, 1), weight[:, : 2 * third])
+
+    copies[0].wait()
+    contribute(head, 0)
+    copies[1].wait()
+
+    @pl.when(head == 0)
+    def _():
+        out_ref[1] = jnp.zeros(out_ref.shape[1:], BF)
+
+    @pl.when(head != 0)
+    def _():
+        contribute(0, 1)
+
+
+def middles(own, weight):
+    _, rows, cols, channels = own.shape
+    out, height = weight.shape
+    return pl.pallas_call(
+        middle_kernel,
+        in_specs=[whole(), far_spec()],
+        out_specs=[whole(), whole()],
+        out_shape=[
+            jax.ShapeDtypeStruct((2, rows - 2, cols, 2 * out), BF),
+            jax.ShapeDtypeStruct((2, 2, cols, 2 * out), F32),
+        ],
+        scratch_shapes=[
+            pltpu.VMEM((2, out, height // 3), BF),
+            pltpu.SemaphoreType.DMA((2,)),
+        ],
+        compiler_params=params(),
+        cost_estimate=pl.CostEstimate(
+            flops=2 * 2 * 2 * 3 * cols * 9 * channels * out,
+            bytes_accessed=2 * (own.size + weight.size),
+            transcendentals=0,
+        ),
+        name="middle",
+    )(own, far(weight))
+
+
+def edge_kernel(rim_ref, above_ref, below_ref, weight_hbm, out_ref, var, weight_ref, sems):
+    _, _, cols, channels = var.shape
+    depth = weight_ref.shape[3]
+    head = lax.axis_index("head")
+    copies = [
+        [
+            pltpu.make_async_copy(
+                weight_hbm.at[:, pl.ds((t * 3 + 2 * n) * depth, depth)],
+                weight_ref.at[t, n],
+                sems.at[t * 2 + n],
+            )
+            for n in range(2)
+        ]
+        for t in range(2)
+    ]
+    for pair in copies:
+        for copy in pair:
+            copy.start()
+
+    for n, far_rim in enumerate((above_ref, below_ref)):
+        even, odd = far_rim[:cols], far_rim[cols : 2 * cols]
+        var[n, 0] = shift_down(odd.astype(F32)).astype(BF)
+        var[n, 1] = even
+        var[n, 2] = odd
+        var[n, 3] = shift_up(even.astype(F32)).astype(BF)
+
+    def contribute(f, t):
+        for n in range(2):
+            late = tap_sum(lambda v, r: var[n, v], (0,), (0,), weight_ref[t, n])
+            out_ref[f, n] = (rim_ref[f, n] + late).astype(BF)
+
+    for copy in copies[0]:
+        copy.wait()
+    contribute(head, 0)
+    for copy in copies[1]:
+        copy.wait()
+
+    @pl.when(head == 0)
+    def _():
+        out_ref[1] = jnp.zeros(out_ref.shape[1:], BF)
+
+    @pl.when(head != 0)
+    def _():
+        contribute(0, 1)
+
+
+def edges(rim, above, below, weight, channels):
+    _, _, cols, width = rim.shape
+    out, height = weight.shape
+    return pl.pallas_call(
+        edge_kernel,
+        in_specs=[whole(), whole(), whole(), far_spec()],
+        out_specs=whole(),
+        out_shape=jax.ShapeDtypeStruct(rim.shape, BF),
+        scratch_shapes=[
+            pltpu.VMEM((2, 4, cols, channels), BF),
+            pltpu.VMEM((2, 2, out, height // 9), BF),
+            pltpu.SemaphoreType.DMA((4,)),
+        ],
+        compiler_params=params(),
+        cost_estimate=pl.CostEstimate(
+            flops=2 * 2 * 2 * 2 * cols * 3 * channels * out,
+            bytes_accessed=2 * (above.size + weight.size),
+            transcendentals=0,
+        ),
+        name="edge",
+    )(rim, above, below, far(weight))
+
+
+def mix_kernel(weight_ref, out_ref):
+    channels = weight_ref.shape[1] // 9
 
     def tap(h, w):
         start = (h * 3 + w) * channels
-        return weight_ref[t, :, start : start + channels].astype(F32)
+        return weight_ref[:, start : start + channels].astype(F32)
 
     lines = {}
     for w in range(3):
@@ -416,135 +537,25 @@
             for b in range(2):
                 for v in range(2):
                     start = (u * 2 + v) * channels
-                    out_ref[t, a * 2 + b, :, start : start + channels] = mixed[b][v].astype(BF)
-
-
-def mix_kernel(own_ref, weight_hbm, mixed_hbm, middle_ref, weight_ref, mixed_ref, sems, out_sems):
-    rows = own_ref.shape[1]
-    head = lax.axis_index("head")
-    inner = range(1, rows - 1)
-    copies = slices(weight_hbm, weight_ref, sems, 3)
-    for copy in copies:
-        copy.start()
-
-    def line(n, r):
-        return own_ref[n, r]
-
-    outs = [pltpu.make_async_copy(mixed_ref.at[t], mixed_hbm.at[t], out_sems.at[t]) for t in range(3)]
-    shape = middle_ref.shape[1:]
-    for t in range(3):
-        copies[t].wait()
-        mix_third(weight_ref, mixed_ref, t)
-        outs[t].start()
-        if t == 0:
-
-            @pl.when(head == 0)
-            def _():
-                middle_ref[0] = cached_sum(line, inner, weight_ref[0]).reshape(shape)
-                middle_ref[1] = jnp.zeros(shape, BF)
-
-            @pl.when(head != 0)
-            def _():
-                middle_ref[1] = cached_sum(line, inner, weight_ref[0]).reshape(shape)
-
-        if t == 1:
-
-            @pl.when(head != 0)
-            def _():
-                middle_ref[0] = cached_sum(line, inner, weight_ref[1]).reshape(shape)
-
-    for copy in outs:
-        copy.wait()
-
-
-def mix(own, weight):
-    _, rows, cols, channels = own.shape
+                    out_ref[0, a * 2 + b, :, start : start + channels] = mixed[b][v].astype(BF)
+
+
+def mix(weight):
     out, height = weight.shape
     third = height // 3
     shape = (3, 4, out, third // 9 * 4)
     return pl.pallas_call(
         mix_kernel,
-        in_specs=[whole(), far_spec()],
-        out_specs=[far_spec(), whole()],
-        out_shape=[
-            pltpu.HBM(shape, BF),
-            jax.ShapeDtypeStruct((2, rows - 2, cols, 2 * out), BF),
-        ],
-        scratch_shapes=[
-            pltpu.VMEM((3, out, third), BF),
-            pltpu.VMEM(shape, BF),
-            pltpu.SemaphoreType.DMA((3,)),
-            pltpu.SemaphoreType.DMA((3,)),
-        ],
-        compiler_params=params(0, 24),
+        grid=(3,),
+        in_specs=[pl.BlockSpec((out, third), lambda t: (0, t))],
+        out_specs=pl.BlockSpec((1,) + shape[1:], lambda t: (t, 0, 0, 0)),
+        out_shape=jax.ShapeDtypeStruct(shape, BF),
+        compiler_params=params(1),
         cost_estimate=pl.CostEstimate(
-            flops=2 * 2 * 2 * 2 * cols * third * out,
-            bytes_accessed=6 * weight.size,
-            transcendentals=0,
+            flops=4 * weight.size, bytes_accessed=6 * weight.size, transcendentals=0
         ),
         name="mix",
-    )(own, far(weight))
-
-
-def edge_kernel(own_ref, above_ref, below_ref, weight_hbm, out_ref, var, weight_ref, sems):
-    _, rows, cols, channels = own_ref.shape
-    head = lax.axis_index("head")
-    first_copy, second_copy = slices(weight_hbm, weight_ref, sems, 2)
-    first_copy.start()
-
-    @pl.when(head != 0)
-    def _():
-        second_copy.start()
-
-    for n, rim in enumerate((above_ref, below_ref)):
-        even, odd = rim[:cols], rim[cols : 2 * cols]
-        var[n, 0] = shift_down(odd.astype(F32)).astype(BF)
-        var[n, 1] = even
-        var[n, 2] = odd
-        var[n, 3] = shift_up(even.astype(F32)).astype(BF)
-
-    def line(n, r):
-        if r < 0:
-            return var[0, n]
-        return var[1, n] if r == rows else own_ref[n, r]
-
-    outer = (0, rows - 1)
-    shape = out_ref.shape[1:]
-    first_copy.wait()
-
-    @pl.when(head == 0)
-    def _():
-        out_ref[0] = cached_sum(line, outer, weight_ref[0]).reshape(shape)
-        out_ref[1] = jnp.zeros(shape, BF)
-
-    @pl.when(head != 0)
-    def _():
-        out_ref[1] = cached_sum(line, outer, weight_ref[0]).reshape(shape)
-        second_copy.wait()
-        out_ref[0] = cached_sum(line, outer, weight_ref[1]).reshape(shape)
-
-
-def edges(own, above, below, weight):
-    _, rows, cols, channels = own.shape
-    out, height = weight.shape
-    return pl.pallas_call(
-        edge_kernel,
-        in_specs=[whole(), whole(), whole(), far_spec()],
-        out_specs=whole(),
-        out_shape=jax.ShapeDtypeStruct((2, 2, cols, 2 * out), BF),
-        scratch_shapes=[
-            pltpu.VMEM((2, 4, cols, channels), BF),
-            pltpu.VMEM((2, out, height // 3), BF),
-            pltpu.SemaphoreType.DMA((2,)),
-        ],
-        compiler_params=params(),
-        cost_estimate=pl.CostEstimate(
-            flops=2 * 2 * 2 * 2 * cols * 9 * channels * out,
-            bytes_accessed=2 * (own.size + weight.size),
-            transcendentals=0,
-        ),
-        name="edge",
-    )(own, above, below, far(weight))
+    )(weight)
 
 
 def spread(source_ref, var):
@@ -611,7 +622,7 @@
             transcendentals=0,
         ),
         name="own_part",
-    )(activated, far(mixed), far(mixed))
+    )(activated, mixed, mixed)
 
 
 def prior_kernel(source_ref, middle_ref, edge_ref, own_ref, old_ref, new_ref, out_ref, var, total_ref, scr):
@@ -659,14 +670,8 @@
                         :, q * 128 : (q + 1) * 128
                     ]
 
-            def pack(i, carry):
-                for n in range(16):
-                    at = i * 16 + n
-                    tile = scr[pl.ds(pl.multiple_of(at * fine, fine), fine), :]
-                    out_ref[f, at] = tile.astype(BF)
-                return carry
-
-            lax.fori_loop(0, out_ref.shape[1] // 16, pack, 0)
+            for at in range(out_ref.shape[1]):
+                out_ref[f, at] = scr[at * fine : (at + 1) * fine, :].astype(BF)
 
 
 def prior_part(received, middle, edge, own_sum, mixed):
@@ -700,18 +705,20 @@
             transcendentals=0,
         ),
         name="prior_part",
-    )(received, middle, edge, own_sum, far(mixed), far(mixed))
+    )(received, middle, edge, own_sum, mixed, mixed)
     return out.transpose(0, 2, 1, 3).reshape(frames, fine, tiles * 128)
 
 
-def latent_kernel(facts_ref, parts_ref, own_ref, above_ref, below_ref, clean_ref, send_ref, out_ref, scr):
+def latent_kernel(step_ref, parts_ref, own_ref, above_ref, below_ref, clean_ref, send_ref, out_ref, scr):
     sources, three, unit, lanes = parts_ref.shape
     cols = own_ref.shape[0]
     frames, chunks, halves = out_ref.shape[:3]
     groups = frames * halves
     group = lanes // groups
     features = sources * 128
-    level = facts_ref[0:1, :]
+    fraction = 1.0 - step_ref[0].astype(F32) / NSTEPS
+    fraction = jnp.full((1, lanes), fraction, F32)
+    level = SHIFT_FACTOR * fraction / (1.0 + (SHIFT_FACTOR - 1.0) * fraction)
     total = parts_ref[0].astype(F32)
     for source in range(1, sources):
         total = total + parts_ref[source].astype(F32)
@@ -750,13 +757,13 @@
             out_ref[f, i] = scr[at : at + halves, :].astype(BF)
 
 
-def latent(facts, parts, own, above, below, frames, halves, chunks):
+def latent(step_index, parts, own, above, below, frames, halves, chunks):
     sources, three, unit, lanes = parts.shape
     cols = own.shape[0]
     shape = jax.ShapeDtypeStruct((three, cols, lanes), BF)
     return pl.pallas_call(
         latent_kernel,
-        in_specs=[whole()] * 5,
+        in_specs=[smem()] + [whole()] * 4,
         out_specs=[whole(), whole(), whole()],
         out_shape=[shape, shape, jax.ShapeDtypeStruct((frames, chunks, halves, 128), BF)],
         scratch_shapes=[pltpu.VMEM((cols + frames * chunks * halves, lanes), F32)],
@@ -765,7 +772,7 @@
             flops=2 * parts.size, bytes_accessed=2 * parts.size, transcendentals=0
         ),
         name="latent",
-    )(facts, parts, own, above, below)
+    )(step_index, parts, own, above, below)
 
 
 def first_kernel(
@@ -945,26 +952,28 @@
         values,
         final_gain,
         out_weight,
-        span_index * NSTEPS + step_index,
         cache_flags,
         feature_cache,
         noisy_latent,
         latent_cache,
     )
     parts = lax.all_to_all(sent, "seq", 0, 0, tiled=True)
-    own_frame, up, down, small = prepare(facts, cache, noisy, latents, channels)
+    own_frame, up, down, small = prepare(
+        span_index, facts, cache, noisy, latents, channels
+    )
     above = lax.ppermute(down, "seq", [(i, i + 1) for i in range(slabs - 1)])
     below = lax.ppermute(up, "seq", [(i + 1, i) for i in range(slabs - 1)])
-    mixed, middle = mix(own_frame, second)
+    middle, rim = middles(own_frame, second)
     above, below, middle = lax.optimization_barrier((above, below, middle))
 
-    clean, send, out = latent(facts, parts, small, above, below, frames, halves, width // 128)
-    edge = edges(own_frame, above, below, second)
+    clean, send, out = latent(step_index, parts, small, above, below, frames, halves, width // 128)
+    edge = edges(rim, above, below, second, channels)
     received = swapped(send, "head")
     activated, send = first(
         clean, received, small, above, below, first_weight, first_gain.reshape(-1, 128), middle, edge
     )
     arrived = swapped(send, "head")
+    mixed = mix(second)
     own_sum = own_part(activated, mixed)
     decoded = prior_part(arrived, middle, edge, own_sum, mixed)
     return (out.transpose(0, 2, 1, 3).reshape(frames, halves, width), decoded)

time: 45.2 us -> 39.9 us (0.88)
  Pallas kernels: 28.4 us -> 22.1 us
  waiting for transfers between devices: 1.48 us -> 2.9 us
    pallas_call x1, Pallas kernels: 6.04 us -> 3.89 us  [prior_part(): pl.pallas_call(prior_kernel, grid=(parities,), in_specs=[pl.BlockSpec(rec...]
    pallas_call x1, Pallas kernels: 4.63 us -> 2.68 us  [own_part(): pl.pallas_call(own_kernel, grid=(parities,), in_specs=[pl.BlockSpec(activ...]
    pallas_call x1, Pallas kernels: 4.17 us -> 2.28 us  [edges(): pl.pallas_call(edge_kernel, in_specs=[whole(), whole(), whole(), far_spec...]
    ppermute x1, waiting for transfers between devices: 1.47 us -> 2.89 us  [body(): below = lax.ppermute(up, 'seq', [(i + 1, i) for i in range(slabs - 1)])]
    pallas_call x4 -> x5, Pallas kernels: 12.3 us -> 12 us  [the longest x1 4.2 us: attention(): pl.pallas_call(kernel, in_specs=[far_spec()] * 9, out_specs=[whole()] * l...]
  transfers between devices with their start and end apart: 5 -> 5, of which waited for: 1 -> 1; matrix products, arithmetic and copies ran while one was open for 0% -> 0% of each run, Pallas kernels for 35% -> 29%
where the time goes in v4:
time: 39.9 us; the launch traced here: 39.6 us
  Pallas kernels  22.1 us (55%)
  starting transfers between devices  12.5 us (31%)
  waiting for transfers between devices  2.9 us (7%)
  between operations  2.08 us (5%)
    all_to_all x1, starting transfers between devices, body(): parts = lax.all_to_all(sent, 'seq', 0, 0, tiled=True)  5.62 us
    pallas_call x1, Pallas kernels, attention(): pl.pallas_call(kernel, in_specs=[far_spec()] * 9, out_specs=[whole()] * l...  4.2 us
    pallas_call x1, Pallas kernels, middles(): pl.pallas_call(middle_kernel, in_specs=[whole(), far_spec()], out_specs=[...  3.94 us
    pallas_call x1, Pallas kernels, prior_part(): pl.pallas_call(prior_kernel, grid=(parities,), in_specs=[pl.BlockSpec(rec...  3.89 us
    ppermute x1, starting transfers between devices, body(): above = lax.ppermute(down, 'seq', [(i, i + 1) for i in range(slabs - 1)])  3.09 us
    ppermute x1, starting transfers between devices, body(): below = lax.ppermute(up, 'seq', [(i + 1, i) for i in range(slabs - 1)])  3.09 us
    ppermute x1, waiting for transfers between devices, body(): below = lax.ppermute(up, 'seq', [(i + 1, i) for i in range(slabs - 1)])  2.89 us
    pallas_call x1, Pallas kernels, own_part(): pl.pallas_call(own_kernel, grid=(parities,), in_specs=[pl.BlockSpec(activ...  2.68 us
  transfers between devices with their start and end apart: 5, of which 1 were waited for; matrix products, arithmetic and copies ran while one was open for 0% of the time, Pallas kernels for 29%

profile of v4, /device:TPU:17, one launch (start us, length us, event | category | flops | bytes accessed | tf_op | source)
XLA Modules:
  0.0 39.6 jit_solution(9235576393124180461)
XLA Ops:
  0.6 4.2 %attention.1 = (bf16[8,3,48,128]{3,2,1,0:T(8,128)(2,1)}, f32[8,128]{1,0:T(8,128)S(1)}, bf16[2,480,4,128]{3,2,1,0:T(4,128)(2,1)S(1)}, bf16[2,10,2,128]{3,2,1,0:T(2,128)(2,1)S(1)}, bf16[2,10,2,128]{3,2,1,0:T(2,128)(2,1)S(1)}) custom-call(s32[2,2,16]{2,1,0:T(2,128)} %refs_0_.1, bf16[2,320,128]{2,1,0:T(8,128)(2,1)} %bitcast.30, bf16[1280,128]{1,0:T(8,128)(2,1)} %bitcast.28, ...), custom_call_target="tpu_custom_call" | custom-call | flops 629145600 | bytes 819200 | tf_op jit(solution)/shard_map/attention/pallas_call | solution.py:209
  4.8 5.6 %all-to-all-start = ((bf16[8,3,48,128]{3,2,1,0:T(8,128)(2,1)}), bf16[8,3,48,128]{3,2,1,0:T(8,128)(2,1)S(1)}, u32[]{:S(2)}, u32[]{:S(2)}) async-start(bf16[8,3,48,128]{3,2,1,0:T(8,128)(2,1)} %get-tuple-element.21), calls=%async_computation | async-start | bytes 589824 | tf_op jit(solution)/shard_map/all_to_all | solution.py:960
  11.1 0.7 %prepare.1 = (bf16[4,4,80,384]{3,2,1,0:T(8,128)(2,1)S(1)}, bf16[200,384]{1,0:T(8,128)(2,1)S(1)}, bf16[200,384]{1,0:T(8,128)(2,1)S(1)}, bf16[40,256]{1,0:T(8,128)(2,1)S(1)}) custom-call(s32[1]{0:T(128)S(6)} %copy.17.span_ref, f32[8,128]{1,0:T(8,128)S(1)} %get-tuple-element.22.facts_ref, bf16[2,480,4,128]{3,2,1,0:T(4,128)(2,1)S(1)} %get-tuple-element.23.cache_ref, ...), custom_call_target="tpu_custom_call" | custom-call | flops 491520 | bytes 2949120 | tf_op jit(solution)/shard_map/prepare/pallas_call | solution.py:339
  11.8 3.1 %collective-permute-start = (bf16[200,384]{1,0:T(8,128)(2,1)S(1)}, bf16[200,384]{1,0:T(8,128)(2,1)S(1)}, u32[]{:S(2)}, u32[]{:S(2)}) collective-permute-start(bf16[200,384]{1,0:T(8,128)(2,1)S(1)} %get-tuple-element.27), channel_id=1, source_target_pairs={{0,2},{2,4},{4,6},{6,8},{8,10},{10,12},{12,14},{1,3},{3,5},{5,7},{... | collective-permute-start | bytes 460808 | tf_op jit(solution)/shard_map/ppermute | solution.py:964
  14.9 3.1 %collective-permute-start.1 = (bf16[200,384]{1,0:T(8,128)(2,1)S(1)}, bf16[200,384]{1,0:T(8,128)(2,1)S(1)}, u32[]{:S(2)}, u32[]{:S(2)}) collective-permute-start(bf16[200,384]{1,0:T(8,128)(2,1)S(1)} %get-tuple-element.28), channel_id=1, source_target_pairs={{2,0},{4,2},{6,4},{8,6},{10,8},{12,10},{14,12},{3,1},{5,3},{7,5},{... | collective-permute-start | bytes 460808 | tf_op jit(solution)/shard_map/ppermute | solution.py:965
  18.7 3.9 %middle.1 = (bf16[2,2,80,384]{3,2,1,0:T(8,128)(2,1)S(1)}, f32[2,2,80,384]{3,2,1,0:T(8,128)S(1)}) custom-call(bf16[4,4,80,384]{3,2,1,0:T(8,128)(2,1)S(1)} %get-tuple-element.29.own_ref, bf16[192,10368]{1,0:T(8,128)(2,1)} %bitcast.22), custom_call_target="tpu_custom_call" | custom-call | flops 1274019840 | bytes 4964352 | tf_op jit(solution)/shard_map/middle/pallas_call | solution.py:428
  22.6 0.0 copy-start.1
  22.6 0.0 copy-start.2
  22.7 0.0 collective-permute-done.above_ref
  22.7 2.9 %collective-permute-done.1.below_ref = bf16[200,384]{1,0:T(8,128)(2,1)S(1)} collective-permute-done((bf16[200,384]{1,0:T(8,128)(2,1)S(1)}, bf16[200,384]{1,0:T(8,128)(2,1)S(1)}, u32[]{:S(2)}, u32[]{:S(2)}) %collective-permute-start.1) | collective-permute-done | bytes 153632 | tf_op jit(solution)/shard_map/ppermute | solution.py:965
  25.6 0.0 all-to-all-done.parts_ref
  25.6 0.0 copy-start
  25.6 1.2 %latent.1 = (bf16[3,40,128]{2,1,0:T(8,128)(2,1)S(1)}, bf16[3,40,128]{2,1,0:T(8,128)(2,1)S(1)}, bf16[2,10,2,128]{3,2,1,0:T(2,128)(2,1)}) custom-call(s32[1]{0:T(128)S(6)} %copy.16.step_ref, bf16[8,3,48,128]{3,2,1,0:T(8,128)(2,1)S(1)} %all-to-all-done.parts_ref, bf16[40,256]{1,0:T(8,128)(2,1)S(1)} %get-tuple-element.26.own_ref, ...), custom_call_target="tpu_custom_call" | custom-call | flops 294912 | bytes 294912 | tf_op jit(solution)/shard_map/latent/pallas_call | solution.py:764
  26.8 0.7 %collective-permute-start.2 = (bf16[3,40,128]{2,1,0:T(8,128)(2,1)S(1)}, bf16[3,40,128]{2,1,0:T(8,128)(2,1)S(1)}, u32[]{:S(2)}, u32[]{:S(2)}) collective-permute-start(bf16[3,40,128]{2,1,0:T(8,128)(2,1)S(1)} %get-tuple-element.35), channel_id=1, source_target_pairs={{0,1},{1,0},{2,3},{3,2},{4,5},{5,4},{6,7},{7,6},{8,9},{9,8},{10,11... | collective-permute-start | bytes 92168 | tf_op jit(solution)/shard_map/ppermute | solution.py:925
  27.4 2.3 %edge.1.edge_ref = bf16[2,2,80,384]{3,2,1,0:T(8,128)(2,1)S(1)} custom-call(f32[2,2,80,384]{3,2,1,0:T(8,128)S(1)} %get-tuple-element.37.rim_ref, bf16[200,384]{1,0:T(8,128)(2,1)S(1)} %collective-permute-done.above_ref, bf16[200,384]{1,0:T(8,128)(2,1)S(1)} %collective-permute-done.1.below_ref, bf16[192,10368]{1,0:T(8,128)(2,1)} %bitcast.23), custom_call_target="tpu_custom_call" | custom-call | flops 283115520 | bytes 4134912 | tf_op jit(solution)/shard_map/edge/pallas_call | solution.py:499
  29.7 0.0 collective-permute-done.2.received_ref
  29.8 0.0 copy-done.1
  29.8 0.0 copy-done.2
  29.8 1.3 %first.1 = (bf16[2,4,80,384]{3,2,1,0:T(8,128)(2,1)S(1)}, bf16[2,4,80,384]{3,2,1,0:T(8,128)(2,1)S(1)}) custom-call(bf16[3,40,128]{2,1,0:T(8,128)(2,1)S(1)} %get-tuple-element.34.clean_ref, bf16[3,40,128]{2,1,0:T(8,128)(2,1)S(1)} %collective-permute-done.2.received_ref, bf16[40,256]{1,0:T(8,128)(2,1)S(1)} %get-tuple-element.26.own_ref, ...), custom_call_target="tpu_custom_call" | custom-call | flops 212336640 | bytes 983040 | tf_op jit(solution)/shard_map/first/pallas_call | solution.py:906
  31.1 0.1 collective-permute-start.3
  31.1 0.0 copy-done
  31.2 1.9 %mix.1.old_ref.new_ref = bf16[3,4,192,1536]{3,2,1,0:T(8,128)(2,1)S(1)} custom-call(bf16[192,10368]{1,0:T(8,128)(2,1)S(1)} %bitcast.24), custom_call_target="tpu_custom_call" | custom-call | flops 7962624 | bytes 11943936 | tf_op jit(solution)/shard_map/mix/pallas_call | solution.py:547
  33.0 2.7 %own_part.1.own_ref = f32[4,2,2,80,192]{4,3,2,1,0:T(8,128)S(1)} custom-call(bf16[2,4,80,384]{3,2,1,0:T(8,128)(2,1)S(1)} %get-tuple-element.39.source_ref, bf16[3,4,192,1536]{3,2,1,0:T(8,128)(2,1)S(1)} %mix.1.old_ref.new_ref, bf16[3,4,192,1536]{3,2,1,0:T(8,128)(2,1)S(1)} %mix.1.old_ref.new_ref), custom_call_target="tpu_custom_call" | custom-call | flops 1132462080 | bytes 5210112 | tf_op jit(solution)/shard_map/own_part/pallas_call | solution.py:607
  35.7 0.0 collective-permute-done.3.source_ref
  35.7 3.9 %prior_part.1 = bf16[2,240,4,128]{3,2,1,0:T(4,128)(2,1)} custom-call(bf16[2,4,80,384]{3,2,1,0:T(8,128)(2,1)S(1)} %collective-permute-done.3.source_ref, bf16[2,2,80,384]{3,2,1,0:T(8,128)(2,1)S(1)} %get-tuple-element.36.middle_ref, bf16[2,2,80,384]{3,2,1,0:T(8,128)(2,1)S(1)} %edge.1.edge_ref, f32[4,2,2,80,192]{4,3,2,1,0:T(8,128)S(1)} %own_part.1.own_ref, ...), custom_call_target="tpu_custom_call" | custom-call | flops 1132462080 | bytes 5210112 | tf_op jit(solution)/shard_map/prior_part/pallas_call | solution.py:683
Async XLA Ops:
  4.8 20.7 %all-to-all-start = ((bf16[8,3,48,128]{3,2,1,0:T(8,128)(2,1)}), bf16[8,3,48,128]{3,2,1,0:T(8,128)(2,1)S(1)}, u32[]{:S(2)}, u32[]{:S(2)}) async-start(bf16[8,3,48,128]{3,2,1,0:T(8,128)(2,1)} %get-tuple-element.21), calls=%async_computation | async-start | bytes 589824 | tf_op jit(solution)/shard_map/all_to_all | solution.py:960
  11.8 10.8 %collective-permute-start = (bf16[200,384]{1,0:T(8,128)(2,1)S(1)}, bf16[200,384]{1,0:T(8,128)(2,1)S(1)}, u32[]{:S(2)}, u32[]{:S(2)}) collective-permute-start(bf16[200,384]{1,0:T(8,128)(2,1)S(1)} %get-tuple-element.27), channel_id=1, source_target_pairs={{0,2},{2,4},{4,6},{6,8},{8,10},{10,12},{12,14},{1,3},{3,5},{5,7},{... | collective-permute-start | bytes 460808 | tf_op jit(solution)/shard_map/ppermute | solution.py:964
  14.9 10.6 %collective-permute-start.1 = (bf16[200,384]{1,0:T(8,128)(2,1)S(1)}, bf16[200,384]{1,0:T(8,128)(2,1)S(1)}, u32[]{:S(2)}, u32[]{:S(2)}) collective-permute-start(bf16[200,384]{1,0:T(8,128)(2,1)S(1)} %get-tuple-element.28), channel_id=1, source_target_pairs={{2,0},{4,2},{6,4},{8,6},{10,8},{12,10},{14,12},{3,1},{5,3},{7,5},{... | collective-permute-start | bytes 460808 | tf_op jit(solution)/shard_map/ppermute | solution.py:965
  22.6 7.1 %copy-start.1 = (bf16[432,384]{1,0:T(8,128)(2,1)S(1)}, bf16[432,384]{1,0:T(8,128)(2,1)}, u32[]{:S(2)}) copy-start(bf16[432,384]{1,0:T(8,128)(2,1)} %weight_ref.1) | copy-start | bytes 995332
  22.6 7.1 %copy-start.2 = (bf16[384]{0:T(512)(128)(2,1)S(1)}, bf16[384]{0:T(512)(128)(2,1)}, u32[]{:S(2)}) copy-start(bf16[384]{0:T(512)(128)(2,1)} %param.26) | copy-start | bytes 2308
  25.6 5.6 %copy-start = (bf16[10368,192]{0,1:T(8,128)(2,1)S(1)}, bf16[10368,192]{0,1:T(8,128)(2,1)}, u32[]{:S(2)}) copy-start(bf16[10368,192]{0,1:T(8,128)(2,1)} %param.27) | copy-start | bytes 11943940
  26.8 2.9 %collective-permute-start.2 = (bf16[3,40,128]{2,1,0:T(8,128)(2,1)S(1)}, bf16[3,40,128]{2,1,0:T(8,128)(2,1)S(1)}, u32[]{:S(2)}, u32[]{:S(2)}) collective-permute-start(bf16[3,40,128]{2,1,0:T(8,128)(2,1)S(1)} %get-tuple-element.35), channel_id=1, source_target_pairs={{0,1},{1,0},{2,3},{3,2},{4,5},{5,4},{6,7},{7,6},{8,9},{9,8},{10,11... | collective-permute-start | bytes 92168 | tf_op jit(solution)/shard_map/ppermute | solution.py:925
  31.1 4.7 %collective-permute-start.3 = (bf16[2,4,80,384]{3,2,1,0:T(8,128)(2,1)S(1)}, bf16[2,4,80,384]{3,2,1,0:T(8,128)(2,1)S(1)}, u32[]{:S(2)}, u32[]{:S(2)}) collective-permute-start(bf16[2,4,80,384]{3,2,1,0:T(8,128)(2,1)S(1)} %get-tuple-element.38), channel_id=1, source_target_pairs={{0,1},{1,0},{2,3},{3,2},{4,5},{5,4},{6,7},{7,6},{8,9},{9,8},{10,11... | collective-permute-start | bytes 1474568 | tf_op jit(solution)/shard_map/ppermute | solution.py:925

commit v5 on v4

--- a/solution.py
+++ b/solution.py
@@ -92,7 +92,10 @@
     edge = jnp.zeros(out_ref.shape[2:], BF)
     out_ref[0, 0] = edge
     out_ref[rows_total - 1, 2] = edge
-    for copy in key_copies + value_copies:
+    for copy in key_copies:
+        copy.wait()
+    first_scores = [dot_last(q_ref[f, : rows * cols, :], k_ref[...]) for f in range(frames)]
+    for copy in value_copies:
         copy.wait()
 
     scale = 1.4426950408889634 / head_size**0.5
@@ -113,7 +116,10 @@
             at = step * (rows * cols)
             if not isinstance(step, int):
                 at = pl.multiple_of(at, 16)
-            scores = dot_last(q_ref[f, pl.ds(at, rows * cols), :], keys)
+            if isinstance(step, int) and step == 0:
+                scores = first_scores[f]
+            else:
+                scores = dot_last(q_ref[f, pl.ds(at, rows * cols), :], keys)
             row_max = jnp.max(scores, axis=1, keepdims=True)
             weights = jnp.exp2((scores - row_max) * scale).astype(BF)
             blended = dot(weights, values)
@@ -150,8 +156,9 @@
                     out_ref[jnp.maximum(row - 1, 0), 2] = unit
 
     steps = rows_total // rows
+    block(0)
     if steps <= 2:
-        for step in range(steps):
+        for step in range(1, steps):
             block(step)
     else:
 
@@ -159,7 +166,7 @@
             block(step)
             return carry
 
-        lax.fori_loop(0, steps, one, 0)
+        lax.fori_loop(1, steps, one, 0)
 
     for copy in later:
         copy.wait()
@@ -220,7 +227,7 @@
             pltpu.VMEM(weight.shape, BF),
             pltpu.SemaphoreType.DMA((9,)),
         ],
-        compiler_params=params(0, 16),
+        compiler_params=params(0, 40),
         cost_estimate=pl.CostEstimate(
             flops=6 * count * k.shape[0] * head_size,
             bytes_accessed=2 * (q.size + k.size + v.size),
@@ -447,25 +454,22 @@
     )(own, far(weight))
 
 
-def edge_kernel(rim_ref, above_ref, below_ref, weight_hbm, out_ref, var, weight_ref, sems):
+def edge_slices(weight_hbm, slices_ref, sems):
+    depth = slices_ref.shape[3]
+    return [
+        pltpu.make_async_copy(
+            weight_hbm.at[:, pl.ds((t * 3 + 2 * n) * depth, depth)],
+            slices_ref.at[t, n],
+            sems.at[t * 2 + n],
+        )
+        for t in range(2)
+        for n in range(2)
+    ]
+
+
+def edge_kernel(rim_ref, above_ref, below_ref, weight_ref, out_ref, var):
     _, _, cols, channels = var.shape
-    depth = weight_ref.shape[3]
     head = lax.axis_index("head")
-    copies = [
-        [
-            pltpu.make_async_copy(
-                weight_hbm.at[:, pl.ds((t * 3 + 2 * n) * depth, depth)],
-                weight_ref.at[t, n],
-                sems.at[t * 2 + n],
-            )
-            for n in range(2)
-        ]
-        for t in range(2)
-    ]
-    for pair in copies:
-        for copy in pair:
-            copy.start()
-
     for n, far_rim in enumerate((above_ref, below_ref)):
         even, odd = far_rim[:cols], far_rim[cols : 2 * cols]
         var[n, 0] = shift_down(odd.astype(F32)).astype(BF)
@@ -478,11 +482,7 @@
             late = tap_sum(lambda v, r: var[n, v], (0,), (0,), weight_ref[t, n])
             out_ref[f, n] = (rim_ref[f, n] + late).astype(BF)
 
-    for copy in copies[0]:
-        copy.wait()
     contribute(head, 0)
-    for copy in copies[1]:
-        copy.wait()
 
     @pl.when(head == 0)
     def _():
@@ -495,17 +495,13 @@
 
 def edges(rim, above, below, weight, channels):
     _, _, cols, width = rim.shape
-    out, height = weight.shape
+    out = weight.shape[2]
     return pl.pallas_call(
         edge_kernel,
-        in_specs=[whole(), whole(), whole(), far_spec()],
+        in_specs=[whole()] * 4,
         out_specs=whole(),
         out_shape=jax.ShapeDtypeStruct(rim.shape, BF),
-        scratch_shapes=[
-            pltpu.VMEM((2, 4, cols, channels), BF),
-            pltpu.VMEM((2, 2, out, height // 9), BF),
-            pltpu.SemaphoreType.DMA((4,)),
-        ],
+        scratch_shapes=[pltpu.VMEM((2, 4, cols, channels), BF)],
         compiler_params=params(),
         cost_estimate=pl.CostEstimate(
             flops=2 * 2 * 2 * 2 * cols * 3 * channels * out,
@@ -513,7 +509,7 @@
             transcendentals=0,
         ),
         name="edge",
-    )(rim, above, below, far(weight))
+    )(rim, above, below, weight)
 
 
 def mix_kernel(weight_ref, out_ref):
@@ -521,7 +517,7 @@
 
     def tap(h, w):
         start = (h * 3 + w) * channels
-        return weight_ref[:, start : start + channels].astype(F32)
+        return weight_ref[:, start : start + channels]
 
     lines = {}
     for w in range(3):
@@ -537,7 +533,7 @@
             for b in range(2):
                 for v in range(2):
                     start = (u * 2 + v) * channels
-                    out_ref[0, a * 2 + b, :, start : start + channels] = mixed[b][v].astype(BF)
+                    out_ref[0, a * 2 + b, :, start : start + channels] = mixed[b][v]
 
 
 def mix(weight):
@@ -653,25 +649,35 @@
     def _():
         fine = 2 * coarse_rows
         pieces = 2 * width // 128
-        keep = jnp.where(head == 0, 1.0, 0.0)
-        for f in range(frames):
-            for row in range(fine):
-                side = (row % 2) * 2
-                sides = [total_ref[side + n, f, row // 2] for n in range(2)]
-                line = jnp.concatenate(sides, axis=1)
-                if row in (0, fine - 1):
-                    mine = edge_ref[f, min(row, 1)]
-                else:
-                    mine = middle_ref[f, row - 1]
-                extra = mine.astype(F32) + source_ref[f, row].astype(F32)
-                line = line + keep * extra
-                for q in range(pieces):
-                    scr[pl.ds(q * fine + row, cols, stride=pieces * fine), :] = line[
-                        :, q * 128 : (q + 1) * 128
-                    ]
-
-            for at in range(out_ref.shape[1]):
-                out_ref[f, at] = scr[at * fine : (at + 1) * fine, :].astype(BF)
+
+        def assemble(extra):
+            for f in range(frames):
+                for row in range(fine):
+                    side = (row % 2) * 2
+                    sides = [total_ref[side + n, f, row // 2] for n in range(2)]
+                    line = jnp.concatenate(sides, axis=1)
+                    if extra:
+                        if row in (0, fine - 1):
+                            mine = edge_ref[f, min(row, 1)]
+                        else:
+                            mine = middle_ref[f, row - 1]
+                        line = line + (mine.astype(F32) + source_ref[f, row].astype(F32))
+                    for q in range(pieces):
+                        at = f * cols * pieces * fine + q * fine + row
+                        scr[pl.ds(at, cols, stride=pieces * fine), :] = line[
+                            :, q * 128 : (q + 1) * 128
+                        ]
+                for at in range(out_ref.shape[1]):
+                    start = (f * out_ref.shape[1] + at) * fine
+                    out_ref[f, at] = scr[start : start + fine, :].astype(BF)
+
+        @pl.when(head == 0)
+        def _():
+            assemble(True)
+
+        @pl.when(head != 0)
+        def _():
+            assemble(False)
 
 
 def prior_part(received, middle, edge, own_sum, mixed):
@@ -696,7 +702,7 @@
         scratch_shapes=[
             pltpu.VMEM((3, frames, coarse, cols, channels), BF),
             pltpu.VMEM(own_sum.shape, F32),
-            pltpu.VMEM((tiles * fine, 128), F32),
+            pltpu.VMEM((frames * tiles * fine, 128), F32),
         ],
         compiler_params=params(1),
         cost_estimate=pl.CostEstimate(
@@ -709,7 +715,12 @@
     return out.transpose(0, 2, 1, 3).reshape(frames, fine, tiles * 128)
 
 
-def latent_kernel(step_ref, parts_ref, own_ref, above_ref, below_ref, clean_ref, send_ref, out_ref, scr):
+def latent_kernel(
+    step_ref, parts_ref, own_ref, above_ref, below_ref, weight_hbm, clean_ref, send_ref, out_ref, slices_ref, scr, sems
+):
+    copies = edge_slices(weight_hbm, slices_ref, sems)
+    for copy in copies:
+        copy.start()
     sources, three, unit, lanes = parts_ref.shape
     cols = own_ref.shape[0]
     frames, chunks, halves = out_ref.shape[:3]
@@ -755,24 +766,34 @@
         for i in range(chunks):
             at = cols + (f * chunks + i) * halves
             out_ref[f, i] = scr[at : at + halves, :].astype(BF)
-
-
-def latent(step_index, parts, own, above, below, frames, halves, chunks):
+    for copy in copies:
+        copy.wait()
+
+
+def latent(step_index, parts, own, above, below, weight, frames, halves, chunks):
     sources, three, unit, lanes = parts.shape
     cols = own.shape[0]
     shape = jax.ShapeDtypeStruct((three, cols, lanes), BF)
     return pl.pallas_call(
         latent_kernel,
-        in_specs=[smem()] + [whole()] * 4,
-        out_specs=[whole(), whole(), whole()],
-        out_shape=[shape, shape, jax.ShapeDtypeStruct((frames, chunks, halves, 128), BF)],
-        scratch_shapes=[pltpu.VMEM((cols + frames * chunks * halves, lanes), F32)],
+        in_specs=[smem()] + [whole()] * 4 + [far_spec()],
+        out_specs=[whole()] * 4,
+        out_shape=[
+            shape,
+            shape,
+            jax.ShapeDtypeStruct((frames, chunks, halves, 128), BF),
+            jax.ShapeDtypeStruct((2, 2, weight.shape[0], weight.shape[1] // 9), BF),
+        ],
+        scratch_shapes=[
+            pltpu.VMEM((cols + frames * chunks * halves, lanes), F32),
+            pltpu.SemaphoreType.DMA((4,)),
+        ],
         compiler_params=params(0, 8),
         cost_estimate=pl.CostEstimate(
             flops=2 * parts.size, bytes_accessed=2 * parts.size, transcendentals=0
         ),
         name="latent",
-    )(step_index, parts, own, above, below)
+    )(step_index, parts, own, above, below, far(weight))
 
 
 def first_kernel(
@@ -966,8 +987,10 @@
     middle, rim = middles(own_frame, second)
     above, below, middle = lax.optimization_barrier((above, below, middle))
 
-    clean, send, out = latent(step_index, parts, small, above, below, frames, halves, width // 128)
-    edge = edges(rim, above, below, second, channels)
+    clean, send, out, slices = latent(
+        step_index, parts, small, above, below, second, frames, halves, width // 128
+    )
+    edge = edges(rim, above, below, slices, channels)
     received = swapped(send, "head")
     activated, send = first(
         clean, received, small, above, below, first_weight, first_gain.reshape(-1, 128), middle, edge

time: 39.9 us -> 38.7 us (0.970)
  Pallas kernels: 22.1 us -> 20.8 us
    pallas_call x1, Pallas kernels: 1.87 us -> 1.09 us  [mix(): pl.pallas_call(mix_kernel, grid=(3,), in_specs=[pl.BlockSpec((out, third)...]
  transfers between devices with their start and end apart: 5 -> 5, of which waited for: 1 -> 1; matrix products, arithmetic and copies ran while one was open for 0% -> 0% of each run, Pallas kernels for 29% -> 25%
where the time goes in v5:
time: 38.7 us; the launch traced here: 38.4 us
  Pallas kernels  20.8 us (54%)
  starting transfers between devices  12.6 us (33%)
  waiting for transfers between devices  2.9 us (7%)
  between operations  2.07 us (5%)
    all_to_all x1, starting transfers between devices, body(): parts = lax.all_to_all(sent, 'seq', 0, 0, tiled=True)  5.62 us
    pallas_call x1, Pallas kernels, middles(): pl.pallas_call(middle_kernel, in_specs=[whole(), far_spec()], out_specs=[...  3.94 us
    pallas_call x1, Pallas kernels, prior_part(): pl.pallas_call(prior_kernel, grid=(parities,), in_specs=[pl.BlockSpec(rec...  3.89 us
    pallas_call x1, Pallas kernels, attention(): pl.pallas_call(kernel, in_specs=[far_spec()] * 9, out_specs=[whole()] * l...  3.87 us
    ppermute x1, starting transfers between devices, body(): above = lax.ppermute(down, 'seq', [(i, i + 1) for i in range(slabs - 1)])  3.09 us
    ppermute x1, starting transfers between devices, body(): below = lax.ppermute(up, 'seq', [(i + 1, i) for i in range(slabs - 1)])  3.09 us
    ppermute x1, waiting for transfers between devices, body(): below = lax.ppermute(up, 'seq', [(i + 1, i) for i in range(slabs - 1)])  2.89 us
    pallas_call x1, Pallas kernels, own_part(): pl.pallas_call(own_kernel, grid=(parities,), in_specs=[pl.BlockSpec(activ...  2.68 us
  transfers between devices with their start and end apart: 5, of which 1 were waited for; matrix products, arithmetic and copies ran while one was open for 0% of the time, Pallas kernels for 25%

profile of v5, /device:TPU:17, one launch (start us, length us, event | category | flops | bytes accessed | tf_op | source)
XLA Modules:
  0.0 38.4 jit_solution(7456611674731630423)
XLA Ops:
  0.6 3.9 %attention.1 = (bf16[8,3,48,128]{3,2,1,0:T(8,128)(2,1)}, f32[8,128]{1,0:T(8,128)S(1)}, bf16[2,480,4,128]{3,2,1,0:T(4,128)(2,1)S(1)}, bf16[2,10,2,128]{3,2,1,0:T(2,128)(2,1)S(1)}, bf16[2,10,2,128]{3,2,1,0:T(2,128)(2,1)S(1)}) custom-call(s32[2,2,16]{2,1,0:T(2,128)} %refs_0_.1, bf16[2,320,128]{2,1,0:T(8,128)(2,1)} %bitcast.30, bf16[1280,128]{1,0:T(8,128)(2,1)} %bitcast.28, ...), custom_call_target="tpu_custom_call" | custom-call | flops 629145600 | bytes 819200 | tf_op jit(solution)/shard_map/attention/pallas_call | solution.py:216
  4.5 5.6 %all-to-all-start = ((bf16[8,3,48,128]{3,2,1,0:T(8,128)(2,1)}), bf16[8,3,48,128]{3,2,1,0:T(8,128)(2,1)S(1)}, u32[]{:S(2)}, u32[]{:S(2)}) async-start(bf16[8,3,48,128]{3,2,1,0:T(8,128)(2,1)} %get-tuple-element.22), calls=%async_computation | async-start | bytes 589824 | tf_op jit(solution)/shard_map/all_to_all | solution.py:981
  10.8 0.7 %prepare.1 = (bf16[4,4,80,384]{3,2,1,0:T(8,128)(2,1)S(1)}, bf16[200,384]{1,0:T(8,128)(2,1)S(1)}, bf16[200,384]{1,0:T(8,128)(2,1)S(1)}, bf16[40,256]{1,0:T(8,128)(2,1)S(1)}) custom-call(s32[1]{0:T(128)S(6)} %copy.17.span_ref, f32[8,128]{1,0:T(8,128)S(1)} %get-tuple-element.23.facts_ref, bf16[2,480,4,128]{3,2,1,0:T(4,128)(2,1)S(1)} %get-tuple-element.24.cache_ref, ...), custom_call_target="tpu_custom_call" | custom-call | flops 491520 | bytes 2949120 | tf_op jit(solution)/shard_map/prepare/pallas_call | solution.py:346
  11.5 3.1 %collective-permute-start = (bf16[200,384]{1,0:T(8,128)(2,1)S(1)}, bf16[200,384]{1,0:T(8,128)(2,1)S(1)}, u32[]{:S(2)}, u32[]{:S(2)}) collective-permute-start(bf16[200,384]{1,0:T(8,128)(2,1)S(1)} %get-tuple-element.28), channel_id=1, source_target_pairs={{0,2},{2,4},{4,6},{6,8},{8,10},{10,12},{12,14},{1,3},{3,5},{5,7},{... | collective-permute-start | bytes 460808 | tf_op jit(solution)/shard_map/ppermute | solution.py:985
  14.6 3.1 %collective-permute-start.1 = (bf16[200,384]{1,0:T(8,128)(2,1)S(1)}, bf16[200,384]{1,0:T(8,128)(2,1)S(1)}, u32[]{:S(2)}, u32[]{:S(2)}) collective-permute-start(bf16[200,384]{1,0:T(8,128)(2,1)S(1)} %get-tuple-element.29), channel_id=1, source_target_pairs={{2,0},{4,2},{6,4},{8,6},{10,8},{12,10},{14,12},{3,1},{5,3},{7,5},{... | collective-permute-start | bytes 460808 | tf_op jit(solution)/shard_map/ppermute | solution.py:986
  18.4 3.9 %middle.1 = (bf16[2,2,80,384]{3,2,1,0:T(8,128)(2,1)S(1)}, f32[2,2,80,384]{3,2,1,0:T(8,128)S(1)}) custom-call(bf16[4,4,80,384]{3,2,1,0:T(8,128)(2,1)S(1)} %get-tuple-element.30.own_ref, bf16[192,10368]{1,0:T(8,128)(2,1)} %bitcast.22), custom_call_target="tpu_custom_call" | custom-call | flops 1274019840 | bytes 4964352 | tf_op jit(solution)/shard_map/middle/pallas_call | solution.py:435
  22.3 0.0 copy-start.1
  22.3 0.0 copy-start.2
  22.3 0.0 collective-permute-done.above_ref
  22.3 2.9 %collective-permute-done.1.below_ref = bf16[200,384]{1,0:T(8,128)(2,1)S(1)} collective-permute-done((bf16[200,384]{1,0:T(8,128)(2,1)S(1)}, bf16[200,384]{1,0:T(8,128)(2,1)S(1)}, u32[]{:S(2)}, u32[]{:S(2)}) %collective-permute-start.1) | collective-permute-done | bytes 153632 | tf_op jit(solution)/shard_map/ppermute | solution.py:986
  25.2 0.0 all-to-all-done.parts_ref
  25.2 0.0 copy-start
  25.2 2.2 %latent.1 = (bf16[3,40,128]{2,1,0:T(8,128)(2,1)S(1)}, bf16[3,40,128]{2,1,0:T(8,128)(2,1)S(1)}, bf16[2,10,2,128]{3,2,1,0:T(2,128)(2,1)}, bf16[2,2,192,1152]{3,2,1,0:T(8,128)(2,1)S(1)}) custom-call(s32[1]{0:T(128)S(6)} %copy.16.step_ref, bf16[8,3,48,128]{3,2,1,0:T(8,128)(2,1)S(1)} %all-to-all-done.parts_ref, bf16[40,256]{1,0:T(8,128)(2,1)S(1)} %get-tuple-element.27.own_ref, ...), custom_call_target="tpu_custom_call" | custom-call | flops 294912 | bytes 294912 | tf_op jit(solution)/shard_map/latent/pallas_call | solution.py:777
  27.4 0.7 %collective-permute-start.2 = (bf16[3,40,128]{2,1,0:T(8,128)(2,1)S(1)}, bf16[3,40,128]{2,1,0:T(8,128)(2,1)S(1)}, u32[]{:S(2)}, u32[]{:S(2)}) collective-permute-start(bf16[3,40,128]{2,1,0:T(8,128)(2,1)S(1)} %get-tuple-element.36), channel_id=1, source_target_pairs={{0,1},{1,0},{2,3},{3,2},{4,5},{5,4},{6,7},{7,6},{8,9},{9,8},{10,11... | collective-permute-start | bytes 92168 | tf_op jit(solution)/shard_map/ppermute | solution.py:946
  28.2 1.1 %edge.1.edge_ref = bf16[2,2,80,384]{3,2,1,0:T(8,128)(2,1)S(1)} custom-call(f32[2,2,80,384]{3,2,1,0:T(8,128)S(1)} %get-tuple-element.38.rim_ref, bf16[200,384]{1,0:T(8,128)(2,1)S(1)} %collective-permute-done.above_ref, bf16[200,384]{1,0:T(8,128)(2,1)S(1)} %collective-permute-done.1.below_ref, bf16[2,2,192,1152]{3,2,1,0:T(8,128)(2,1)S(1)} %get-tuple-element.39.weight_ref), custom_call_target="tpu_custom_call" | custom-call | flops 283115520 | bytes 1923072 | tf_op jit(solution)/shard_map/edge/pallas_call | solution.py:499
  29.3 0.0 collective-permute-done.2.received_ref
  29.3 0.0 copy-done.1
  29.3 0.0 copy-done.2
  29.3 1.3 %first.1 = (bf16[2,4,80,384]{3,2,1,0:T(8,128)(2,1)S(1)}, bf16[2,4,80,384]{3,2,1,0:T(8,128)(2,1)S(1)}) custom-call(bf16[3,40,128]{2,1,0:T(8,128)(2,1)S(1)} %get-tuple-element.35.clean_ref, bf16[3,40,128]{2,1,0:T(8,128)(2,1)S(1)} %collective-permute-done.2.received_ref, bf16[40,256]{1,0:T(8,128)(2,1)S(1)} %get-tuple-element.27.own_ref, ...), custom_call_target="tpu_custom_call" | custom-call | flops 212336640 | bytes 983040 | tf_op jit(solution)/shard_map/first/pallas_call | solution.py:927
  30.6 0.1 collective-permute-start.3
  30.7 0.0 copy-done
  30.7 1.1 %mix.1.old_ref.new_ref = bf16[3,4,192,1536]{3,2,1,0:T(8,128)(2,1)S(1)} custom-call(bf16[192,10368]{1,0:T(8,128)(2,1)S(1)} %bitcast.24), custom_call_target="tpu_custom_call" | custom-call | flops 7962624 | bytes 11943936 | tf_op jit(solution)/shard_map/mix/pallas_call | solution.py:543
  31.8 2.7 %own_part.1.own_ref = f32[4,2,2,80,192]{4,3,2,1,0:T(8,128)S(1)} custom-call(bf16[2,4,80,384]{3,2,1,0:T(8,128)(2,1)S(1)} %get-tuple-element.41.source_ref, bf16[3,4,192,1536]{3,2,1,0:T(8,128)(2,1)S(1)} %mix.1.old_ref.new_ref, bf16[3,4,192,1536]{3,2,1,0:T(8,128)(2,1)S(1)} %mix.1.old_ref.new_ref), custom_call_target="tpu_custom_call" | custom-call | flops 1132462080 | bytes 5210112 | tf_op jit(solution)/shard_map/own_part/pallas_call | solution.py:603
  34.5 0.0 collective-permute-done.3.source_ref
  34.5 3.9 %prior_part.1 = bf16[2,240,4,128]{3,2,1,0:T(4,128)(2,1)} custom-call(bf16[2,4,80,384]{3,2,1,0:T(8,128)(2,1)S(1)} %collective-permute-done.3.source_ref, bf16[2,2,80,384]{3,2,1,0:T(8,128)(2,1)S(1)} %get-tuple-element.37.middle_ref, bf16[2,2,80,384]{3,2,1,0:T(8,128)(2,1)S(1)} %edge.1.edge_ref, f32[4,2,2,80,192]{4,3,2,1,0:T(8,128)S(1)} %own_part.1.own_ref, ...), custom_call_target="tpu_custom_call" | custom-call | flops 1132462080 | bytes 5210112 | tf_op jit(solution)/shard_map/prior_part/pallas_call | solution.py:689
Async XLA Ops:
  4.5 20.7 %all-to-all-start = ((bf16[8,3,48,128]{3,2,1,0:T(8,128)(2,1)}), bf16[8,3,48,128]{3,2,1,0:T(8,128)(2,1)S(1)}, u32[]{:S(2)}, u32[]{:S(2)}) async-start(bf16[8,3,48,128]{3,2,1,0:T(8,128)(2,1)} %get-tuple-element.22), calls=%async_computation | async-start | bytes 589824 | tf_op jit(solution)/shard_map/all_to_all | solution.py:981
  11.5 10.8 %collective-permute-start = (bf16[200,384]{1,0:T(8,128)(2,1)S(1)}, bf16[200,384]{1,0:T(8,128)(2,1)S(1)}, u32[]{:S(2)}, u32[]{:S(2)}) collective-permute-start(bf16[200,384]{1,0:T(8,128)(2,1)S(1)} %get-tuple-element.28), channel_id=1, source_target_pairs={{0,2},{2,4},{4,6},{6,8},{8,10},{10,12},{12,14},{1,3},{3,5},{5,7},{... | collective-permute-start | bytes 460808 | tf_op jit(solution)/shard_map/ppermute | solution.py:985
  14.6 10.6 %collective-permute-start.1 = (bf16[200,384]{1,0:T(8,128)(2,1)S(1)}, bf16[200,384]{1,0:T(8,128)(2,1)S(1)}, u32[]{:S(2)}, u32[]{:S(2)}) collective-permute-start(bf16[200,384]{1,0:T(8,128)(2,1)S(1)} %get-tuple-element.29), channel_id=1, source_target_pairs={{2,0},{4,2},{6,4},{8,6},{10,8},{12,10},{14,12},{3,1},{5,3},{7,5},{... | collective-permute-start | bytes 460808 | tf_op jit(solution)/shard_map/ppermute | solution.py:986
  22.3 7.0 %copy-start.1 = (bf16[432,384]{1,0:T(8,128)(2,1)S(1)}, bf16[432,384]{1,0:T(8,128)(2,1)}, u32[]{:S(2)}) copy-start(bf16[432,384]{1,0:T(8,128)(2,1)} %weight_ref.1) | copy-start | bytes 995332
  22.3 7.0 %copy-start.2 = (bf16[384]{0:T(512)(128)(2,1)S(1)}, bf16[384]{0:T(512)(128)(2,1)}, u32[]{:S(2)}) copy-start(bf16[384]{0:T(512)(128)(2,1)} %param.26) | copy-start | bytes 2308
  25.2 5.5 %copy-start = (bf16[10368,192]{0,1:T(8,128)(2,1)S(1)}, bf16[10368,192]{0,1:T(8,128)(2,1)}, u32[]{:S(2)}) copy-start(bf16[10368,192]{0,1:T(8,128)(2,1)} %param.27) | copy-start | bytes 11943940
  27.4 1.9 %collective-permute-start.2 = (bf16[3,40,128]{2,1,0:T(8,128)(2,1)S(1)}, bf16[3,40,128]{2,1,0:T(8,128)(2,1)S(1)}, u32[]{:S(2)}, u32[]{:S(2)}) collective-permute-start(bf16[3,40,128]{2,1,0:T(8,128)(2,1)S(1)} %get-tuple-element.36), channel_id=1, source_target_pairs={{0,1},{1,0},{2,3},{3,2},{4,5},{5,4},{6,7},{7,6},{8,9},{9,8},{10,11... | collective-permute-start | bytes 92168 | tf_op jit(solution)/shard_map/ppermute | solution.py:946
  30.6 3.9 %collective-permute-start.3 = (bf16[2,4,80,384]{3,2,1,0:T(8,128)(2,1)S(1)}, bf16[2,4,80,384]{3,2,1,0:T(8,128)(2,1)S(1)}, u32[]{:S(2)}, u32[]{:S(2)}) collective-permute-start(bf16[2,4,80,384]{3,2,1,0:T(8,128)(2,1)S(1)} %get-tuple-element.40), channel_id=1, source_target_pairs={{0,1},{1,0},{2,3},{3,2},{4,5},{5,4},{6,7},{7,6},{8,9},{9,8},{10,11... | collective-permute-start | bytes 1474568 | tf_op jit(solution)/shard_map/ppermute | solution.py:946
